TPU v7x, 128 devices: a whole 4x4x4 slice. The times are simulated.
128 devices in a mesh: seq: 16 (over y, x), ctx: 8 (over z, core).
Axes of the slice: x: 4, y: 4, z: 4, core: 2. Of those that a mesh axis runs over, the one named last changes fastest.
Arguments:
- hidden_in: bfloat16 [16, 1024, 1024], P('seq', 'ctx'), may hold values from -6 to 6
- positions: int32 [16, 1024], P('seq', 'ctx'), may hold values from 0 to 1534, as said below
- starts: int32 [16, 2], P('seq'), may hold values from 0 to 768, as said below
- routes: int32 [16, 1024, 4], P('seq', 'ctx'), may hold values from 0 to 7, all different within a row; in each aligned block of 128 rows (0 to 127, 128 to 255, ..., all dimensions but the last counted through in order) at most 80 rows name the same one
- qkv_weight: bfloat16 [2048, 1024], P(('seq', 'ctx')), may hold values from -0.1875 to 0.1875
- out_weight: bfloat16 [1024, 1024], P(('seq', 'ctx')), may hold values from -1.5 to 1.5
- expert_in: bfloat16 [1024, 8, 1024], P(('seq', 'ctx')), may hold values from -0.1875 to 0.1875
- expert_out: bfloat16 [1024, 8, 512], P(('seq', 'ctx')), may hold values from -1.5 to 1.5
- router: bfloat16 [1024, 8], replicated, may hold values from -0.09375 to 0.09375
- attn_gain: bfloat16 [1024], replicated, may hold values from 0.25 to 1.75
- query_gain: bfloat16 [1024], replicated, may hold values from 0.25 to 1.75
- key_gain: bfloat16 [512], replicated, may hold values from 0.25 to 1.75
- mlp_gain: bfloat16 [1024], replicated, may hold values from 0.25 to 1.75
- out_grad: bfloat16 [16, 1024, 1024], P('seq', 'ctx'), may hold values from -6 to 6
Outputs:
- result: bfloat16 [16, 1024, 1024], P('seq', 'ctx')
- grad_input: float32 [16, 1024, 1024], P('seq', 'ctx')
- grad_qkv: float32 [2048, 1024], P(('seq', 'ctx'))
- grad_out: float32 [1024, 1024], P(('seq', 'ctx'))
- grad_expert_in: float32 [1024, 8, 1024], P(('seq', 'ctx'))
- grad_expert_out: float32 [1024, 8, 512], P(('seq', 'ctx'))
- grad_router: float32 [1024, 8], replicated
- grad_attn_gain: float32 [1024], replicated
- grad_query_gain: float32 [1024], replicated
- grad_key_gain: float32 [512], replicated
- grad_mlp_gain: float32 [1024], replicated
Inputs may be any that keep to these rules, and one draw needn't show every extreme that they name: `routes`: each row names 4 different experts; among the 128 tokens of one sequence on one device (aligned blocks), no expert is named by more than 80 of them. Piece k of a sequence starts at a token index from k * 512 to (k + 1) * 512 - 256; pieces never intersect. Within a sequence positions start at 0 and rise by 1 or 2 from token to token; the last token of every sequence has position 1534.
All inputs are finite; a program needn't handle non-finite values.
Results may differ from a plain program's by a relative error of at most 0.018.
Values may be sent and summed in bfloat16 or wider, within the bound.
A program may use at most 256 MiB of HBM per device.

v0:
```python
import math

import jax
import jax.numpy as jnp
from jax import lax
from jax.sharding import PartitionSpec as P

QUERY_HEADS = 16
KEY_VALUE_HEADS = 8
PIECE = 256


EPSILON = 1e-06
ROPE_BASE = 10000.0
MASKED = -1e30


def rms_scale(field):
    return lax.rsqrt(jnp.mean(field * field, axis=-1, keepdims=True) + EPSILON)


def rms_back(upstream, normed, scales):
    return scales * (upstream - normed * jnp.mean(upstream * normed, axis=-1, keepdims=True))


def rotary_tables(positions, half_size):
    frequency = ROPE_BASE ** (-jnp.arange(half_size, dtype=jnp.float32) * 2.0 / (2 * half_size))
    angles = positions.astype(jnp.float32)[:, None] * frequency
    return (jnp.cos(angles)[:, None, :], jnp.sin(angles)[:, None, :])


def apply_rotary(field, cosine_values, sine_values):
    half_size = field.shape[-1] // 2
    lower_half = field[..., :half_size]
    upper_half = field[..., half_size:]
    return jnp.concatenate(
        [
            lower_half * cosine_values - upper_half * sine_values,
            upper_half * cosine_values + lower_half * sine_values,
        ],
        axis=-1,
    )


def rotate_back(upstream, cosine_values, sine_values):
    half_size = upstream.shape[-1] // 2
    lower_half = upstream[..., :half_size]
    upper_half = upstream[..., half_size:]
    return jnp.concatenate(
        [
            lower_half * cosine_values + upper_half * sine_values,
            upper_half * cosine_values - lower_half * sine_values,
        ],
        axis=-1,
    )


def piece_ids(places, piece_starts):
    inside = (places[..., None] >= piece_starts) & (places[..., None] < piece_starts + PIECE)
    labels = jnp.arange(piece_starts.shape[-1], dtype=jnp.int32) + 1
    return jnp.sum(inside.astype(jnp.int32) * labels, axis=-1)


def masked_scores(q_rows, k_all, allowed):
    score_scale = q_rows.shape[-1] ** (-0.5)
    scores = (
        jnp.einsum("btkgd,bskd->bkgts", q_rows, k_all, preferred_element_type=jnp.float32)
        * score_scale
    )
    return jnp.where(allowed[:, None, None], scores, MASKED)


def attend(packed):
    q_rows, k_all, v_all, allowed = packed
    scores = masked_scores(q_rows, k_all, allowed)
    row_peak = jnp.max(scores, axis=-1, keepdims=True)
    exp_terms = jnp.exp(scores - row_peak)
    row_total = jnp.sum(exp_terms, axis=-1, keepdims=True)
    attn_probs = (exp_terms / row_total).astype(jnp.bfloat16)
    attention_mixed = jnp.einsum(
        "bkgts,bskd->btkgd", attn_probs, v_all, preferred_element_type=jnp.float32
    )
    return (attention_mixed, row_peak + jnp.log(row_total))


def attend_back(packed):
    q_rows, k_all, v_all, allowed, log_total, d_mixed = packed
    score_scale = q_rows.shape[-1] ** (-0.5)
    scores = masked_scores(q_rows, k_all, allowed)
    attn_probs = jnp.exp(scores - log_total)
    d_probs = jnp.einsum("btkgd,bskd->bkgts", d_mixed, v_all, preferred_element_type=jnp.float32)
    d_scores = (
        attn_probs * (d_probs - jnp.sum(attn_probs * d_probs, axis=-1, keepdims=True))
    ).astype(jnp.bfloat16)
    d_query = (
        jnp.einsum("bkgts,bskd->btkgd", d_scores, k_all, preferred_element_type=jnp.float32)
        * score_scale
    )
    d_key = (
        jnp.einsum("bkgts,btkgd->bskd", d_scores, q_rows, preferred_element_type=jnp.float32)
        * score_scale
    )
    d_value = jnp.einsum(
        "bkgts,btkgd->bskd",
        attn_probs.astype(jnp.bfloat16),
        d_mixed,
        preferred_element_type=jnp.float32,
    )
    return (d_query, d_key, d_value)


def local(
    hidden_in,
    positions,
    starts,
    routes,
    qkv_weight,
    out_weight,
    expert_in,
    expert_out,
    router,
    attn_gain,
    query_gain,
    key_gain,
    mlp_gain,
    out_grad,
):
    seqs_here, rows_seq, model_width = hidden_in.shape
    token_rows = seqs_here * rows_seq
    key_value_width = key_gain.shape[0]
    head_count = QUERY_HEADS
    key_value_head_count = KEY_VALUE_HEADS
    head_width = model_width // head_count
    query_group_width = head_count // key_value_head_count
    experts = router.shape[1]
    pick_count = routes.shape[2]
    hidden_ff = expert_out.shape[2]
    capacity = seqs_here * (5 * rows_seq * pick_count // (4 * experts))
    full_len = rows_seq * lax.axis_size("ctx")
    block_seqs = math.gcd(seqs_here, 4)
    block_count = seqs_here // block_seqs

    def grouped(field):
        return field.reshape((block_count, block_seqs) + field.shape[1:])

    x_flat = hidden_in.reshape(token_rows, model_width).astype(jnp.float32)
    scale_one = rms_scale(x_flat)
    normed_one = x_flat * scale_one
    attn_gain_f = attn_gain.astype(jnp.float32)
    x_low = (normed_one * attn_gain_f).astype(jnp.bfloat16)
    qkv_whole, out_whole = (
        lax.all_gather(qkv_weight, ("seq", "ctx"), axis=0, tiled=True),
        lax.all_gather(out_weight, ("seq", "ctx"), axis=0, tiled=True),
    )
    qkv = jnp.dot(x_low, qkv_whole.T, preferred_element_type=jnp.float32)
    q_raw = qkv[:, :model_width]
    key_unnormed = qkv[:, model_width : model_width + key_value_width]
    v_raw = qkv[:, model_width + key_value_width :]
    q_scale = rms_scale(q_raw)
    q_normed = q_raw * q_scale
    k_scale = rms_scale(key_unnormed)
    k_normed = key_unnormed * k_scale
    query_gain_f = query_gain.astype(jnp.float32)
    key_gain_f = key_gain.astype(jnp.float32)
    cosine_values, sine_values = rotary_tables(positions.reshape(token_rows), head_width // 2)
    query_rotated = apply_rotary(
        (q_normed * query_gain_f).reshape(token_rows, head_count, head_width),
        cosine_values,
        sine_values,
    ).astype(jnp.bfloat16)
    key_rotated = apply_rotary(
        (k_normed * key_gain_f).reshape(token_rows, key_value_head_count, head_width),
        cosine_values,
        sine_values,
    ).astype(jnp.bfloat16)
    value_reduced = v_raw.astype(jnp.bfloat16)
    k_all, v_all = (
        lax.all_gather(
            key_rotated.reshape(seqs_here, rows_seq, key_value_width), "ctx", axis=1, tiled=True
        ),
        lax.all_gather(
            value_reduced.reshape(seqs_here, rows_seq, key_value_width), "ctx", axis=1, tiled=True
        ),
    )
    row_pos = lax.axis_index("ctx") * rows_seq + jnp.arange(rows_seq, dtype=jnp.int32)
    key_pos = jnp.arange(full_len, dtype=jnp.int32)
    row_piece = piece_ids(jnp.broadcast_to(row_pos, (seqs_here, rows_seq)), starts[:, None, :])
    key_piece = piece_ids(jnp.broadcast_to(key_pos, (seqs_here, full_len)), starts[:, None, :])
    allowed = (key_pos[None, None, :] <= row_pos[None, :, None]) | (
        row_piece[:, :, None] == key_piece[:, None, :]
    ) & (row_piece[:, :, None] > 0)
    q_groups = grouped(
        query_rotated.reshape(
            seqs_here, rows_seq, key_value_head_count, query_group_width, head_width
        )
    )
    k_groups = grouped(k_all.reshape(seqs_here, full_len, key_value_head_count, head_width))
    v_groups = grouped(v_all.reshape(seqs_here, full_len, key_value_head_count, head_width))
    mask_groups = grouped(allowed)
    attn_mixed, log_total = lax.map(attend, (q_groups, k_groups, v_groups, mask_groups))
    attn_low = attn_mixed.reshape(token_rows, model_width).astype(jnp.bfloat16)
    midway = x_flat + jnp.dot(attn_low, out_whole.T, preferred_element_type=jnp.float32)
    scale_two = rms_scale(midway)
    normed_two = midway * scale_two
    mlp_gain_f = mlp_gain.astype(jnp.float32)
    h_low = (normed_two * mlp_gain_f).astype(jnp.bfloat16)
    gates = jax.nn.softmax(jnp.dot(h_low, router, preferred_element_type=jnp.float32), axis=-1)
    flat_route = routes.reshape(token_rows * pick_count)
    expert_ids = jnp.arange(experts, dtype=jnp.int32)
    member = (flat_route[:, None] == expert_ids).astype(jnp.int32)
    slot_rank = jnp.sum((jnp.cumsum(member, axis=0) - member) * member, axis=1)
    slot_of = flat_route * capacity + slot_rank
    slot_src = (
        jnp.zeros((experts * capacity,), jnp.int32)
        .at[slot_of]
        .set(jnp.arange(token_rows * pick_count, dtype=jnp.int32))
    )
    slot_live = jnp.zeros((experts * capacity,), jnp.float32).at[slot_of].set(1.0)
    slot_tok = slot_src // pick_count
    member_f = member.reshape(token_rows, pick_count, experts).astype(jnp.float32)
    pick_gate = jnp.sum(member_f * gates[:, None, :], axis=-1)
    slot_gate = jnp.zeros((experts * capacity,), jnp.float32).at[slot_of].set(pick_gate.reshape(-1))
    slots_in = jnp.where(
        slot_live[:, None] > 0, h_low[slot_tok], jnp.zeros((), jnp.bfloat16)
    ).reshape(experts, capacity, model_width)
    columns = slots_in
    gate_up = jnp.einsum(
        "ecd,def->ecf",
        columns,
        lax.all_gather(expert_in, ("seq", "ctx"), axis=0, tiled=True),
        preferred_element_type=jnp.float32,
    )
    gate_part = gate_up[..., :hidden_ff]
    up_part = gate_up[..., hidden_ff:]
    gate_sig = jax.nn.sigmoid(gate_part)
    swish_part = gate_part * gate_sig
    act_low = (swish_part * up_part).astype(jnp.bfloat16)
    expert_res = jnp.einsum(
        "ecf,def->ecd",
        act_low,
        lax.all_gather(expert_out, ("seq", "ctx"), axis=0, tiled=True),
        preferred_element_type=jnp.float32,
    )
    flat_res = expert_res.reshape(experts * capacity, model_width)
    mixture = (
        jnp.zeros((token_rows, model_width), jnp.float32)
        .at[slot_tok]
        .add(flat_res * slot_gate[:, None])
    )
    result = (midway + mixture).astype(jnp.bfloat16).reshape(hidden_in.shape)
    d_top = out_grad.reshape(token_rows, model_width).astype(jnp.float32)
    d_slot_rows = d_top[slot_tok]
    d_expert = (
        (d_slot_rows * slot_gate[:, None])
        .astype(jnp.bfloat16)
        .reshape(experts, capacity, model_width)
    )
    d_gate_slot = jnp.sum(d_slot_rows * flat_res, axis=-1) * slot_live
    columns = d_expert
    d_act = jnp.einsum(
        "ecd,def->ecf",
        columns,
        lax.all_gather(expert_out, ("seq", "ctx"), axis=0, tiled=True),
        preferred_element_type=jnp.float32,
    )
    d_gate_up = jnp.concatenate(
        [d_act * up_part * gate_sig * (1.0 + gate_part * (1.0 - gate_sig)), d_act * swish_part],
        axis=-1,
    ).astype(jnp.bfloat16)
    d_slots = jnp.einsum(
        "ecf,def->ecd",
        d_gate_up,
        lax.all_gather(expert_in, ("seq", "ctx"), axis=0, tiled=True),
        preferred_element_type=jnp.float32,
    )
    d_hidden = (
        jnp.zeros((token_rows, model_width), jnp.float32)
        .at[slot_tok]
        .add(d_slots.reshape(experts * capacity, model_width))
    )
    columns = slots_in
    grad_expert_in = lax.psum_scatter(
        jnp.einsum("ecd,ecf->def", columns, d_gate_up, preferred_element_type=jnp.float32),
        ("seq", "ctx"),
        scatter_dimension=0,
        tiled=True,
    )
    columns = d_expert
    grad_expert_out = lax.psum_scatter(
        jnp.einsum("ecd,ecf->def", columns, act_low, preferred_element_type=jnp.float32),
        ("seq", "ctx"),
        scatter_dimension=0,
        tiled=True,
    )
    d_pick = d_gate_slot[slot_of].reshape(token_rows, pick_count)
    d_gates = jnp.sum(member_f * d_pick[:, :, None], axis=1)
    d_logits = (gates * (d_gates - jnp.sum(gates * d_gates, axis=-1, keepdims=True))).astype(
        jnp.bfloat16
    )
    d_hidden = d_hidden + jnp.dot(d_logits, router.T, preferred_element_type=jnp.float32)
    router_local = jnp.dot(h_low.T, d_logits, preferred_element_type=jnp.float32)
    mlp_local = jnp.sum(d_hidden * normed_two, axis=0)
    d_midway = d_top + rms_back(d_hidden * mlp_gain_f, normed_two, scale_two)
    d_branch = d_midway.astype(jnp.bfloat16)
    d_attn_low = jnp.dot(d_branch, out_whole, preferred_element_type=jnp.float32).astype(
        jnp.bfloat16
    )
    picked = d_branch
    grad_out = lax.psum_scatter(
        jnp.einsum("to,ti->oi", picked, attn_low, preferred_element_type=jnp.float32),
        ("seq", "ctx"),
        scatter_dimension=0,
        tiled=True,
    )
    d_mixed_groups = grouped(
        d_attn_low.reshape(seqs_here, rows_seq, key_value_head_count, query_group_width, head_width)
    )
    d_query, d_key_all, d_value_all = lax.map(
        attend_back, (q_groups, k_groups, v_groups, mask_groups, log_total, d_mixed_groups)
    )
    d_key, d_value = (
        lax.psum_scatter(
            d_key_all.reshape(seqs_here, full_len, key_value_width).astype(jnp.bfloat16),
            "ctx",
            scatter_dimension=1,
            tiled=True,
        ).astype(jnp.float32),
        lax.psum_scatter(
            d_value_all.reshape(seqs_here, full_len, key_value_width).astype(jnp.bfloat16),
            "ctx",
            scatter_dimension=1,
            tiled=True,
        ).astype(jnp.float32),
    )
    d_qn = rotate_back(
        d_query.reshape(token_rows, head_count, head_width), cosine_values, sine_values
    ).reshape(token_rows, model_width)
    d_kn = rotate_back(
        d_key.reshape(token_rows, key_value_head_count, head_width), cosine_values, sine_values
    ).reshape(token_rows, key_value_width)
    query_local = jnp.sum(d_qn * q_normed, axis=0)
    key_local = jnp.sum(d_kn * k_normed, axis=0)
    d_q_raw = rms_back(d_qn * query_gain_f, q_normed, q_scale)
    d_k_raw = rms_back(d_kn * key_gain_f, k_normed, k_scale)
    d_qkv = jnp.concatenate(
        [d_q_raw, d_k_raw, d_value.reshape(token_rows, key_value_width)], axis=-1
    ).astype(jnp.bfloat16)
    d_x_low = jnp.dot(d_qkv, qkv_whole, preferred_element_type=jnp.float32)
    picked = d_qkv
    grad_qkv = lax.psum_scatter(
        jnp.einsum("tq,td->qd", picked, x_low, preferred_element_type=jnp.float32),
        ("seq", "ctx"),
        scatter_dimension=0,
        tiled=True,
    )
    attn_local = jnp.sum(d_x_low * normed_one, axis=0)
    grad_input = (d_midway + rms_back(d_x_low * attn_gain_f, normed_one, scale_one)).reshape(
        hidden_in.shape
    )
    grad_attn_gain, grad_query_gain, grad_key_gain, grad_mlp_gain, grad_router = lax.psum(
        (attn_local, query_local, key_local, mlp_local, router_local), ("seq", "ctx")
    )
    return (
        result,
        grad_input,
        grad_qkv,
        grad_out,
        grad_expert_in,
        grad_expert_out,
        grad_router,
        grad_attn_gain,
        grad_query_gain,
        grad_key_gain,
        grad_mlp_gain,
    )


def solution(mesh):
    in_specs = (
        P("seq", "ctx", None),
        P("seq", "ctx"),
        P("seq", None),
        P("seq", "ctx", None),
        P(("seq", "ctx"), None),
        P(("seq", "ctx"), None),
        P(("seq", "ctx"), None, None),
        P(("seq", "ctx"), None, None),
        P(),
        P(),
        P(),
        P(),
        P(),
        P("seq", "ctx", None),
    )
    out_specs = (
        P("seq", "ctx", None),
        P("seq", "ctx", None),
        P(("seq", "ctx"), None),
        P(("seq", "ctx"), None),
        P(("seq", "ctx"), None, None),
        P(("seq", "ctx"), None, None),
        P(),
        P(),
        P(),
        P(),
        P(),
    )
    return jax.shard_map(local, mesh=mesh, in_specs=in_specs, out_specs=out_specs, check_vma=False)
```

profile of v0, /device:TPU:0, one launch (start us, length us, event | category | flops | bytes accessed | tf_op | source)
XLA Modules:
  0.0 3146.8 jit_solution(7050579265357424226)
XLA Ops:
  8.7 1.1 fusion.34
  9.8 70.8 %all-gather.8.cloned.1.call-done = bf16[2048,1024]{1,0:T(8,128)(2,1)} async-done(((bf16[16,1024]{1,0:T(8,128)(2,1)}), bf16[2048,1024]{1,0:T(8,128)(2,1)}) %all-gather.8.cloned.1.call-update) | async-done | bytes 4194320 | tf_op jit(solution)/shard_map/all_gather | solution.py:152
  80.6 3.8 fusion.45
  90.7 1.1 reduce-window.6
  92.2 2.4 scatter_custom_fusion.1
  95.3 2.4 scatter_custom_fusion
  98.5 2.9 gather_fusion.1
  102.5 1.2 multiply_reduce_fusion.6
  104.3 1.9 fusion.37
  106.2 1.2 copy.92
  107.5 0.8 subtract_convert_fusion
  108.3 2.3 copy.90
  110.6 21.5 all-gather.10.cloned.1.call-done
  132.1 2.7 fusion.70
  134.8 1.1 fusion.3
  136.0 2.1 copy-done.2
  138.2 2.2 fusion.16
  140.4 60.9 %all-gather.12.cloned.1.call-done = bf16[1024,1024]{1,0:T(8,128)(2,1)} async-done(((bf16[8,1024]{1,0:T(8,128)(2,1)}), bf16[1024,1024]{1,0:T(8,128)(2,1)}) %all-gather.12.cloned.1.call-update) | async-done | bytes 2097168 | tf_op jit(solution)/shard_map/all_gather | solution.py:153
  201.3 2.6 multiply_reduce_fusion.5
  204.5 3.6 gather_fusion
  209.5 1.3 log_add_fusion
  210.8 74.4 %all-gather.14.cloned.1.call-done = bf16[1024,8,1024]{2,0,1:T(8,128)(2,1)} async-done(((bf16[8,8,1024]{2,0,1:T(8,128)(2,1)}), bf16[1024,8,1024]{2,0,1:T(8,128)(2,1)}) %all-gather.14.cloned.1.call-update) | async-done | bytes 16777232 | tf_op jit(solution)/shard_map/all_gather | solution.py:230
  285.3 9.3 fusion.19
  294.5 1.6 copy-done.9
  296.1 1.3 multiply_convert_fusion.3
  297.4 65.1 %all-gather.16.cloned.1.call-done = bf16[1024,8,512]{2,0,1:T(8,128)(2,1)} async-done(((bf16[8,8,512]{2,0,1:T(8,128)(2,1)}), bf16[1024,8,512]{2,0,1:T(8,128)(2,1)}) %all-gather.16.cloned.1.call-update) | async-done | bytes 8388624 | tf_op jit(solution)/shard_map/all_gather | solution.py:241
  362.4 8.3 multiply_reduce_fusion
  372.2 2.4 gather_fusion.2
  377.1 2.7 scatter_custom_fusion.2
  380.8 6.6 multiply_convert_fusion.2
  387.5 13.0 fusion.20
  400.5 10.7 scatter_fusion.1
  411.3 0.8 multiply_reduce_fusion.1
  413.6 5.5 fusion
  419.4 1.7 fusion.8
  421.1 1.4 fusion.12
  423.1 3.9 copy.120
  426.9 2.8 copy.124
  429.9 4.8 bitcast_convert_fusion
  434.7 1.4 copy.107
  436.1 2.7 fusion.41
  438.9 1.1 copy-done.13
  440.1 3.0 convolution_multiply_fusion
  443.4 0.9 copy-done.7
  444.3 0.8 multiply_reduce_fusion.2
  445.2 16.3 reduce-scatter.19.cloned.1.call-done
  461.5 1.0 reshape_bitcast_fusion
  463.9 30.9 reduce-scatter.9.cloned.1.call-done
  494.7 5.5 fusion.38
  500.6 1.4 copy-done.5
  502.0 9.2 convolution_bitcast_fusion.1
  511.2 17.6 copy.109
  528.9 1.2 copy-done.8
  530.4 13.2 convolution_bitcast_fusion
  543.6 33.1 %copy.108 = f32[1024,8,1024]{2,1,0:T(8,128)} copy(f32[1024,8,1024]{0,2,1:T(8,128)} %convolution_bitcast_fusion) | data formatting | bytes 67108864 | tf_op jit(solution)/shard_map/ecd,ecf->def/transpose | solution.py:283
  577.4 2.0 bitcast_multiply_fusion.1
  579.4 9.5 scatter_fusion
  589.8 3.3 fusion.33
  593.2 66.2 %all-reduce = (f32[1024,8]{0,1:T(8,128)}, f32[1024]{0:T(1024)}, f32[1024]{0:T(1024)}, f32[512]{0:T(512)}, f32[1024]{0:T(1024)}) all-reduce(f32[1024,8]{0,1:T(8,128)S(1)} %fusion.73, f32[1024]{0:T(1024)S(1)} %get-tuple-element.90, f32[1024]{0:T(1024)S(1)} %copy-done.60, ...), channel_id=1, replica_groups=mesh['seq'=16,'ctx'=8] {'seq','ctx'}, use_global_device_ids=true, to_apply=%region_33.34 | all-reduce | flops 11776 | bytes 94208 | tf_op jit(solution)/shard_map/psum | solution.py:360
  659.4 1.0 fusion.32
  660.4 480.7 %reduce-scatter.13.cloned.1.call-done = f32[8,1024]{1,0:T(8,128)} async-done(((f32[1024,1024]{1,0:T(8,128)}), f32[8,1024]{1,0:T(8,128)}) %reduce-scatter.13.cloned.1.call-update) | async-done | bytes 32784 | tf_op jit(solution)/shard_map/reduce_scatter | solution.py:309
  1141.1 646.9 %reduce-scatter.11.cloned.1.call-done = f32[16,1024]{1,0:T(8,128)} async-done(((f32[2048,1024]{1,0:T(8,128)}), f32[16,1024]{1,0:T(8,128)}) %reduce-scatter.11.cloned.1.call-update) | async-done | bytes 65552 | tf_op jit(solution)/shard_map/reduce_scatter | solution.py:350
  1788.0 661.8 %reduce-scatter.17.cloned.1.call-done = f32[8,8,512]{2,1,0:T(8,128)} async-done(((f32[1024,8,512]{2,1,0:T(8,128)}), f32[8,8,512]{2,1,0:T(8,128)}) %reduce-scatter.17.cloned.1.call-update) | async-done | bytes 131088 | tf_op jit(solution)/shard_map/reduce_scatter | solution.py:289
  2449.7 689.8 %reduce-scatter.15.cloned.1.call-done = f32[8,8,1024]{2,1,0:T(8,128)} async-done(((f32[1024,8,1024]{2,1,0:T(8,128)}), f32[8,8,1024]{2,1,0:T(8,128)}) %reduce-scatter.15.cloned.1.call-update) | async-done | bytes 262160 | tf_op jit(solution)/shard_map/reduce_scatter | solution.py:282
  (266 shorter events, 24.4 us)
Async XLA Ops:
  7.2 200.9 %copy-start = (bf16[1024,8]{0,1:T(8,128)(2,1)S(1)}, bf16[1024,8]{0,1:T(8,128)(2,1)}, u32[]{:S(2)}) copy-start(bf16[1024,8]{0,1:T(8,128)(2,1)} %param.22) | copy-start | bytes 49156
  7.2 73.4 %all-gather.8.cloned.1.call-start = ((), (), s32[]{:S(2)}) async-start(), calls=%async_computation.6 | async-start | bytes 4227072 | tf_op jit(solution)/shard_map/all_gather | solution.py:152
  7.9 100.4 %all-gather.18.cloned.1.call-start = ((), (), s32[]{:S(2)}) async-start(), calls=%async_computation.16 | async-start | bytes 1179648 | tf_op jit(solution)/shard_map/all_gather | solution.py:181
  8.7 71.9 %copy-start.38 = (f32[1024]{0:T(1024)}, f32[1024]{0:T(1024)S(1)}, u32[]{:S(2)}) copy-start(f32[1024]{0:T(1024)S(1)} %convert_element_type.160) | copy-start | bytes 12292
  9.8 70.8 %copy-start.71 = (f32[128]{0:T(128)}, f32[128]{0:T(128)S(1)}, u32[]{:S(2)}) copy-start(f32[128]{0:T(128)S(1)} %add_rsqrt_fusion.3) | copy-start | bytes 1540
  9.8 75.5 %copy-start.79 = (bf16[512]{0:T(512)(128)(2,1)S(1)}, bf16[512]{0:T(512)(128)(2,1)}, u32[]{:S(2)}) copy-start(bf16[512]{0:T(512)(128)(2,1)} %param.25) | copy-start | bytes 3076
  9.8 75.5 %copy-start.80 = (s32[1,128]{1,0:T(1,128)S(1)}, s32[1,128]{1,0:T(1,128)}, u32[]{:S(2)}) copy-start(s32[1,128]{1,0:T(1,128)} %param.15) | copy-start | bytes 1540
  84.4 13.4 copy-start.6
  84.4 3.5 copy-start.34
  84.4 4.3 copy-start.48
  84.4 5.1 copy-start.58
  84.4 5.4 copy-start.76
  84.4 5.4 copy-start.77
  84.5 14.0 copy-start.25
  85.2 46.9 %all-gather.10.cloned.1.call-start = ((), (), s32[]{:S(2)}) async-start(), calls=%async_computation.7 | async-start | bytes 1179648 | tf_op jit(solution)/shard_map/all_gather | solution.py:178
  85.4 12.4 copy-start.29
  85.4 12.4 copy-start.31
  87.3 114.0 %all-gather.12.cloned.1.call-start = ((), (), s32[]{:S(2)}) async-start(), calls=%async_computation.8 | async-start | bytes 2113536 | tf_op jit(solution)/shard_map/all_gather | solution.py:153
  87.9 197.4 %all-gather.14.cloned.1.call-start = ((), (), s32[]{:S(2)}) async-start(), calls=%async_computation.9 | async-start | bytes 16908288 | tf_op jit(solution)/shard_map/all_gather | solution.py:230
  88.7 273.7 %all-gather.16.cloned.1.call-start = ((), (), s32[]{:S(2)}) async-start(), calls=%async_computation.10 | async-start | bytes 8454144 | tf_op jit(solution)/shard_map/all_gather | solution.py:241
  89.4 372.1 %reduce-scatter.19.cloned.1.call-start = ((), (), s32[]{:S(2)}) async-start(), calls=%async_computation.17 | async-start | bytes 1179648
  89.8 13.9 copy-start.41
  92.2 9.3 copy-start.65
  98.5 3.7 copy-start.78
  101.4 261.0 %copy-start.4 = (f32[640,1024]{1,0:T(8,128)}, f32[640,1024]{1,0:T(8,128)S(1)}, u32[]{:S(2)}) copy-start(f32[640,1024]{1,0:T(8,128)S(1)} %gather_fusion.1) | copy-start | bytes 7864324
  108.3 26.5 copy-start.23
  134.8 3.3 copy-start.2
  134.8 3.3 copy-start.37
  134.8 3.3 copy-start.17
  138.2 63.1 %copy-start.14 = (bf16[1,128,1024]{2,1,0:T(8,128)(2,1)S(1)}, bf16[1,128,1024]{2,1,0:T(8,128)(2,1)}, u32[]{:S(2)}) copy-start(bf16[1,128,1024]{2,1,0:T(8,128)(2,1)} %param.14) | copy-start | bytes 786436
  201.3 3.1 copy-start.43
  376.9 3.7 copy-start.56
  380.6 6.9 copy-start.61
  387.4 13.0 copy-start.19
  387.4 13.0 copy-start.21
  387.5 13.0 copy-start.46
  400.5 10.8 copy-start.44
  400.5 10.8 copy-start.70
  400.5 11.6 copy-start.26
  412.9 23.2 copy-start.10
  413.5 5.6 slice-start
  413.6 5.8 slice-start.1
  429.8 64.9 %reduce-scatter.9.cloned.1.call-start = ((), (), s32[]{:S(2)}) async-start(), calls=%async_computation.11 | async-start | bytes 1179648 | tf_op jit(solution)/shard_map/reduce_scatter | solution.py:328
  436.0 705.1 %reduce-scatter.13.cloned.1.call-start = ((), (), s32[]{:S(2)}) async-start(), calls=%async_computation.13 | async-start | bytes 4227072 | tf_op jit(solution)/shard_map/reduce_scatter | solution.py:309
  438.9 4.2 copy-start.30
  438.9 4.2 copy-start.32
  438.9 1349.1 %reduce-scatter.11.cloned.1.call-start = ((), (), s32[]{:S(2)}) async-start(), calls=%async_computation.12 | async-start | bytes 8454144 | tf_op jit(solution)/shard_map/reduce_scatter | solution.py:350
  444.3 18.7 copy-start.54
  444.3 18.7 copy-start.75
  445.1 49.7 %copy-start.15 = (bf16[1,128,1024]{2,1,0:T(8,128)(2,1)S(1)}, bf16[1,128,1024]{2,1,0:T(8,128)(2,1)}, u32[]{:S(2)}) copy-start(bf16[1,128,1024]{2,1,0:T(8,128)(2,1)} %param.14) | copy-start | bytes 786436
  445.1 49.7 %copy-start.39 = (f32[1024]{0:T(1024)S(1)}, f32[1024]{0:T(1024)}, u32[]{:S(2)}) copy-start(f32[1024]{0:T(1024)} %copy-done.38) | copy-start | bytes 12292
  445.1 49.7 %copy-start.72 = (f32[128]{0:T(128)S(1)}, f32[128]{0:T(128)}, u32[]{:S(2)}) copy-start(f32[128]{0:T(128)} %copy-done.71) | copy-start | bytes 1540
  445.2 55.0 %copy-start.27 = (bf16[128,1024]{1,0:T(8,128)(2,1)}, bf16[128,1024]{1,0:T(8,128)(2,1)S(1)}, u32[]{:S(2)}) copy-start(bf16[128,1024]{1,0:T(8,128)(2,1)S(1)} %multiply_convert_fusion.4) | copy-start | bytes 786436
  500.3 1949.5 %reduce-scatter.17.cloned.1.call-start = ((), (), s32[]{:S(2)}) async-start(), calls=%async_computation.15 | async-start | bytes 16908288 | tf_op jit(solution)/shard_map/reduce_scatter | solution.py:289
  528.8 2610.7 %reduce-scatter.15.cloned.1.call-start = ((), (), s32[]{:S(2)}) async-start(), calls=%async_computation.14 | async-start | bytes 33816576 | tf_op jit(solution)/shard_map/reduce_scatter | solution.py:282
  579.4 9.5 copy-start.57
  589.0 2550.5 %copy-start.1 = (bf16[1024,8]{0,1:T(8,128)(2,1)S(1)}, bf16[1024,8]{0,1:T(8,128)(2,1)}, u32[]{:S(2)}) copy-start(bf16[1024,8]{0,1:T(8,128)(2,1)} %param.22) | copy-start | bytes 49156
  589.8 3.4 copy-start.59
  589.8 3.4 copy-start.60
  589.8 3.4 copy-start.64
  589.8 69.6 %copy-start.11 = (f32[128,1024]{1,0:T(8,128)S(1)}, f32[128,1024]{1,0:T(8,128)}, u32[]{:S(2)}) copy-start(f32[128,1024]{1,0:T(8,128)} %copy-done.10) | copy-start | bytes 1572868
  589.8 69.6 %copy-start.16 = (bf16[1,128,1024]{2,1,0:T(8,128)(2,1)S(1)}, bf16[1,128,1024]{2,1,0:T(8,128)(2,1)}, u32[]{:S(2)}) copy-start(bf16[1,128,1024]{2,1,0:T(8,128)(2,1)} %param.14) | copy-start | bytes 786436
  589.8 69.6 %copy-start.40 = (f32[1024]{0:T(1024)S(1)}, f32[1024]{0:T(1024)}, u32[]{:S(2)}) copy-start(f32[1024]{0:T(1024)} %copy-done.38) | copy-start | bytes 12292
  589.8 69.6 %copy-start.73 = (f32[128]{0:T(128)S(1)}, f32[128]{0:T(128)}, u32[]{:S(2)}) copy-start(f32[128]{0:T(128)} %copy-done.71) | copy-start | bytes 1540
  (31 other events, 42.5 us)
Sparse Core Ops, SparseCore 0:
  11.2 69.3 all-gather.7
  85.3 21.0 all-gather.17
  108.6 23.4 all-gather.9
  135.1 66.0 all-gather.11
  204.7 80.5 all-gather.13
  288.5 73.8 all-gather.15
  429.9 31.5 reduce-scatter.18
  463.9 30.7 reduce-scatter.8
  497.7 643.3 reduce-scatter.12
  1144.0 643.9 reduce-scatter.10
  1790.9 658.7 reduce-scatter.16
  2452.6 686.8 reduce-scatter.14
where the time goes:
time: 3150 us
  waiting for transfers between devices  2820 us (90%)
  local copies, waits for them, and re-layouts  100 us (3%)
  matrix products  98.1 us (3%)
  blocking collectives  66.2 us (2%)
  other arithmetic  45.6 us (1%)
    reduce_scatter x1, waiting for transfers between devices, local(): lax.psum_scatter(jnp.einsum('ecd,ecf->def', columns, d_gate_up, preferred...  690 us
    reduce_scatter x1, waiting for transfers between devices, local(): lax.psum_scatter(jnp.einsum('ecd,ecf->def', columns, act_low, preferred_e...  662 us
    reduce_scatter x1, waiting for transfers between devices, local(): lax.psum_scatter(jnp.einsum('tq,td->qd', picked, x_low, preferred_element...  647 us
    reduce_scatter x1, waiting for transfers between devices, local(): lax.psum_scatter(jnp.einsum('to,ti->oi', picked, attn_low, preferred_elem...  481 us
    all_gather x1, waiting for transfers between devices, local(): lax.all_gather(expert_in, ('seq', 'ctx'), axis=0, tiled=True)  74.4 us
    all_gather x1, waiting for transfers between devices, local(): lax.all_gather(qkv_weight, ('seq', 'ctx'), axis=0, tiled=True)  70.8 us
    psum x1, blocking collectives, local(): lax.psum((attn_local, query_local, key_local, mlp_local, router_local), (...  66.2 us
    all_gather x1, waiting for transfers between devices, local(): lax.all_gather(expert_out, ('seq', 'ctx'), axis=0, tiled=True)  65.1 us
  transfers between devices with their start and end apart: 12, of which 11 were waited for; matrix products, arithmetic and copies ran while one was open for 5% of the time, Pallas kernels for 0%

commit v1 on v0

v1 whole, which is shorter than its diff:
```python
import jax
import jax.numpy as jnp
import numpy as np
from jax import lax
from jax.sharding import PartitionSpec as P

QUERY_HEADS = 16
KEY_VALUE_HEADS = 8
PIECE = 256
EPSILON = 1e-06
ROPE_BASE = 10000.0
MASKED = -1e30
F32 = jnp.float32
BF16 = jnp.bfloat16


def rms_scale(field):
    return lax.rsqrt(jnp.mean(field * field, axis=-1, keepdims=True) + EPSILON)


def rms_back(upstream, normed, scales):
    return scales * (upstream - normed * jnp.mean(upstream * normed, axis=-1, keepdims=True))


def rotary(field, cosine, sine):
    half = field.shape[-1] // 2
    a, b = field[..., :half], field[..., half:]
    return jnp.concatenate([a * cosine - b * sine, b * cosine + a * sine], axis=-1)


def owner_of(s, c):
    if s < 8:
        return 8 * c + s
    if s < 12:
        return 64 + 4 * c + (s - 8)
    return 96 + 4 * c + (s - 12)


def dot(a, b, ca, cb):
    return lax.dot_general(a, b, (((ca,), (cb,)), ((), ())), preferred_element_type=F32)


def local(hidden_in, positions, starts, routes, qkv_weight, out_weight, expert_in, expert_out,
          router, attn_gain, query_gain, key_gain, mlp_gain, out_grad):
    rows = hidden_in.shape[1]
    width = hidden_in.shape[2]
    me = lax.axis_index("ctx")
    ns, nc = lax.axis_size("seq"), lax.axis_size("ctx")
    perm_in = [(owner_of(s, c), s * nc + c) for s in range(ns) for c in range(nc)]
    perm_out = [(b, a) for a, b in perm_in]
    ag = lambda v, ax: lax.all_gather(v, ax, axis=0, tiled=True)
    a2a = lambda v, sp, cc: lax.all_to_all(v, "ctx", sp, cc, tiled=True)
    w_qkv = ag(lax.ppermute(qkv_weight, ("seq", "ctx"), perm_in), "seq")
    w_out = ag(a2a(out_weight, 1, 0), "seq")
    w_in = ag(a2a(expert_in, 1, 0)[:, 0], "seq")
    w_down = ag(a2a(expert_out, 1, 0)[:, 0], "seq")
    x_own = hidden_in[0].astype(F32)
    x = ag(hidden_in[0], "ctx").astype(F32)
    dy = ag(out_grad[0], "ctx").astype(F32)
    pos = ag(positions[0], "ctx")
    routes_all = ag(routes[0], "ctx")
    s1 = rms_scale(x)
    attn_gain_f = attn_gain.astype(F32)
    x_low = (x * s1 * attn_gain_f).astype(BF16)
    qkv = dot(x_low, w_qkv, 1, 1)
    q, k, v = qkv[:, :128], qkv[:, 128:192], qkv[:, 192:]
    sums = lax.psum(jnp.stack([jnp.sum(q * q, 1), jnp.sum(k * k, 1)]), "ctx")
    sq = lax.rsqrt(sums[0] / 1024 + EPSILON)[:, None]
    sk = lax.rsqrt(sums[1] / 512 + EPSILON)[:, None]
    nq, nk = q * sq, k * sk
    gq = lax.dynamic_slice(query_gain, (128 * me,), (128,)).astype(F32)
    gk = lax.dynamic_slice(key_gain, (64 * me,), (64,)).astype(F32)
    freq = ROPE_BASE ** (-jnp.arange(32, dtype=F32) * 2.0 / 64)
    ang = pos.astype(F32)[:, None] * freq
    cosv, sinv = jnp.cos(ang), jnp.sin(ang)
    q_rot = rotary((nq * gq).reshape(-1, 2, 64), cosv[:, None], sinv[:, None]).astype(BF16)
    k_rot = rotary(nk * gk, cosv, sinv).astype(BF16)
    v_low = v.astype(BF16)
    places = jnp.arange(pos.shape[0], dtype=jnp.int32)
    inside = (places[:, None] >= starts) & (places[:, None] < starts + PIECE)
    label = jnp.sum(inside.astype(jnp.int32) * jnp.array([1, 2], jnp.int32), axis=1)
    allowed = (places[None, :] <= places[:, None]) | (
        (label[:, None] == label[None, :]) & (label[:, None] > 0))
    scores = jnp.einsum("tgd,sd->gts", q_rot, k_rot, preferred_element_type=F32) * 0.125
    scores = jnp.where(allowed[None], scores, MASKED)
    p = jax.nn.softmax(scores, axis=-1)
    p_low = p.astype(BF16)
    attn = jnp.einsum("gts,sd->tgd", p_low, v_low, preferred_element_type=F32)
    attn_low = attn.reshape(-1, 128).astype(BF16)
    rs = lambda t: lax.psum_scatter(t, "ctx", scatter_dimension=0, tiled=True)
    mid = x_own + rs(dot(attn_low, w_out, 1, 1))
    s2 = rms_scale(mid)
    n2 = mid * s2
    gm = mlp_gain.astype(F32)
    h_own = (n2 * gm).astype(BF16)
    gates_own = jax.nn.softmax(jnp.dot(h_own, router, preferred_element_type=F32), axis=-1)
    h = ag(h_own, "ctx")
    gates = ag(gates_own, "ctx")
    routed = jnp.any(routes_all == me, axis=1)
    gate_c = jnp.where(routed, lax.dynamic_slice(gates, (0, me), (gates.shape[0], 1))[:, 0], 0.0)[:, None]
    gu = dot(h, w_in, 1, 0)
    g, u = gu[:, :512], gu[:, 512:]
    sig = jax.nn.sigmoid(g)
    sw = g * sig
    act = (sw * u).astype(BF16)
    res = dot(act, w_down, 1, 1)
    result = (mid + rs(gate_c * res)).astype(BF16)[None]
    d_res = (gate_c * dy).astype(BF16)
    d_gate_c = jnp.where(routed, jnp.sum(dy * res, axis=1), 0.0)
    d_act = dot(d_res, w_down, 1, 0)
    d_gu = jnp.concatenate([d_act * u * sig * (1.0 + g * (1.0 - sig)), d_act * sw], axis=1).astype(BF16)
    d_h = rs(dot(d_gu, w_in, 1, 1))
    g_in = dot(h, d_gu, 0, 0)
    g_down = dot(d_res, act, 0, 0)
    d_gates = a2a(d_gate_c[:, None], 0, 1)
    d_logits = (gates_own * (d_gates - jnp.sum(gates_own * d_gates, axis=1, keepdims=True))).astype(BF16)
    d_h = d_h + dot(d_logits, router, 1, 1)
    router_loc = dot(h_own, d_logits, 0, 0)
    mlp_loc = jnp.sum(d_h * n2, axis=0)
    d_mid = out_grad[0].astype(F32) + rms_back(d_h * gm, n2, s2)
    d_branch_own = d_mid.astype(BF16)
    d_branch = ag(d_branch_own, "ctx")
    d_attn = dot(d_branch, w_out, 1, 0).astype(BF16)
    g_out = dot(d_branch, attn_low, 0, 0)
    dp = jnp.einsum("tgd,sd->gts", d_attn.reshape(-1, 2, 64), v_low, preferred_element_type=F32)
    ds = (p * (dp - jnp.sum(p * dp, axis=-1, keepdims=True))).astype(BF16)
    dq = jnp.einsum("gts,sd->tgd", ds, k_rot, preferred_element_type=F32) * 0.125
    dk = jnp.einsum("gts,tgd->sd", ds, q_rot, preferred_element_type=F32) * 0.125
    dv = jnp.einsum("gts,tgd->sd", p_low, d_attn.reshape(-1, 2, 64), preferred_element_type=F32)
    dnq = rotary(dq, cosv[:, None], -sinv[:, None]).reshape(-1, 128)
    dnk = rotary(dk, cosv, -sinv)
    gq_loc = jnp.sum(dnq * nq, axis=0)
    gk_loc = jnp.sum(dnk * nk, axis=0)
    means = lax.psum(jnp.stack([jnp.sum(dnq * gq * nq, 1), jnp.sum(dnk * gk * nk, 1)]), "ctx")
    d_q = sq * (dnq * gq - nq * means[0][:, None] / 1024)
    d_k = sk * (dnk * gk - nk * means[1][:, None] / 512)
    d_qkv = jnp.concatenate([d_q, d_k, dv], axis=1).astype(BF16)
    d_x_low = rs(dot(d_qkv, w_qkv, 1, 0))
    g_qkv = dot(d_qkv, x_low, 0, 0)
    s1_own = rms_scale(x_own)
    n1_own = x_own * s1_own
    attn_loc = jnp.sum(d_x_low * n1_own, axis=0)
    grad_input = (d_mid + rms_back(d_x_low * attn_gain_f, n1_own, s1_own))[None]
    rss = lambda t: lax.psum_scatter(t, "seq", scatter_dimension=0, tiled=True)
    grad_qkv = lax.ppermute(rss(g_qkv), ("seq", "ctx"), perm_out)
    grad_out = a2a(rss(g_out), 0, 1)
    grad_in = a2a(rss(g_in)[:, None], 0, 1)
    grad_down = a2a(rss(g_down)[:, None], 0, 1)
    gq_all = lax.dynamic_update_slice(jnp.zeros((1024,), F32), gq_loc, (128 * me,))
    gk_all = lax.dynamic_update_slice(jnp.zeros((512,), F32), gk_loc, (64 * me,))
    ga, gqo, gko, gmo, gr = lax.psum((attn_loc, gq_all, gk_all, mlp_loc, router_loc), ("seq", "ctx"))
    return result, grad_input, grad_qkv, grad_out, grad_in, grad_down, gr, ga, gqo, gko, gmo


def solution(mesh):
    t = ("seq", "ctx")
    in_specs = (P("seq", "ctx", None), P("seq", "ctx"), P("seq", None), P("seq", "ctx", None),
                P(t, None), P(t, None), P(t, None, None), P(t, None, None),
                P(), P(), P(), P(), P(), P("seq", "ctx", None))
    out_specs = (P("seq", "ctx", None), P("seq", "ctx", None), P(t, None), P(t, None),
                 P(t, None, None), P(t, None, None), P(), P(), P(), P(), P())
    return jax.shard_map(local, mesh=mesh, in_specs=in_specs, out_specs=out_specs, check_vma=False)
```

time: 3150 us -> 803 us (0.25)
  the two profiles are of different devices: /device:TPU:0 before, /device:TPU:9 now
where the time goes in v1:
time: 803 us; the launch traced here: 794 us
  waiting for transfers between devices  421 us (52%)
  blocking collectives  194 us (24%)
  matrix products  73.4 us (9%)
  starting transfers between devices  45.6 us (6%)
  other arithmetic  32.9 us (4%)
  between operations  17 us (2%)
  local copies, waits for them, and re-layouts  10.3 us (1%)
    reduce_scatter x4, waiting for transfers between devices, local(): rss = lambda t: lax.psum_scatter(t, 'seq', scatter_dimension=0, tiled=True)  231 us
    all_gather x6, waiting for transfers between devices, local(): ag = lambda v, ax: lax.all_gather(v, ax, axis=0, tiled=True)  97 us
    reduce_scatter x4, waiting for transfers between devices, local(): rs = lambda t: lax.psum_scatter(t, 'ctx', scatter_dimension=0, tiled=True)  84 us
    all_gather x5, blocking collectives, local(): ag = lambda v, ax: lax.all_gather(v, ax, axis=0, tiled=True)  69.7 us
    psum x1, blocking collectives, local(): lax.psum((attn_loc, gq_all, gk_all, mlp_loc, router_loc), ('seq', 'ctx'))  68.2 us
    dot_general x14, matrix products, dot(): lax.dot_general(a, b, (((ca,), (cb,)), ((), ())), preferred_element_type=...  50.4 us
    all_to_all x5, starting transfers between devices, local(): a2a = lambda v, sp, cc: lax.all_to_all(v, 'ctx', sp, cc, tiled=True)  30.5 us
    psum x1, blocking collectives, local(): sums = lax.psum(jnp.stack([jnp.sum(q * q, 1), jnp.sum(k * k, 1)]), 'ctx')  22.8 us
  transfers between devices with their start and end apart: 21, of which 13 were waited for; matrix products, arithmetic and copies ran while one was open for 9% of the time, Pallas kernels for 0%

profile of v1, /device:TPU:9, one launch (start us, length us, event | category | flops | bytes accessed | tf_op | source)
XLA Modules:
  0.0 794.1 jit_solution(15250596640842094345)
XLA Ops:
  8.8 6.0 all-to-all-start
  14.8 5.8 collective-permute-start
  23.4 0.9 fusion.12
  25.7 10.3 %all-gather.1 = s32[1,1024]{1,0:T(1,128)S(1)} all-gather(s32[1,128]{1,0:T(1,128)} %param.16), channel_id=3, replica_groups=mesh['seq'=16,'ctx'=8] {'ctx'}, dimensions={1}, use_global_device_ids=true | all-gather | bytes 4608 | tf_op jit(solution)/shard_map/all_gather | solution.py:51
  36.6 16.3 %all_gather.36 = bf16[1024,128]{1,0:T(8,128)(2,1)S(1)} all-gather(bf16[64,128]{1,0:T(8,128)(2,1)S(1)} %bitcast.193), channel_id=1, replica_groups=mesh['seq'=16,'ctx'=8] {'seq'}, dimensions={0}, use_global_device_ids=true | all-gather | bytes 278528 | tf_op jit(solution)/shard_map/all_gather | solution.py:51
  52.9 17.9 %all_gather.34 = bf16[256,1024]{1,0:T(8,128)(2,1)S(1)} all-gather(bf16[16,1024]{1,0:T(8,128)(2,1)S(1)} %collective-permute-done), channel_id=1, replica_groups=mesh['seq'=16,'ctx'=8] {'seq'}, dimensions={0}, use_global_device_ids=true | all-gather | bytes 557056 | tf_op jit(solution)/shard_map/all_gather | solution.py:51
  70.8 2.3 fusion.5
  73.1 2.4 fusion.43
  75.7 22.8 %psum.49 = f32[2,1024]{1,0:T(2,128)S(1)} all-reduce(f32[2,1024]{1,0:T(2,128)S(1)} %pad_maximum_fusion.16), channel_id=1, replica_groups=mesh['seq'=16,'ctx'=8] {'ctx'}, use_global_device_ids=true, to_apply=%region_4.0 | all-reduce | flops 2048 | bytes 16384 | tf_op jit(solution)/shard_map/psum | solution.py:67
  98.8 1.9 fusion.61
  100.8 5.4 fusion.97
  106.3 4.2 fusion.22
  110.6 2.7 fusion.99
  113.5 9.2 %all_to_all.120 = bf16[8,8,1024]{2,0,1:T(8,128)(2,1)} all-to-all(bf16[8,8,1024]{2,0,1:T(8,128)(2,1)S(1)} %copy.58), channel_id=1, replica_groups=mesh['seq'=16,'ctx'=8] {'ctx'}, dimensions={1} | all-to-all | bytes 262144 | tf_op jit(solution)/shard_map/all_to_all | solution.py:52
  122.9 22.8 %reduce-scatter.9.cloned.1.call-done = f32[128,1024]{1,0:T(8,128)} async-done(((f32[1024,1024]{1,0:T(8,128)}), f32[128,1024]{1,0:T(8,128)}) %reduce-scatter.9.cloned.1.call-update) | async-done | bytes 524304 | tf_op jit(solution)/shard_map/reduce_scatter | solution.py:90
  145.7 1.8 multiply_reduce_fusion.3
  148.4 11.6 %all_to_all.121 = bf16[8,8,512]{2,0,1:T(8,128)(2,1)} all-to-all(bf16[8,8,512]{2,0,1:T(8,128)(2,1)S(1)} %copy.59), channel_id=1, replica_groups=mesh['seq'=16,'ctx'=8] {'ctx'}, dimensions={1} | all-to-all | bytes 131072 | tf_op jit(solution)/shard_map/all_to_all | solution.py:52
  160.8 12.0 %all-gather.2 = s32[1,1024,4]{1,2,0:T(4,128)S(1)} all-gather(s32[1,128,4]{1,2,0:T(4,128)S(1)} %copy-done.52), channel_id=4, replica_groups=mesh['seq'=16,'ctx'=8] {'ctx'}, dimensions={1}, use_global_device_ids=true | all-gather | bytes 18432 | tf_op jit(solution)/shard_map/all_gather | solution.py:51
  172.8 1.1 fusion.98
  174.0 18.7 %all-gather.11.cloned.1.call-done = bf16[1024,1024]{1,0:T(8,128)(2,1)} async-done(((bf16[128,1024]{1,0:T(8,128)(2,1)}), bf16[1024,1024]{1,0:T(8,128)(2,1)}) %all-gather.11.cloned.1.call-update) | async-done | bytes 2097168 | tf_op jit(solution)/shard_map/all_gather | solution.py:51
  192.7 6.5 fusion.100
  199.2 2.8 multiply_convert_fusion.2
  202.0 33.0 %all-gather.15.cloned.1.call-done = bf16[1024,512]{1,0:T(8,128)(2,1)} async-done(((bf16[64,512]{1,0:T(8,128)(2,1)}), bf16[1024,512]{1,0:T(8,128)(2,1)}) %all-gather.15.cloned.1.call-update) | async-done | bytes 1048592 | tf_op jit(solution)/shard_map/all_gather | solution.py:51
  235.1 29.0 %all-gather.21.cloned.1.call-done = bf16[1,1024,1024]{2,1,0:T(8,128)(2,1)} async-done(((bf16[1,128,1024]{2,1,0:T(8,128)(2,1)}), bf16[1,1024,1024]{2,1,0:T(8,128)(2,1)}) %all-gather.21.cloned.1.call-update) | async-done | bytes 2097168 | tf_op jit(solution)/shard_map/all_gather | solution.py:51
  264.1 5.2 fusion.9
  269.9 3.5 all-to-all-start.3
  273.4 4.5 all-to-all-done.3
  277.9 13.3 %all_gather.38 = f32[1024,8]{0,1:T(8,128)S(1)} all-gather(f32[128,8]{0,1:T(8,128)S(1)} %get-tuple-element.25), channel_id=1, replica_groups=mesh['seq'=16,'ctx'=8] {'ctx'}, dimensions={0}, use_global_device_ids=true | all-gather | bytes 36864 | tf_op jit(solution)/shard_map/all_gather | solution.py:51
  291.2 5.4 multiply_convert_fusion.1
  296.6 1.0 copy-done.58
  298.0 4.3 fusion.20
  303.0 33.9 %reduce-scatter.13.cloned.1.call-done = f32[128,1024]{1,0:T(8,128)} async-done(((f32[1024,1024]{1,0:T(8,128)}), f32[128,1024]{1,0:T(8,128)}) %reduce-scatter.13.cloned.1.call-update) | async-done | bytes 524304 | tf_op jit(solution)/shard_map/reduce_scatter | solution.py:90
  336.9 2.1 multiply_reduce_fusion
  338.9 1.9 fusion.94
  341.1 4.5 fusion.34
  345.7 6.5 fusion.19
  352.2 16.3 %all-gather.17.cloned.1.call-done = bf16[1024,1024]{1,0:T(8,128)(2,1)} async-done(((bf16[128,1024]{1,0:T(8,128)(2,1)}), bf16[1024,1024]{1,0:T(8,128)(2,1)}) %all-gather.17.cloned.1.call-update) | async-done | bytes 2097168 | tf_op jit(solution)/shard_map/all_gather | solution.py:51
  368.5 2.4 convolution_convert_fusion
  371.0 4.8 fusion.1
  375.8 1.1 slice-done.1
  376.9 2.4 fusion.3
  380.5 1.4 fusion.28
  383.8 12.2 %psum.50 = f32[2,1024]{1,0:T(2,128)S(1)} all-reduce(f32[2,1024]{1,0:T(2,128)S(1)} %pad_maximum_fusion.17), channel_id=1, replica_groups=mesh['seq'=16,'ctx'=8] {'ctx'}, use_global_device_ids=true, to_apply=%region_21.22 | all-reduce | flops 2048 | bytes 16384 | tf_op jit(solution)/shard_map/psum | solution.py:134
  397.6 5.1 fusion.29
  403.4 1.9 fusion.41
  405.6 2.5 fusion.101
  408.2 3.9 fusion.55
  412.2 4.6 broadcast_multiply_fusion
  416.9 26.5 %reduce-scatter.23.cloned.1.call-done = f32[64,512]{1,0:T(8,128)} async-done(((f32[1024,512]{1,0:T(8,128)}), f32[64,512]{1,0:T(8,128)}) %reduce-scatter.23.cloned.1.call-update) | async-done | bytes 131088 | tf_op jit(solution)/shard_map/reduce_scatter | solution.py:144
  443.4 1.7 copy.68
  445.1 7.1 all-to-all-start.6
  452.2 72.0 %reduce-scatter.21.cloned.1.call-done = f32[64,1024]{1,0:T(8,128)} async-done(((f32[1024,1024]{1,0:T(8,128)}), f32[64,1024]{1,0:T(8,128)}) %reduce-scatter.21.cloned.1.call-update) | async-done | bytes 262160 | tf_op jit(solution)/shard_map/reduce_scatter | solution.py:144
  524.2 1.9 copy.66
  526.1 6.7 all-to-all-start.5
  532.9 66.2 %reduce-scatter.17.cloned.1.call-done = f32[16,1024]{1,0:T(8,128)} async-done(((f32[256,1024]{1,0:T(8,128)}), f32[16,1024]{1,0:T(8,128)}) %reduce-scatter.17.cloned.1.call-update) | async-done | bytes 65552 | tf_op jit(solution)/shard_map/reduce_scatter | solution.py:144
  599.1 8.3 %collective-permute-start.1 = (f32[16,1024]{1,0:T(8,128)}, f32[16,1024]{1,0:T(8,128)S(1)}, u32[]{:S(2)}, u32[]{:S(2)}) collective-permute-start(f32[16,1024]{1,0:T(8,128)} %reduce-scatter.17.cloned.1.call-done), channel_id=1, source_target_pairs={{0,0},{1,8},{2,16},{3,24},{4,32},{5,40},{6,48},{7,56},{8,1},{9,9},... | collective-permute-start | bytes 196616 | tf_op jit(solution)/shard_map/ppermute | solution.py:145
  607.4 66.7 %reduce-scatter.19.cloned.1.call-done = f32[64,128]{1,0:T(8,128)} async-done(((f32[1024,128]{1,0:T(8,128)}), f32[64,128]{1,0:T(8,128)}) %reduce-scatter.19.cloned.1.call-update) | async-done | bytes 32784 | tf_op jit(solution)/shard_map/reduce_scatter | solution.py:144
  674.0 7.2 all-to-all-start.4
  682.1 0.9 copy.77
  683.4 2.6 all-to-all-done.4
  686.0 27.3 %reduce-scatter.15.cloned.1.call-done = f32[128,1024]{1,0:T(8,128)} async-done(((f32[1024,1024]{1,0:T(8,128)}), f32[128,1024]{1,0:T(8,128)}) %reduce-scatter.15.cloned.1.call-update) | async-done | bytes 524304 | tf_op jit(solution)/shard_map/reduce_scatter | solution.py:90
  713.3 1.3 fusion.50
  714.6 68.2 %all-reduce = (f32[1024,8]{0,1:T(8,128)}, f32[1024]{0:T(1024)}, f32[1024]{0:T(1024)}, f32[512]{0:T(512)}, f32[1024]{0:T(1024)}) all-reduce(f32[1024,8]{0,1:T(8,128)S(1)} %fusion.102, f32[1024]{0:T(1024)S(1)} %get-tuple-element.17, f32[1024]{0:T(1024)S(1)} %dynamic_update_slice.6, ...), channel_id=1, replica_groups=mesh['seq'=16,'ctx'=8] {'seq','ctx'}, use_global_device_ids=true, to_apply=%region_28.29 | all-reduce | flops 11776 | bytes 94208 | tf_op jit(solution)/shard_map/psum | solution.py:151
  782.8 2.3 fusion.49
  (207 shorter events, 18.1 us)
Async XLA Ops:
  8.0 164.8 %copy-start = (bf16[1024,8]{0,1:T(8,128)(2,1)S(1)}, bf16[1024,8]{0,1:T(8,128)(2,1)}, u32[]{:S(2)}) copy-start(bf16[1024,8]{0,1:T(8,128)(2,1)} %param.23) | copy-start | bytes 49156
  8.0 62.8 %all-gather.19.cloned.1.call-start = ((), (), s32[]{:S(2)}) async-start(), calls=%async_computation.27 | async-start | bytes 2359296 | tf_op jit(solution)/shard_map/all_gather | solution.py:51
  8.8 27.8 %all-to-all-start = ((bf16[8,8,128]{2,0,1:T(8,128)(2,1)}), bf16[8,8,128]{2,0,1:T(8,128)(2,1)S(1)}, u32[]{:S(2)}, u32[]{:S(2)}) async-start(bf16[8,8,128]{2,0,1:T(8,128)(2,1)} %bitcast.208), calls=%async_computation | async-start | bytes 32768 | tf_op jit(solution)/shard_map/all_to_all | solution.py:52
  14.8 130.9 %reduce-scatter.9.cloned.1.call-start = ((), (), s32[]{:S(2)}) async-start(), calls=%async_computation.15 | async-start | bytes 4718592 | tf_op jit(solution)/shard_map/reduce_scatter | solution.py:90
  14.8 38.1 %collective-permute-start = (bf16[16,1024]{1,0:T(8,128)(2,1)}, bf16[16,1024]{1,0:T(8,128)(2,1)S(1)}, u32[]{:S(2)}, u32[]{:S(2)}) collective-permute-start(bf16[16,1024]{1,0:T(8,128)(2,1)} %param.19), channel_id=1, source_target_pairs={{0,0},{8,1},{16,2},{24,3},{32,4},{40,5},{48,6},{56,7},{1,8},{9,9},... | collective-permute-start | bytes 98312 | tf_op jit(solution)/shard_map/ppermute | solution.py:53
  22.0 76.7 %copy-start.43 = (f32[128]{0:T(128)}, f32[128]{0:T(128)S(1)}, u32[]{:S(2)}) copy-start(f32[128]{0:T(128)S(1)} %dynamic-slice_convert_fusion) | copy-start | bytes 1540
  25.0 73.5 %copy-start.45 = (f32[64]{0:T(128)}, f32[64]{0:T(128)S(1)}, u32[]{:S(2)}) copy-start(f32[64]{0:T(128)S(1)} %dynamic-slice_convert_fusion.1) | copy-start | bytes 772
  25.7 49.8 %copy-start.31 = (f32[1024]{0:T(1024)}, f32[1024]{0:T(1024)S(1)}, u32[]{:S(2)}) copy-start(f32[1024]{0:T(1024)S(1)} %convert_element_type.74) | copy-start | bytes 12292
  52.9 57.6 %copy-start.5 = (bf16[1024,128]{1,0:T(8,128)(2,1)}, bf16[1024,128]{1,0:T(8,128)(2,1)S(1)}, u32[]{:S(2)}) copy-start(bf16[1024,128]{1,0:T(8,128)(2,1)S(1)} %all_gather.36) | copy-start | bytes 786436
  70.8 4.9 copy-start.8
  98.5 7.7 copy-start.26
  98.5 7.7 copy-start.28
  100.7 5.6 copy-start.17
  100.7 5.6 copy-start.19
  100.8 5.5 copy-start.13
  100.8 5.5 copy-start.15
  106.3 4.3 copy-start.39
  110.6 12.3 %copy-start.51 = (bf16[1024]{0:T(1024)(128)(2,1)S(1)}, bf16[1024]{0:T(1024)(128)(2,1)}, u32[]{:S(2)}) copy-start(bf16[1024]{0:T(1024)(128)(2,1)} %param.27) | copy-start | bytes 6148
  110.6 35.1 %copy-start.3 = (bf16[1,128,1024]{2,1,0:T(8,128)(2,1)S(1)}, bf16[1,128,1024]{2,1,0:T(8,128)(2,1)}, u32[]{:S(2)}) copy-start(bf16[1,128,1024]{2,1,0:T(8,128)(2,1)} %param.15) | copy-start | bytes 786436
  113.3 35.1 %copy-start.30 = (bf16[8,8,512]{2,1,0:T(8,128)(2,1)S(1)}, bf16[8,8,512]{2,1,0:T(8,128)(2,1)}, u32[]{:S(2)}) copy-start(bf16[8,8,512]{2,1,0:T(8,128)(2,1)} %param.22) | copy-start | bytes 196612
  113.3 47.5 %copy-start.52 = (s32[1,128,4]{1,2,0:T(4,128)S(1)}, s32[1,128,4]{1,2,0:T(4,128)}, u32[]{:S(2)}) copy-start(s32[1,128,4]{1,2,0:T(4,128)} %param.18) | copy-start | bytes 6148
  113.4 60.6 %all-gather.13.cloned.1.call-start = ((), (), s32[]{:S(2)}) async-start(), calls=%async_computation.17 | async-start | bytes 2228224 | tf_op jit(solution)/shard_map/all_gather | solution.py:51
  122.8 69.9 %all-gather.11.cloned.1.call-start = ((), (), s32[]{:S(2)}) async-start(), calls=%async_computation.16 | async-start | bytes 2359296 | tf_op jit(solution)/shard_map/all_gather | solution.py:51
  122.8 25.5 %copy-start.24 = (f32[1024]{0:T(1024)}, f32[1024]{0:T(1024)S(1)}, u32[]{:S(2)}) copy-start(f32[1024]{0:T(1024)S(1)} %convert_element_type.83) | copy-start | bytes 12292
  148.4 86.7 %all-gather.15.cloned.1.call-start = ((), (), s32[]{:S(2)}) async-start(), calls=%async_computation.18 | async-start | bytes 1114112 | tf_op jit(solution)/shard_map/all_gather | solution.py:51
  160.1 104.0 %all-gather.21.cloned.1.call-start = ((), (), s32[]{:S(2)}) async-start(), calls=%async_computation.28 | async-start | bytes 2359296 | tf_op jit(solution)/shard_map/all_gather | solution.py:51
  269.9 8.0 %all-to-all-start.3 = ((f32[8,128,1]{1,2,0:T(1,128)}), f32[8,128,1]{1,2,0:T(1,128)S(1)}, u32[]{:S(2)}, u32[]{:S(2)}) async-start(f32[8,128,1]{1,2,0:T(1,128)} %bitcast.30), calls=%async_computation.6 | async-start | bytes 8192 | tf_op jit(solution)/shard_map/all_to_all | solution.py:52
  273.3 63.5 %reduce-scatter.13.cloned.1.call-start = ((), (), s32[]{:S(2)}) async-start(), calls=%async_computation.20 | async-start | bytes 4718592 | tf_op jit(solution)/shard_map/reduce_scatter | solution.py:90
  291.2 5.4 copy-start.37
  291.2 6.8 copy-start.57
  302.4 66.2 %all-gather.17.cloned.1.call-start = ((), (), s32[]{:S(2)}) async-start(), calls=%async_computation.21 | async-start | bytes 2359296 | tf_op jit(solution)/shard_map/all_gather | solution.py:51
  338.9 6.6 copy-start.49
  340.8 102.6 %reduce-scatter.23.cloned.1.call-start = ((), (), s32[]{:S(2)}) async-start(), calls=%async_computation.26 | async-start | bytes 2228224 | tf_op jit(solution)/shard_map/reduce_scatter | solution.py:144
  345.6 178.6 %reduce-scatter.21.cloned.1.call-start = ((), (), s32[]{:S(2)}) async-start(), calls=%async_computation.25 | async-start | bytes 4456448 | tf_op jit(solution)/shard_map/reduce_scatter | solution.py:144
  352.1 16.4 %copy-start.6 = (bf16[1024,128]{1,0:T(8,128)(2,1)S(1)}, bf16[1024,128]{1,0:T(8,128)(2,1)}, u32[]{:S(2)}) copy-start(bf16[1024,128]{1,0:T(8,128)(2,1)} %copy-done.5) | copy-start | bytes 786436
  352.1 18.8 %copy-start.40 = (f32[2,1024]{1,0:T(2,128)S(1)}, f32[2,1024]{1,0:T(2,128)}, u32[]{:S(2)}) copy-start(f32[2,1024]{1,0:T(2,128)} %copy-done.39) | copy-start | bytes 24580
  352.2 246.9 %reduce-scatter.17.cloned.1.call-start = ((), (), s32[]{:S(2)}) async-start(), calls=%async_computation.23 | async-start | bytes 1114112 | tf_op jit(solution)/shard_map/reduce_scatter | solution.py:144
  370.9 4.9 copy-start.21
  371.0 4.9 slice-start
  371.0 5.9 slice-start.1
  397.6 5.1 copy-start.11
  397.6 5.8 copy-start.9
  397.6 5.8 copy-start.32
  397.6 5.8 copy-start.48
  405.3 268.8 %reduce-scatter.19.cloned.1.call-start = ((), (), s32[]{:S(2)}) async-start(), calls=%async_computation.24 | async-start | bytes 557056 | tf_op jit(solution)/shard_map/reduce_scatter | solution.py:144
  408.1 4.0 copy-start.38
  408.1 305.1 %reduce-scatter.15.cloned.1.call-start = ((), (), s32[]{:S(2)}) async-start(), calls=%async_computation.22 | async-start | bytes 4718592 | tf_op jit(solution)/shard_map/reduce_scatter | solution.py:90
  412.1 370.6 %reduce-scatter.11.cloned.1.call-start = ((), (), s32[]{:S(2)}) async-start(), calls=%async_computation.19 | async-start | bytes 4718592 | tf_op jit(solution)/shard_map/reduce_scatter | solution.py:90
  416.7 116.1 %copy-start.55 = (f32[128]{0:T(128)S(1)}, f32[128]{0:T(128)}, u32[]{:S(2)}) copy-start(f32[128]{0:T(128)} %get-tuple-element.40) | copy-start | bytes 1540
  416.7 264.5 %copy-start.4 = (bf16[128,1024]{1,0:T(8,128)(2,1)S(1)}, bf16[128,1024]{1,0:T(8,128)(2,1)}, u32[]{:S(2)}) copy-start(bf16[128,1024]{1,0:T(8,128)(2,1)} %multiply_convert_fusion.4) | copy-start | bytes 786436
  416.7 264.5 %copy-start.35 = (bf16[128,8]{0,1:T(8,128)(2,1)S(1)}, bf16[128,8]{0,1:T(8,128)(2,1)}, u32[]{:S(2)}) copy-start(bf16[128,8]{0,1:T(8,128)(2,1)} %multiply_convert_fusion.6) | copy-start | bytes 6148
  416.7 266.2 %copy-start.54 = (f32[128]{0:T(128)S(1)}, f32[128]{0:T(128)}, u32[]{:S(2)}) copy-start(f32[128]{0:T(128)} %get-tuple-element.11) | copy-start | bytes 1540
  416.8 266.4 %copy-start.56 = (f32[64]{0:T(128)S(1)}, f32[64]{0:T(128)}, u32[]{:S(2)}) copy-start(f32[64]{0:T(128)} %get-tuple-element.13) | copy-start | bytes 772
  416.8 296.5 %copy-start.33 = (f32[1024]{0:T(1024)S(1)}, f32[1024]{0:T(1024)}, u32[]{:S(2)}) copy-start(f32[1024]{0:T(1024)} %copy-done.31) | copy-start | bytes 12292
  416.8 297.8 %copy-start.36 = (f32[1024]{0:T(1024)S(1)}, f32[1024]{0:T(1024)}, u32[]{:S(2)}) copy-start(f32[1024]{0:T(1024)} %get-tuple-element.15) | copy-start | bytes 12292
  416.8 366.0 %copy-start.7 = (bf16[1,128,1024]{2,1,0:T(8,128)(2,1)S(1)}, bf16[1,128,1024]{2,1,0:T(8,128)(2,1)}, u32[]{:S(2)}) copy-start(bf16[1,128,1024]{2,1,0:T(8,128)(2,1)} %param.28) | copy-start | bytes 786436
  416.8 366.0 %copy-start.25 = (f32[1024]{0:T(1024)S(1)}, f32[1024]{0:T(1024)}, u32[]{:S(2)}) copy-start(f32[1024]{0:T(1024)} %copy-done.24) | copy-start | bytes 12292
  416.8 365.9 %copy-start.42 = (f32[128]{0:T(128)S(1)}, f32[128]{0:T(128)}, u32[]{:S(2)}) copy-start(f32[128]{0:T(128)} %copy-done.41) | copy-start | bytes 1540
  416.8 365.9 %copy-start.50 = (f32[128]{0:T(128)S(1)}, f32[128]{0:T(128)}, u32[]{:S(2)}) copy-start(f32[128]{0:T(128)} %copy-done.49) | copy-start | bytes 1540
  416.9 369.5 %copy-start.1 = (bf16[1024,8]{0,1:T(8,128)(2,1)S(1)}, bf16[1024,8]{0,1:T(8,128)(2,1)}, u32[]{:S(2)}) copy-start(bf16[1024,8]{0,1:T(8,128)(2,1)} %param.23) | copy-start | bytes 49156
  445.1 81.1 %all-to-all-start.6 = ((f32[64,1,512]{2,1,0:T(1,128)}), f32[64,1,512]{2,1,0:T(1,128)S(1)}, u32[]{:S(2)}, u32[]{:S(2)}) async-start(f32[64,1,512]{2,1,0:T(1,128)} %copy.68), calls=%async_computation.14 | async-start | bytes 262144 | tf_op jit(solution)/shard_map/all_to_all | solution.py:52
  526.1 81.2 %all-to-all-start.5 = ((f32[64,1,1024]{2,1,0:T(1,128)}), f32[64,1,1024]{2,1,0:T(1,128)S(1)}, u32[]{:S(2)}, u32[]{:S(2)}) async-start(f32[64,1,1024]{2,1,0:T(1,128)} %copy.66), calls=%async_computation.12 | async-start | bytes 524288 | tf_op jit(solution)/shard_map/all_to_all | solution.py:52
  599.1 86.9 %collective-permute-start.1 = (f32[16,1024]{1,0:T(8,128)}, f32[16,1024]{1,0:T(8,128)S(1)}, u32[]{:S(2)}, u32[]{:S(2)}) collective-permute-start(f32[16,1024]{1,0:T(8,128)} %reduce-scatter.17.cloned.1.call-done), channel_id=1, source_target_pairs={{0,0},{1,8},{2,16},{3,24},{4,32},{5,40},{6,48},{7,56},{8,1},{9,9},... | collective-permute-start | bytes 196616 | tf_op jit(solution)/shard_map/ppermute | solution.py:145
  674.0 11.9 %all-to-all-start.4 = ((f32[8,8,128]{2,1,0:T(8,128)}), f32[8,8,128]{2,1,0:T(8,128)S(1)}, u32[]{:S(2)}, u32[]{:S(2)}) async-start(f32[8,8,128]{2,1,0:T(8,128)} %bitcast.198), calls=%async_computation.10 | async-start | bytes 65536 | tf_op jit(solution)/shard_map/all_to_all | solution.py:52
  (19 other events, 35.3 us)
Sparse Core Ops, SparseCore 0:
  10.6 28.0 all-gather.18
  113.5 32.1 reduce-scatter.8
  302.5 34.3 reduce-scatter.12
Sparse Core Ops, SparseCore 1:
  122.9 40.3 all-gather.12
  165.4 27.3 all-gather.10
  194.7 40.3 all-gather.14
  236.8 27.2 all-gather.20
  340.9 27.5 all-gather.16
  371.8 71.5 reduce-scatter.22
  447.0 77.2 reduce-scatter.20
  527.3 71.7 reduce-scatter.16
  602.5 71.5 reduce-scatter.18
  676.5 36.7 reduce-scatter.14
  715.5 37.5 reduce-scatter.10

commit v2 on v1

v2 whole, which is shorter than its diff:
```python
import functools

import jax
import jax.numpy as jnp
from jax import lax
from jax.experimental import pallas as pl
from jax.experimental.pallas import tpu as pltpu
from jax.sharding import PartitionSpec as P

PIECE = 256
EPSILON = 1e-06
ROPE_BASE = 10000.0
MASKED = -1e30
F32 = jnp.float32
BF16 = jnp.bfloat16
MESH = pl.DeviceIdType.MESH
HI = lax.Precision.HIGHEST
SEMS = 320


def dot(a, b, ca, cb, precision=None):
    return lax.dot_general(a, b, (((ca,), (cb,)), ((), ())), precision=precision,
                           preferred_element_type=F32)


def iota(shape, axis):
    return lax.broadcasted_iota(jnp.int32, shape, axis)


class Sems:
    def __init__(self, send, recv):
        self.send, self.recv, self.used, self.log = send, recv, 0, []

    def take(self, count):
        base = self.used
        self.used += count
        assert self.used <= SEMS
        return base


def kernel(hid, og, wq, wo, wi, wd, par1, par2, tbl, starts, rt, rout,
           res_o, gi_o, gq_o, go_o, gin_o, gdn_o, sm_o,
           xl, dyb, hb, dbb, tb, wqb, wo1, wi1, wd1, wob, wib, wdb,
           qkvb, scb, qr, ka, kb, va, vb, at, pb, drawb, dgub, agb,
           part, sibb, rin, st, stb, st2, gtb, dgs, dgr, midb, dab, dqb, dkv, dnb, dqkv,
           gin_s, gin_r, gdn_s, gdn_r, go_s, go_r, gq_s, gq_r, gsum_in, gsum_dn, gsum_o,
           sm3, sm1, sm2, acc, send, recv):
    s, c = lax.axis_index("seq"), lax.axis_index("ctx")
    z, k = lax.div(c, 2), lax.rem(c, 2)
    sems = Sems(send, recv)
    sib = (s, z * 2 + 1 - k)
    drain = []

    def zdev(dz):
        return (s, lax.rem(z + dz, 4) * 2 + k)

    def cpeer(dc):
        return (s, lax.rem(c + dc, 8))

    def speer(ds):
        return (lax.rem(s + ds, 16), c)

    def copy(src, dst, index, slot, dev):
        return pltpu.make_async_remote_copy(src_ref=src, dst_ref=dst, send_sem=send.at[index],
                                            recv_sem=recv.at[slot], device_id=dev, device_id_type=MESH)

    def got(dst, slot):
        copy(dst, dst, slot, slot, sib).wait_recv()

    def sent(src, index):
        copy(src, src, index, index, sib).wait_send()

    c4, r4 = lax.div(c, 4), lax.rem(c, 4)
    tg = jnp.where(s < 8, s, jnp.where(s < 12, 2 * (s - 8) + c4, 2 * (s - 12) + c4))
    ts = jnp.where(s < 8, c, jnp.where(s < 12, 8 + r4, 12 + r4))
    mine = tg == c

    def owner(j):
        half = lax.div(c, 2)
        odd = 4 * lax.rem(c, 2)
        os = jnp.where(j < 8, c, jnp.where(j < 12, 8 + half, 12 + half))
        oc = jnp.where(j < 8, j, jnp.where(j < 12, odd + j - 8, odd + j - 12))
        return os, oc

    def not_me(dev):
        return jnp.logical_or(dev[0] != s, dev[1] != c)

    bar = pltpu.get_barrier_semaphore()
    for dc in range(1, 8):
        pl.semaphore_signal(bar, inc=1, device_id=cpeer(dc), device_id_type=MESH)

    def sig_seq(ds, _):
        pl.semaphore_signal(bar, inc=1, device_id=speer(ds), device_id_type=MESH)
        return 0
    lax.fori_loop(1, 16, sig_seq, 0)

    def sig_own(j, _):
        dev = owner(j)

        @pl.when(not_me(dev))
        def _():
            pl.semaphore_signal(bar, inc=1, device_id=dev, device_id_type=MESH)
        dev2 = (j, tg)

        @pl.when(not_me(dev2))
        def _():
            pl.semaphore_signal(bar, inc=1, device_id=dev2, device_id_type=MESH)
        return 0
    lax.fori_loop(0, 16, sig_own, 0)

    gain_a = par1[0:1, :]
    gain_m = par1[1:2, :]
    gains = par2[pl.ds(c, 1), :]
    x = hid[...].astype(F32)
    s1 = lax.rsqrt(jnp.mean(x * x, axis=-1, keepdims=True) + EPSILON)
    xl[c] = (x * s1 * gain_a).astype(BF16)
    tb[c] = tbl[...]
    dyb[c] = og[...]
    wo1[c] = wo[c]
    wi1[c] = wi[c]
    wd1[c] = wd[c]

    @pl.when(mine)
    def _():
        wqb[ts] = wq[...]
    pl.semaphore_wait(bar, 54 - 2 * mine.astype(jnp.int32))

    def ag_start(buf):
        base = sems.take(7)
        for dz in (1, 3, 2):
            copy(buf.at[c], buf.at[c], base + dz - 1, base + dz - 1, zdev(dz)).start()
        copy(buf.at[c], buf.at[c], base + 3, base + 3, sib).start()

        def done():
            for i in range(7):
                sent(buf.at[c], base + i)
        drain.append(done)
        return base

    def ag_chip(buf, base, n, dz):
        ch = lax.rem(z - dz + 4, 4)
        b = ch * 2 + k

        @pl.when(n > 0)
        def _():
            got(buf.at[b], base + dz - 1)
            copy(buf.at[b], buf.at[b], base + 3 + dz, base + 3 + dz, sib).start()
        got(buf.at[b], base + 3 + dz)
        return ch

    def gray(n):
        return jnp.where(n == 2, 3, jnp.where(n == 3, 2, n))

    xbase = ag_start(xl)
    qs = sems.take(16)

    def send_q(j, _):
        dev = (j, tg)

        @pl.when(not_me(dev))
        def _():
            copy(wq, wqb.at[ts], qs + j, qs + ts, dev).start()
        return 0
    lax.fori_loop(0, 16, send_q, 0)
    tbase = ag_start(tb)
    w1 = sems.take(21)
    for a, (src, dst) in enumerate(((wo, wo1), (wd, wd1), (wi, wi1))):
        for dc in range(1, 8):
            dev = cpeer(dc)
            copy(src.at[dev[1]], dst.at[c], w1 + 7 * a + dc - 1, w1 + 7 * a + dc - 1, dev).start()

    ws = sems.take(45)
    for a, (one, full, width) in enumerate(((wo1, wob, 128), (wd1, wdb, 512), (wi1, wib, 1024))):
        for dc in range(1, 8):
            got(one.at[0], w1 + 7 * a + dc - 1)
        full[s] = one[...].astype(F32).reshape(64, width).astype(BF16)

        def send_w(ds, _, a=a, full=full):
            copy(full.at[s], full.at[s], ws + 15 * a + ds - 1, ws + 15 * a + ds - 1, speer(ds)).start()
            return 0
        lax.fori_loop(1, 16, send_w, 0)

    def got_w(a, full):
        def body(ds, _):
            got(full.at[0], ws + 15 * a + ds - 1)
            return 0
        lax.fori_loop(1, 16, body, 0)

    def wait_q(j, _):
        @pl.when(not_me(owner(j)))
        def _():
            got(wqb.at[0], qs + j)
        return 0
    lax.fori_loop(0, 16, wait_q, 0)

    lane = iota((1, 256), 1)
    sel8 = jnp.where(iota((8, 256), 0) == 0, jnp.where(iota((8, 256), 1) < 128, 1.0, 0.0),
                     jnp.where((iota((8, 256), 0) == 1) & (iota((8, 256), 1) >= 128)
                               & (iota((8, 256), 1) < 192), 1.0, 0.0))

    def put_rows(ref, ch, rows):
        ref[pl.ds(2 * ch, 1), :] = rows[0:1, 0:128]
        ref[pl.ds(2 * ch + 1, 1), :] = rows[0:1, 128:256]
        ref[pl.ds(8 + 2 * ch, 1), :] = rows[1:2, 0:128]
        ref[pl.ds(9 + 2 * ch, 1), :] = rows[1:2, 128:256]

    def qkv_step(n, _):
        dz = gray(n)
        ch = ag_chip(xl, xbase, n, dz)
        qkv = dot(xl[pl.ds(2 * ch, 2)].reshape(256, 1024), wqb[...].reshape(256, 1024), 1, 1)
        qkvb[ch] = qkv
        put_rows(st, ch, dot(sel8, qkv * qkv, 1, 1, HI))
        return 0
    lax.fori_loop(0, 4, qkv_step, 0)

    def all_reduce(own, slots):
        base = sems.take(7)
        slots[c] = own[...]
        for dc in range(1, 8):
            copy(slots.at[c], slots.at[c], base + dc - 1, base + dc - 1, cpeer(dc)).start()

        def finish():
            for dc in range(1, 8):
                got(slots.at[0], base + dc - 1)
            return jnp.sum(slots[...], axis=0)

        def done():
            for i in range(7):
                sent(slots.at[c], base + i)
        drain.append(done)
        return finish

    row16 = iota((16, 128), 0)
    count = jnp.where(row16 < 8, 1.0 / 1024, 1.0 / 512)
    finish = all_reduce(st, stb.at[0])
    dybase = ag_start(dyb)

    def table_step(n, _):
        ag_chip(tb, tbase, n, gray(n))
        return 0
    lax.fori_loop(0, 4, table_step, 0)
    st[...] = lax.rsqrt(finish() * count + EPSILON)

    def pick(b):
        r, l = iota((16, 256), 0), iota((16, 256), 1)
        return jnp.where(((r == b) & (l < 128)) | ((r == 8 + b) & (l >= 128) & (l < 192)), 1.0, 0.0)

    even = lax.rem(lax.div(iota((128, 128), 1), 32), 2) == 0
    low64 = iota((128, 128), 1) < 64

    def tables(b):
        t = tb[b]
        t2 = pltpu.roll(t, 32, 1)
        return jnp.where(even, t, t2), jnp.where(even, -t2, t)

    def partner(w):
        return jnp.where(even, pltpu.roll(w, 96, 1), pltpu.roll(w, 32, 1))

    def rope_step(b, _):
        rows = pl.ds(lax.rem(b, 2) * 128, 128)
        ch = lax.div(b, 2)
        scale = dot(st[...], pick(b), 0, 0, HI) + jnp.where(lane >= 192, 1.0, 0.0)
        scb[ch, rows, :] = scale
        normed = qkvb[ch, rows, :] * scale
        qkvb[ch, rows, :] = normed
        w = normed * gains
        cs, sn = tables(b)
        wq_, wk_ = w[:, :128], w[:, 128:]
        qr[b] = ((wq_ * cs + partner(wq_) * sn) * 0.125).astype(BF16)
        kv = wk_ * jnp.where(low64, cs, 1.0) + partner(wk_) * jnp.where(low64, sn, 0.0)
        k0 = jnp.where(low64, kv, 0.0)
        v1 = jnp.where(low64, 0.0, kv)
        ka[b] = k0.astype(BF16)
        kb[b] = pltpu.roll(k0, 64, 1).astype(BF16)
        va[b] = pltpu.roll(v1, 64, 1).astype(BF16)
        vb[b] = v1.astype(BF16)
        return 0
    lax.fori_loop(0, 8, rope_step, 0)

    def rs_new():
        return sems.take(4), sems.take(3)

    def rs_first(r, base, ch):
        copy(part.at[r, ch, 1 - k], sibb.at[r, ch], base[0] + ch, base[0] + ch, sib).start()

    def rs_second(r, base, ch):
        got(sibb.at[r, ch], base[0] + ch)
        part[r, ch, k] = (part[r, ch, k].astype(F32) + sibb[r, ch].astype(F32)).astype(BF16)
        dz = lax.rem(ch - z + 4, 4)

        @pl.when(dz > 0)
        def _():
            copy(part.at[r, ch, k], rin.at[r, dz - 1], base[1] + dz - 1, base[1] + dz - 1,
                 (s, ch * 2 + k)).start()

    def rs_finish(r, base):
        for i in range(3):
            got(rin.at[r, i], base[1] + i)

        def done():
            for i in range(4):
                sent(part.at[r, 0, 0], base[0] + i)
            for i in range(3):
                sent(part.at[r, 0, 0], base[1] + i)
        drain.append(done)
        total = part[r, z, k].astype(F32)
        for i in range(3):
            total = total + rin[r, i].astype(F32)
        return total

    st0, st1 = starts[0, 0], starts[0, 1]

    def limits(ch):
        row = ch * 256 + iota((256, 1), 0)
        lim = jnp.where((row >= st0) & (row < st0 + PIECE), st0 + PIECE - 1, row)
        return jnp.where((row >= st1) & (row < st1 + PIECE), st1 + PIECE - 1, lim)

    def keys(ref, length):
        return ref[0:length // 128].reshape(length, 128)

    def attend(ch, length):
        q = qr[pl.ds(2 * ch, 2)].reshape(256, 128)
        allowed = iota((256, length), 1) <= limits(ch)
        out = None
        for h, (kk, vv) in enumerate(((ka, va), (kb, vb))):
            sc = jnp.where(allowed, dot(q, keys(kk, length), 1, 1), MASKED)
            e = jnp.exp(sc - jnp.max(sc, axis=-1, keepdims=True))
            p = (e * (1.0 / jnp.sum(e, axis=-1, keepdims=True))).astype(BF16)
            pb[h, ch, :, 0:length] = p
            o = dot(p, keys(vv, length), 1, 0)
            out = o if out is None else out + o
        at[ch] = out.astype(BF16)

    got_w(0, wob)
    rs_mid = rs_new()

    def fwd_step(n, _):
        ch = lax.rem(z + 1 + n, 4)

        @pl.when(ch < 2)
        def _():
            attend(ch, 512)

        @pl.when(ch >= 2)
        def _():
            attend(ch, 1024)
        o = dot(at[ch], wob[...].reshape(1024, 128), 1, 1)
        part[0, ch] = o.astype(BF16).reshape(2, 128, 1024)
        rs_first(0, rs_mid, ch)

        @pl.when(n > 0)
        def _():
            rs_second(0, rs_mid, lax.rem(z + n, 4))
        return 0
    lax.fori_loop(0, 4, fwd_step, 0)
    rs_second(0, rs_mid, z)

    got_w(1, wdb)

    def draw_step(n, _):
        ch = ag_chip(dyb, dybase, n, gray(n))
        drawb[ch] = dot(dyb[pl.ds(2 * ch, 2)].reshape(256, 1024), wdb[...].reshape(1024, 512), 1, 0)
        return 0
    lax.fori_loop(0, 4, draw_step, 0)

    mid = hid[...].astype(F32) + rs_finish(0, rs_mid)
    midb[...] = mid
    s2 = lax.rsqrt(jnp.mean(mid * mid, axis=-1, keepdims=True) + EPSILON)
    h_own = (mid * s2 * gain_m).astype(BF16)
    hb[c] = h_own
    logits = dot(rout[...], h_own, 1, 1)
    e8 = jnp.exp(logits - jnp.max(logits, axis=0, keepdims=True))
    gates = e8 / jnp.sum(e8, axis=0, keepdims=True)
    er = iota((8, 128), 0)
    member = jnp.zeros((8, 128), F32)
    for j in range(4):
        member = member + jnp.where(rt[j:j + 1, :] == er, 1.0, 0.0)
    gtb[c] = gates * member
    gbase = sems.take(7)
    for dc in range(1, 8):
        copy(gtb.at[c], gtb.at[c], gbase + dc - 1, gbase + dc - 1, cpeer(dc)).start()
    hbase = ag_start(hb)
    got_w(2, wib)
    for dc in range(1, 8):
        got(gtb.at[0], gbase + dc - 1)

    one_c = jnp.where(iota((8, 128), 0) == c, 1.0, 0.0)
    rs_res, rs_dh = rs_new(), rs_new()

    def expert_step(n, _):
        dz = gray(n)
        ch = ag_chip(hb, hbase, n, dz)
        gu = dot(hb[pl.ds(2 * ch, 2)].reshape(256, 1024), wib[...].reshape(1024, 1024), 1, 0)
        g, u = gu[:, :512], gu[:, 512:]
        sig = 1.0 / (1.0 + jnp.exp(-g))
        sw = g * sig
        act = sw * u
        gate = jnp.concatenate([dot(gtb[2 * ch], one_c, 0, 0, HI), dot(gtb[2 * ch + 1], one_c, 0, 0, HI)], axis=0)
        gate = jnp.concatenate([gate] * 4, axis=1)
        draw = drawb[ch]
        ag = (act * gate).astype(BF16)
        agb[ch] = ag
        rows = dot(jnp.ones((8, 512), F32), act * draw, 1, 1, HI)
        dgs[2 * ch] = rows[:, 0:128]
        dgs[2 * ch + 1] = rows[:, 128:256]
        d_act = draw * gate
        dgub[ch, :, 0:512] = (d_act * u * sig * (1.0 + g * (1.0 - sig))).astype(BF16)
        dgub[ch, :, 512:1024] = (d_act * sw).astype(BF16)
        dh = dot(dgub[ch], wib[...].reshape(1024, 1024), 1, 1)
        part[1, ch] = dh.astype(BF16).reshape(2, 128, 1024)
        rs_first(1, rs_dh, ch)
        rs = dot(agb[ch], wdb[...].reshape(1024, 512), 1, 1)
        part[2, ch] = rs.astype(BF16).reshape(2, 128, 1024)
        rs_first(2, rs_res, ch)

        @pl.when(n > 0)
        def _():
            before = lax.rem(z - gray(n - 1) + 4, 4)
            rs_second(1, rs_dh, before)
            rs_second(2, rs_res, before)
        return 0
    lax.fori_loop(0, 4, expert_step, 0)
    dbase = sems.take(7)
    dgr[c] = dgs[c]
    for dc in range(1, 8):
        dev = cpeer(dc)
        copy(dgs.at[dev[1]], dgr.at[c], dbase + dc - 1, dbase + dc - 1, dev).start()
    last = lax.rem(z + 2, 4)
    rs_second(1, rs_dh, last)
    rs_second(2, rs_res, last)

    gs = sems.take(45)

    def send_g(a, src, dst):
        dst[s] = src[s]

        def body(ds, _):
            dev = speer(ds)
            copy(src.at[dev[0]], dst.at[s], gs + 15 * a + ds - 1, gs + 15 * a + ds - 1, dev).start()
            return 0
        lax.fori_loop(1, 16, body, 0)

        def done():
            def wait(ds, _):
                sent(src.at[0], gs + 15 * a + ds - 1)
                return 0
            lax.fori_loop(1, 16, wait, 0)
        drain.append(done)

    def got_g(a, dst):
        def body(ds, _):
            got(dst.at[0], gs + 15 * a + ds - 1)
            return 0
        lax.fori_loop(1, 16, body, 0)

    def gdn_step(i, _):
        cols = pl.ds(pl.multiple_of(i * 256, 256), 256)
        g = dot(dyb[:, :, cols].reshape(1024, 256), agb[...].reshape(1024, 512), 0, 0)
        gdn_s[pl.ds(4 * i, 4)] = g.astype(BF16).reshape(4, 64, 512)
        return 0
    lax.fori_loop(0, 4, gdn_step, 0)
    send_g(1, gdn_s, gdn_r)

    for dc in range(1, 8):
        got(dgr.at[0], dbase + dc - 1)
    dg = jnp.concatenate([dgr[e, 0:1, :] for e in range(8)], axis=0) * member
    d_logits = (gates * (dg - jnp.sum(gates * dg, axis=0, keepdims=True))).astype(BF16)
    d_h = rs_finish(1, rs_dh) + dot(d_logits, rout[...], 0, 0)
    mid = midb[...]
    s2 = lax.rsqrt(jnp.mean(mid * mid, axis=-1, keepdims=True) + EPSILON)
    n2 = mid * s2
    up = d_h * gain_m
    d_mid = og[...].astype(F32) + s2 * (up - n2 * jnp.mean(up * n2, axis=-1, keepdims=True))
    gi_o[...] = d_mid
    dbb[c] = d_mid.astype(BF16)
    bbase = ag_start(dbb)
    g_router = dot(d_logits, hb[c], 1, 0)
    g_mlp = jnp.sum(d_h * n2, axis=0, keepdims=True)
    for p in range(8):
        cut = slice(128 * p, 128 * p + 128)
        sm3[p, 0:8, :] = g_router[:, cut]
        sm3[p, 9:10, :] = g_mlp[:, cut]

    def gin_step(i, _):
        cols = pl.ds(pl.multiple_of(i * 256, 256), 256)
        g = dot(hb[:, :, cols].reshape(1024, 256), dgub[...].reshape(1024, 1024), 0, 0)
        gin_s[pl.ds(4 * i, 4)] = g.astype(BF16).reshape(4, 64, 1024)
        return 0
    lax.fori_loop(0, 4, gin_step, 0)
    send_g(0, gin_s, gin_r)
    res_o[...] = (midb[...] + rs_finish(2, rs_res)).astype(BF16)

    dkv[...] = jnp.zeros_like(dkv)
    low256 = iota((256, 128), 1) < 64

    def attend_back(ch, length):
        da = dab[ch]
        q = qr[pl.ds(2 * ch, 2)].reshape(256, 128).astype(F32)
        daf = da.astype(F32)
        dq = None
        left, right = [], []
        for h, (kk, vv) in enumerate(((ka, va), (kb, vb))):
            p = pb[h, ch, :, 0:length]
            pf = p.astype(F32)
            dp = dot(da, keys(vv, length), 1, 1)
            ds = (pf * (dp - jnp.sum(pf * dp, axis=-1, keepdims=True))).astype(BF16)
            o = dot(ds, keys(kk, length), 1, 0)
            dq = o if dq is None else dq + o
            qh = jnp.where(low256, q if h == 0 else pltpu.roll(q, 64, 1), 0.0)
            dh_ = jnp.where(low256, 0.0, daf if h == 1 else pltpu.roll(daf, 64, 1))
            left += [ds, p]
            right += [qh.astype(BF16), dh_.astype(BF16)]
        dqb[ch] = dq * 0.125
        for l, r in zip(left, right):
            dkv[0:length, :] += dot(l, r, 0, 0)

    def bwd_step(n, _):
        ch = ag_chip(dbb, bbase, n, gray(n))
        dab[ch] = dot(dbb[pl.ds(2 * ch, 2)].reshape(256, 1024), wob[...].reshape(1024, 128), 1, 0).astype(BF16)

        @pl.when(ch < 2)
        def _():
            attend_back(ch, 512)

        @pl.when(ch >= 2)
        def _():
            attend_back(ch, 1024)
        return 0
    lax.fori_loop(0, 4, bwd_step, 0)

    acc[...] = jnp.zeros_like(acc)

    def unrope_step(ch, _):
        for kk in range(2):
            b = 2 * ch + kk
            rows = slice(128 * kk, 128 * kk + 128)
            cs, sn = tables(b)
            wq_ = dqb[ch, rows, :]
            wk_ = dkv[pl.ds(pl.multiple_of(b * 128, 128), 128), :]
            dq = wq_ * cs - partner(wq_) * sn
            dk = wk_ * jnp.where(low64, cs, 1.0) - partner(wk_) * jnp.where(low64, sn, 0.0)
            dn = jnp.concatenate([dq, dk], axis=1)
            normed = qkvb[ch, rows, :]
            acc[1:2, 0:256] += jnp.sum(dn * normed, axis=0, keepdims=True)
            dnb[ch, rows, :] = dn * gains
        put_rows(st2, ch, dot(sel8, dnb[ch] * qkvb[ch], 1, 1, HI))
        return 0
    lax.fori_loop(0, 4, unrope_step, 0)
    finish2 = all_reduce(st2, stb.at[1])

    def go_step(i, _):
        cols = pl.ds(pl.multiple_of(i * 256, 256), 256)
        g = dot(dbb[:, :, cols].reshape(1024, 256), at[...].reshape(1024, 128), 0, 0)
        go_s[pl.ds(4 * i, 4)] = g.astype(BF16).reshape(4, 64, 128)
        return 0
    lax.fori_loop(0, 4, go_step, 0)
    send_g(2, go_s, go_r)
    st2[...] = finish2() * count

    rs_dx = rs_new()

    def dx_step(n, _):
        ch = lax.rem(z + 1 + n, 4)
        for kk in range(2):
            b = 2 * ch + kk
            rows = slice(128 * kk, 128 * kk + 128)
            mean = dot(st2[...], pick(b), 0, 0, HI)
            d = scb[ch, rows, :] * (dnb[ch, rows, :] - qkvb[ch, rows, :] * mean)
            dqkv[ch, rows, :] = d.astype(BF16)
        dx = dot(dqkv[ch], wqb[...].reshape(256, 1024), 1, 0)
        part[3, ch] = dx.astype(BF16).reshape(2, 128, 1024)
        rs_first(3, rs_dx, ch)
        acc[0:1, :] += jnp.sum(dx * xl[pl.ds(2 * ch, 2)].reshape(256, 1024).astype(F32), axis=0, keepdims=True)

        @pl.when(n > 0)
        def _():
            rs_second(3, rs_dx, lax.rem(z + n, 4))
        return 0
    lax.fori_loop(0, 4, dx_step, 0)
    rs_second(3, rs_dx, z)

    g_attn = acc[0:1, :] / gain_a
    for p in range(8):
        sm3[p, 8:9, :] = g_attn[:, 128 * p:128 * p + 128]
        sm3[p, 10:16, :] = jnp.zeros((6, 128), F32)
    m1, m2, m3 = sems.take(7), sems.take(15), sems.take(7)
    sm1[c] = sm3[c]
    for dc in range(1, 8):
        dev = cpeer(dc)
        copy(sm3.at[dev[1]], sm1.at[c], m1 + dc - 1, m1 + dc - 1, dev).start()

    g = dot(dqkv[...].reshape(1024, 256), xl[...].reshape(1024, 1024), 0, 0)
    gq_s[...] = g.astype(BF16).reshape(16, 16, 1024)
    qg = sems.take(16)
    qr_sem = sems.take(16)

    @pl.when(mine)
    def _():
        gq_r[s] = gq_s[ts]

    def send_gq(j, _):
        dev = owner(j)

        @pl.when(not_me(dev))
        def _():
            copy(gq_s.at[j], gq_r.at[s], qg + j, qr_sem + s, dev).start()
        return 0
    lax.fori_loop(0, 16, send_gq, 0)

    for dc in range(1, 8):
        got(sm1.at[0], m1 + dc - 1)
    tot = jnp.sum(sm1[...], axis=0)
    r16 = iota((16, 128), 0)
    tot = tot + jnp.where(r16 == 10, acc[1:2, 0:128], 0.0) + jnp.where(r16 == 11, acc[1:2, 128:256], 0.0)
    sm2[s] = tot

    def send_m(ds, _):
        copy(sm2.at[s], sm2.at[s], m2 + ds - 1, m2 + ds - 1, speer(ds)).start()
        return 0
    lax.fori_loop(1, 16, send_m, 0)

    a2 = sems.take(21)
    for a, (src, tot_ref, out, width) in enumerate(((gin_r, gsum_in, gin_o, 1024), (gdn_r, gsum_dn, gdn_o, 512),
                                                    (go_r, gsum_o, go_o, 128))):
        got_g(a, src)

        def add(i, t, src=src):
            return t + src[i].astype(F32)
        tot_ref[...] = lax.fori_loop(1, 16, add, src[0].astype(F32)).reshape(8, 8, width)
        out[c] = tot_ref[c]
        for dc in range(1, 8):
            dev = cpeer(dc)
            copy(tot_ref.at[dev[1]], out.at[c], a2 + 7 * a + dc - 1, a2 + 7 * a + dc - 1, dev).start()

    def got_m(ds, _):
        got(sm2.at[0], m2 + ds - 1)
        return 0
    lax.fori_loop(1, 16, got_m, 0)
    sm_o[c] = jnp.sum(sm2[...], axis=0)
    for dc in range(1, 8):
        copy(sm_o.at[c], sm_o.at[c], m3 + dc - 1, m3 + dc - 1, cpeer(dc)).start()

    d_x = rs_finish(3, rs_dx)
    x = hid[...].astype(F32)
    s1 = lax.rsqrt(jnp.mean(x * x, axis=-1, keepdims=True) + EPSILON)
    n1 = x * s1
    up = d_x * gain_a
    gi_o[...] += s1 * (up - n1 * jnp.mean(up * n1, axis=-1, keepdims=True))

    def wait_gq(j, _):
        @pl.when(not_me((j, tg)))
        def _():
            got(gq_r.at[0], qr_sem + j)
        return 0
    lax.fori_loop(0, 16, wait_gq, 0)

    def add_q(i, t):
        return t + gq_r[i].astype(F32)
    gq_o[...] = lax.fori_loop(1, 16, add_q, gq_r[0].astype(F32))

    for a, out in enumerate((gin_o, gdn_o, go_o)):
        for dc in range(1, 8):
            got(out.at[0], a2 + 7 * a + dc - 1)
    for dc in range(1, 8):
        got(sm_o.at[0], m3 + dc - 1)
    for done in drain:
        done()
    for a, src in enumerate((wo, wd, wi)):
        for dc in range(1, 8):
            sent(src.at[0], w1 + 7 * a + dc - 1)
    for a, full in enumerate((wob, wdb, wib)):
        def wait(ds, _, a=a, full=full):
            sent(full.at[0], ws + 15 * a + ds - 1)
            return 0
        lax.fori_loop(1, 16, wait, 0)

    def wait_qs(j, _):
        @pl.when(not_me((j, tg)))
        def _():
            sent(wq, qs + j)

        @pl.when(not_me(owner(j)))
        def _():
            sent(gq_s.at[0], qg + j)
        return 0
    lax.fori_loop(0, 16, wait_qs, 0)
    for dc in range(1, 8):
        sent(gtb.at[0], gbase + dc - 1)
        sent(dgs.at[0], dbase + dc - 1)
        sent(sm3.at[0], m1 + dc - 1)
        sent(sm_o.at[0], m3 + dc - 1)
        for a, tot_ref in enumerate((gsum_in, gsum_dn, gsum_o)):
            sent(tot_ref.at[0], a2 + 7 * a + dc - 1)

    def wait_m(ds, _):
        sent(sm2.at[0], m2 + ds - 1)
        return 0
    lax.fori_loop(1, 16, wait_m, 0)


def local(hidden_in, positions, starts, routes, qkv_weight, out_weight, expert_in, expert_out,
          router, attn_gain, query_gain, key_gain, mlp_gain, out_grad):
    par1 = jnp.stack([attn_gain, mlp_gain]).astype(F32)
    par2 = jnp.concatenate([query_gain.astype(F32).reshape(8, 128), key_gain.astype(F32).reshape(8, 64),
                            jnp.ones((8, 64), F32)], axis=1)
    lane = jnp.arange(128)
    freq = ROPE_BASE ** (-(lane % 32).astype(F32) * 2.0 / 64)
    ang = positions[0].astype(F32)[:, None] * freq
    tbl = jnp.where((lane // 32) % 2 == 0, jnp.cos(ang), jnp.sin(ang))
    wo = out_weight.reshape(8, 8, 128).transpose(1, 0, 2)
    wi = expert_in.transpose(1, 0, 2)
    wd = expert_out.transpose(1, 0, 2)
    V = pltpu.VMEM
    scratch = dict(
        xl=V((8, 128, 1024), BF16), dyb=V((8, 128, 1024), BF16), hb=V((8, 128, 1024), BF16),
        dbb=V((8, 128, 1024), BF16), tb=V((8, 128, 128), F32), wqb=V((16, 16, 1024), BF16),
        wo1=V((8, 8, 128), BF16), wi1=V((8, 8, 1024), BF16), wd1=V((8, 8, 512), BF16),
        wob=V((16, 64, 128), BF16), wib=V((16, 64, 1024), BF16), wdb=V((16, 64, 512), BF16),
        qkvb=V((4, 256, 256), F32), scb=V((4, 256, 256), F32), qr=V((8, 128, 128), BF16),
        ka=V((8, 128, 128), BF16), kb=V((8, 128, 128), BF16), va=V((8, 128, 128), BF16), vb=V((8, 128, 128), BF16),
        at=V((4, 256, 128), BF16), pb=V((2, 4, 256, 1024), BF16), drawb=V((4, 256, 512), F32),
        dgub=V((4, 256, 1024), BF16), agb=V((4, 256, 512), BF16),
        part=V((4, 4, 2, 128, 1024), BF16), sibb=V((4, 4, 128, 1024), BF16), rin=V((4, 3, 128, 1024), BF16),
        st=V((16, 128), F32), stb=V((2, 8, 16, 128), F32), st2=V((16, 128), F32), gtb=V((8, 8, 128), F32),
        dgs=V((8, 8, 128), F32), dgr=V((8, 8, 128), F32), midb=V((128, 1024), F32), dab=V((4, 256, 128), BF16),
        dqb=V((4, 256, 128), F32), dkv=V((1024, 128), F32), dnb=V((4, 256, 256), F32), dqkv=V((4, 256, 256), BF16),
        gin_s=V((16, 64, 1024), BF16), gin_r=V((16, 64, 1024), BF16), gdn_s=V((16, 64, 512), BF16),
        gdn_r=V((16, 64, 512), BF16), go_s=V((16, 64, 128), BF16), go_r=V((16, 64, 128), BF16),
        gq_s=V((16, 16, 1024), BF16), gq_r=V((16, 16, 1024), BF16),
        gsum_in=V((8, 8, 1024), F32), gsum_dn=V((8, 8, 512), F32), gsum_o=V((8, 8, 128), F32),
        sm3=V((8, 16, 128), F32), sm1=V((8, 16, 128), F32), sm2=V((16, 16, 128), F32), acc=V((8, 1024), F32),
        send=pltpu.SemaphoreType.DMA((SEMS,)), recv=pltpu.SemaphoreType.DMA((SEMS,)))
    vm = pl.BlockSpec(memory_space=pltpu.VMEM)
    outs = pl.pallas_call(
        kernel,
        out_shape=[jax.ShapeDtypeStruct(sh, dt) for sh, dt in (
            ((128, 1024), BF16), ((128, 1024), F32), ((16, 1024), F32), ((8, 8, 128), F32),
            ((8, 8, 1024), F32), ((8, 8, 512), F32), ((8, 16, 128), F32))],
        in_specs=[vm] * 9 + [pl.BlockSpec(memory_space=pltpu.SMEM)] + [vm] * 2,
        out_specs=[vm] * 7,
        scratch_shapes=list(scratch.values()),
        compiler_params=pltpu.CompilerParams(collective_id=0, has_side_effects=True,
                                             vmem_limit_bytes=60 * 2**20),
        name="layer",
    )(hidden_in[0], out_grad[0], qkv_weight, wo, wi, wd, par1, par2, tbl, starts, routes[0].T, router.T)
    res, gi, gq, go, gin, gdn, sm = outs
    rows = sm.transpose(1, 0, 2)
    return (res[None], gi[None], gq, go.transpose(1, 0, 2).reshape(8, 1024), gin.transpose(1, 0, 2),
            gdn.transpose(1, 0, 2), rows[0:8].reshape(8, 1024).T, rows[8].reshape(1024), rows[10].reshape(1024),
            rows[11, :, :64].reshape(512), rows[9].reshape(1024))


def solution(mesh):
    t = ("seq", "ctx")
    in_specs = (P("seq", "ctx", None), P("seq", "ctx"), P("seq", None), P("seq", "ctx", None),
                P(t, None), P(t, None), P(t, None, None), P(t, None, None),
                P(), P(), P(), P(), P(), P("seq", "ctx", None))
    out_specs = (P("seq", "ctx", None), P("seq", "ctx", None), P(t, None), P(t, None),
                 P(t, None, None), P(t, None, None), P(), P(), P(), P(), P())
    return jax.shard_map(local, mesh=mesh, in_specs=in_specs, out_specs=out_specs, check_vma=False)
```

time: 803 us -> 216 us (0.27)
  waiting for transfers between devices: 421 us -> 0 us
  Pallas kernels: 0 us -> 197 us
  blocking collectives: 194 us -> 0 us
  matrix products: 73.4 us -> 0 us
  starting transfers between devices: 45.6 us -> 0 us
  other arithmetic: 32.9 us -> 2.18 us
  between operations: 17 us -> 0.69 us
    reduce_scatter x8 -> x0, waiting for transfers between devices: 315 us -> none  [the longest x4 231 us: local(): rss = lambda t: lax.psum_scatter(t, 'seq', scatter_dimension=0, tiled=True)]
    pallas_call x0 -> x1, Pallas kernels: none -> 197 us  [local(): pl.pallas_call(kernel, out_shape=[jax.ShapeDtypeStruct(sh, dt) for sh, dt...]
    psum x3 -> x0, blocking collectives: 103 us -> none  [the longest x1 68.2 us: local(): lax.psum((attn_loc, gq_all, gk_all, mlp_loc, router_loc), ('seq', 'ctx'))]
    all_gather x6 -> x0, waiting for transfers between devices: 97 us -> none  [local(): ag = lambda v, ax: lax.all_gather(v, ax, axis=0, tiled=True)]
    all_gather x5 -> x0, blocking collectives: 69.7 us -> none  [local(): ag = lambda v, ax: lax.all_gather(v, ax, axis=0, tiled=True)]
    dot_general x20 -> x0, matrix products: 67.9 us -> none  [the longest x14 50.4 us: dot(): lax.dot_general(a, b, (((ca,), (cb,)), ((), ())), preferred_element_type=...]
    all_to_all x5 -> x0, starting transfers between devices: 30.5 us -> none  [local(): a2a = lambda v, sp, cc: lax.all_to_all(v, 'ctx', sp, cc, tiled=True)]
    all_to_all x2 -> x0, blocking collectives: 20.8 us -> none  [local(): a2a = lambda v, sp, cc: lax.all_to_all(v, 'ctx', sp, cc, tiled=True)]
  transfers between devices with their start and end apart: 21 -> 0, of which waited for: 13 -> 0; matrix products, arithmetic and copies ran while one was open for 9% -> 0% of each run, Pallas kernels for 0% -> 0%
where the time goes in v2:
time: 216 us; the launch traced here: 214 us
  Pallas kernels  197 us (91%)
  local copies, waits for them, and re-layouts  13.7 us (6%)
  other arithmetic  2.18 us (1%)
    pallas_call x1, Pallas kernels, local(): pl.pallas_call(kernel, out_shape=[jax.ShapeDtypeStruct(sh, dt) for sh, dt...  197 us
    unnamed x30, local copies, waits for them, and re-layouts  9.31 us

profile of v2, /device:TPU:9, one launch (start us, length us, event | category | flops | bytes accessed | tf_op | source)
XLA Modules:
  0.0 213.9 jit_solution(9357748329363078142)
XLA Ops:
  0.6 0.0 copy-start.10
  0.7 1.6 copy.31
  2.3 0.0 copy-start.3
  2.3 0.0 copy-done.10
  2.3 0.9 fusion.tbl
  3.3 0.0 copy-done.3
  3.3 0.0 copy-start.6
  3.3 0.7 copy.32
  3.9 0.0 copy-done.6
  4.0 0.0 copy-start.9
  4.0 0.7 copy-done.9
  4.6 0.1 reshape.72
  4.7 0.1 pad.2.clone
  4.8 0.0 copy-start.7
  4.8 0.6 maximum_maximum_fusion.par2
  5.4 0.1 copy-done.7
  5.5 0.0 copy-start.8
  5.5 0.7 copy-done.8
  6.2 0.6 maximum_convert_fusion.par1
  6.8 197.3 %layer.1 = (bf16[128,1024]{1,0:T(8,128)(2,1)}, f32[128,1024]{1,0:T(8,128)}, f32[16,1024]{1,0:T(8,128)}, f32[8,8,128]{2,1,0:T(8,128)}, f32[8,8,1024]{2,1,0:T(8,12...) custom-call(bf16[128,1024]{1,0:T(8,128)(2,1)} %bitcast.37, bf16[128,1024]{1,0:T(8,128)(2,1)} %bitcast.38, ...), custom_call_target="tpu_custom_call" | custom-call | tf_op jit(solution)/shard_map/layer/pallas_call | solution.py:734
  204.0 1.5 fusion.7
  205.5 1.4 slice_bitcast_fusion
  206.9 0.8 slice_reduce_fusion
  207.7 0.7 reshape_squeeze.14
  208.3 0.0 copy-start.2
  208.3 0.0 copy-start.1
  208.3 1.9 copy.27
  210.2 0.0 copy-start
  210.2 0.0 copy-done.2
  210.2 0.7 copy.28
  210.9 0.0 copy-done.1
  210.9 0.7 copy.37
  211.6 0.0 copy-done
  211.6 0.0 copy-start.4
  211.6 0.8 copy.38
  212.4 0.1 copy-done.4
  212.5 0.0 copy-start.5
  212.5 0.6 copy.39
  213.1 0.1 copy-done.5
  213.3 0.6 copy.40
  (7 shorter events, 0.0 us)
Async XLA Ops:
  0.6 1.7 copy-start.10
  2.3 1.0 copy-start.3
  3.3 0.7 copy-start.6
  4.0 0.7 copy-start.9
  4.8 0.7 copy-start.7
  5.5 0.7 copy-start.8
  208.3 1.9 copy-start.2
  208.3 2.6 %copy-start.1 = (bf16[128,1024]{1,0:T(8,128)(2,1)S(1)}, bf16[128,1024]{1,0:T(8,128)(2,1)}, u32[]{:S(2)}) copy-start(bf16[128,1024]{1,0:T(8,128)(2,1)} %get-tuple-element.18) | copy-start | bytes 786436
  210.2 1.4 copy-start
  211.6 0.9 copy-start.4
  212.5 0.8 copy-start.5

commit v3 on v2

v3 whole, which is shorter than its diff:
```python
import functools

import jax
import jax.numpy as jnp
from jax import lax
from jax.experimental import pallas as pl
from jax.experimental.pallas import tpu as pltpu
from jax.sharding import PartitionSpec as P

PIECE = 256
EPSILON = 1e-06
ROPE_BASE = 10000.0
MASKED = -1e30
F32 = jnp.float32
BF16 = jnp.bfloat16
MESH = pl.DeviceIdType.MESH
SENDS, RECVS = 36, 74


def dot(a, b, ca, cb):
    return lax.dot_general(a, b, (((ca,), (cb,)), ((), ())), preferred_element_type=F32)


def iota(shape, axis):
    return lax.broadcasted_iota(jnp.int32, shape, axis)


class Copies:
    def __init__(self, send, recv, dev):
        self.send, self.recv, self.dev = send, recv, dev
        self.drains, self.sends, self.recvs = [], 0, 0

    def group(self, count, total):
        first, mine = self.recvs, self.sends
        self.recvs += count
        self.sends += 1
        assert self.recvs <= RECVS and self.sends <= SENDS
        return Group(self, first, mine, total)


class Group:
    def __init__(self, owner, first, mine, total):
        self.owner, self.first, self.mine = owner, first, mine
        if total is not None:
            owner.drains.append((self, total))

    def make(self, src, dst, i, dev):
        return pltpu.make_async_remote_copy(
            src_ref=src, dst_ref=dst, send_sem=self.owner.send.at[self.mine],
            recv_sem=self.owner.recv.at[self.first + i], device_id=dev, device_id_type=MESH)

    def put(self, src, dst, i, dev):
        self.make(src, dst, i, dev).start()

    def got(self, dst, i=0):
        self.make(dst, dst, i, self.owner.dev).wait_recv()

    def sent(self, src):
        self.make(src, src, 0, self.owner.dev).wait_send()


def kernel(hid, og, wq, wo, wd, par1, par2, tbl, starts, rt, rout,
           res_o, gi_o, gq_o, go_o, gw_o, sm_o,
           xl, dyb, hb, dbb, tb, wqb, wo1, wd1, wob, wb,
           qkvb, scb, qr, ka, kb, va, vb, at, pb, drawb, dgub, agb,
           part, sibb, rin, st, stb, st2, gtb, dgs, dgr, midb, dab, dkv, dqkv,
           g_s, g_r1, g_p, g_r2, go_s, go_r, gq_s, gq_r, gq_t, gsum, gsum_o,
           sm3, sm1, sm2, acc, send, recv):
    s, c = lax.axis_index("seq"), lax.axis_index("ctx")
    z, k = lax.div(c, 2), lax.rem(c, 2)
    y, x_ = lax.div(s, 4), lax.rem(s, 4)
    sib = (s, z * 2 + 1 - k)
    cp = Copies(send, recv, sib)
    dnb, dqb = drawb.at[:, :, 0:256], drawb.at[:, :, 256:384]

    def zdev(dz):
        return (s, lax.rem(z + dz, 4) * 2 + k)

    def cpeer(dc):
        return (s, lax.rem(c + dc, 8))

    def speer(ds):
        return (lax.rem(s + ds, 16), c)

    def near(d):
        return jnp.where(k == 0, y * 4 + lax.rem(x_ + d, 4), lax.rem(y + d, 4) * 4 + x_)

    def far(d):
        return jnp.where(k == 0, lax.rem(y + d, 4) * 4 + x_, y * 4 + lax.rem(x_ + d, 4))

    def cross(a, b):
        return jnp.where(k == 0, lax.rem(y + b, 4) * 4 + lax.rem(x_ + a, 4),
                         lax.rem(y + a, 4) * 4 + lax.rem(x_ + b, 4))

    c4, r4 = lax.div(c, 4), lax.rem(c, 4)
    tg = jnp.where(s < 8, s, jnp.where(s < 12, 2 * (s - 8) + c4, 2 * (s - 12) + c4))
    ts = jnp.where(s < 8, c, jnp.where(s < 12, 8 + r4, 12 + r4))
    mine = (tg == c) & (ts == s)

    def owner(j):
        half = lax.div(c, 2)
        odd = 4 * lax.rem(c, 2)
        os = jnp.where(j < 8, c, jnp.where(j < 12, 8 + half, 12 + half))
        oc = jnp.where(j < 8, j, jnp.where(j < 12, odd + j - 8, odd + j - 12))
        return os, oc

    home = owner(s)
    tk = lax.rem(tg, 2)
    ty, tx = lax.div(ts, 4), lax.rem(ts, 4)

    def aim(a):
        return jnp.where(tk == 0, ty * 4 + lax.rem(tx + a, 4), lax.rem(ty + a, 4) * 4 + tx), tg

    def not_me(dev):
        return jnp.logical_or(dev[0] != s, dev[1] != c)

    bar = pltpu.get_barrier_semaphore()

    for a in range(4):
        source = owner(near(a))

        @pl.when(not_me(source))
        def _(source=source):
            pl.semaphore_signal(bar, inc=1, device_id=source, device_id_type=MESH)
    for dc in range(1, 8):
        pl.semaphore_signal(bar, inc=1, device_id=cpeer(dc), device_id_type=MESH)
    for d in range(1, 4):
        pl.semaphore_signal(bar, inc=1, device_id=(near(d), c), device_id_type=MESH)
        pl.semaphore_signal(bar, inc=1, device_id=(far(d), c), device_id_type=MESH)

    gain_a = par1[0:1, :]
    gain_m = par1[1:2, :]
    gains = par2[pl.ds(c, 1), :]
    x = hid[...].astype(F32)
    s1 = lax.rsqrt(jnp.mean(x * x, axis=-1, keepdims=True) + EPSILON)
    xl[c] = (x * s1 * gain_a).astype(BF16)
    tb[c] = tbl[...]
    dyb[c] = og[...]
    wo1[c] = wo[c]
    wd1[c] = wd[c]

    selfish = jnp.int32(0)
    for a in range(4):
        selfish = selfish + jnp.where(not_me(aim(a)), 0, 1)

    @pl.when(selfish > 0)
    def _():
        wqb[ts] = wq[...]
    pl.semaphore_wait(bar, 17 - selfish)

    def ag_start(buf):
        g = cp.group(7, buf.at[0:7])
        for dz in (1, 3, 2):
            g.put(buf.at[c], buf.at[c], dz - 1, zdev(dz))
        g.put(buf.at[c], buf.at[c], 3, sib)
        return g

    def gray(n):
        return jnp.where(n == 2, 3, jnp.where(n == 3, 2, n))

    def ag_pass(buf, g, n):
        dz = gray(n)
        b = lax.rem(z - dz + 4, 4) * 2 + k
        g.got(buf.at[b], dz - 1)
        g.put(buf.at[b], buf.at[b], 3 + dz, sib)

    def ag_have(buf, g, n):
        dz = gray(n)
        ch = lax.rem(z - dz + 4, 4)
        g.got(buf.at[ch * 2 + 1 - k], 3 + dz)
        return ch

    def ag_next(buf, g, n):
        @pl.when(n < 3)
        def _():
            ag_pass(buf, g, n + 1)

    def xy_start(buf):
        near_g = cp.group(1, buf.at[0:3])
        far_g = cp.group(1, buf.at[0:12])
        for d in (1, 3, 2):
            near_g.put(buf.at[s], buf.at[s], 0, (near(d), c))
        for d in (1, 3, 2):
            far_g.put(buf.at[s], buf.at[s], 0, (far(d), c))
        return near_g, far_g

    def xy_pass(buf, g):
        g[0].got(buf.at[0:3])
        for a in (1, 3, 2):
            block = near(a)
            for d in (1, 3, 2):
                g[1].put(buf.at[block], buf.at[block], 0, (far(d), c))

    def xy_have(buf, g):
        g[1].got(buf.at[0:12])

    def ctx_put(src, dst, own=True):
        g = cp.group(1, dst.at[0:7])
        for dc in range(1, 8):
            dev = cpeer(dc)
            g.put(src.at[dev[1]] if own else src.at[c], dst.at[c], 0, dev)
        return g

    home_g = cp.group(4, None)
    for a in (0, 1, 3, 2):
        dev = aim(a)

        @pl.when(not_me(dev))
        def _(dev=dev, a=a):
            home_g.put(wq, wqb.at[ts], a, dev)
    wo_g = ctx_put(wo, wo1)
    wd_g = ctx_put(wd, wd1)
    x_g = ag_start(xl)
    tb_g = ctx_put(tb, tb, False)

    wq_g = cp.group(1, wqb.at[0:12])
    for a in range(4):
        block = near(a)

        @pl.when(not_me(owner(block)))
        def _(a=a):
            home_g.got(wqb.at[0], (4 - a) % 4)
        for d in (1, 3, 2):
            wq_g.put(wqb.at[block], wqb.at[block], 0, (far(d), c))
    wo_g.got(wo1.at[0:7])
    wob[s] = wo1[...].astype(F32).reshape(64, 128).astype(BF16)
    wo_x = xy_start(wob)
    wd_g.got(wd1.at[0:7])
    wb[s] = wd1[...].astype(F32).reshape(64, 1536).astype(BF16)
    w_x = xy_start(wb)
    ag_pass(xl, x_g, 1)
    ag_pass(xl, x_g, 2)
    xy_pass(wob, wo_x)
    wq_g.got(wqb.at[0:12])

    def wi_full():
        return wb[:, :, 0:1024].reshape(1024, 1024)

    def wd_full():
        return wb[:, :, 1024:1536].reshape(1024, 512)

    lane = iota((1, 256), 1)

    def halves(v):
        high = v.astype(BF16)
        return high, (v - high.astype(F32)).astype(BF16)

    def split(v):
        return jnp.concatenate(halves(v), axis=0)

    def row_sums(ones, v):
        high, low = halves(v)
        return dot(ones, high, 1, 1) + dot(ones, low, 1, 1)

    sel8 = jnp.where(iota((8, 256), 0) == 0, jnp.where(iota((8, 256), 1) < 128, 1.0, 0.0),
                     jnp.where((iota((8, 256), 0) == 1) & (iota((8, 256), 1) >= 128)
                               & (iota((8, 256), 1) < 192), 1.0, 0.0)).astype(BF16)

    def put_rows(ref, ch, rows):
        ref[pl.ds(2 * ch, 1), :] = rows[0:1, 0:128]
        ref[pl.ds(2 * ch + 1, 1), :] = rows[0:1, 128:256]
        ref[pl.ds(8 + 2 * ch, 1), :] = rows[1:2, 0:128]
        ref[pl.ds(9 + 2 * ch, 1), :] = rows[1:2, 128:256]

    def qkv_step(n, _):
        @pl.when(n == 2)
        def _():
            ag_pass(xl, x_g, 3)
        ch = ag_have(xl, x_g, n)
        qkv = dot(xl[pl.ds(2 * ch, 2)].reshape(256, 1024), wqb[...].reshape(256, 1024), 1, 1)
        qkvb[ch] = qkv
        put_rows(st, ch, row_sums(sel8, qkv * qkv))
        return 0
    lax.fori_loop(0, 4, qkv_step, 0)

    def all_reduce(own, slots):
        slots[c] = own[...]
        g = ctx_put(slots, slots, False)

        def finish():
            g.got(slots.at[0:7])
            return jnp.sum(slots[...], axis=0)
        return finish

    row16 = iota((16, 128), 0)
    count = jnp.where(row16 < 8, 1.0 / 1024, 1.0 / 512)
    finish = all_reduce(st, stb.at[0])
    dy_g = ag_start(dyb)
    xy_pass(wb, w_x)
    tb_g.got(tb.at[0:7])
    scale_parts = split(lax.rsqrt(finish() * count + EPSILON))

    def pick(b):
        r, l = lax.rem(iota((32, 256), 0), 16), iota((32, 256), 1)
        return jnp.where(((r == b) & (l < 128)) | ((r == 8 + b) & (l >= 128) & (l < 192)), 1.0, 0.0).astype(BF16)

    even = lax.rem(lax.div(iota((128, 128), 1), 32), 2) == 0
    low64 = iota((128, 128), 1) < 64

    def tables(b):
        t = tb[b]
        r = pltpu.roll(t, 64, 1)
        low = iota((64, 128), 1) < 64
        t = jnp.concatenate([jnp.where(low, t, r), jnp.where(low, r, t)], axis=0)
        t2 = pltpu.roll(t, 32, 1)
        return jnp.where(even, t, t2), jnp.where(even, -t2, t)

    def partner(w):
        return jnp.where(even, pltpu.roll(w, 96, 1), pltpu.roll(w, 32, 1))

    def rope_step(b, _):
        rows = pl.ds(lax.rem(b, 2) * 128, 128)
        ch = lax.div(b, 2)
        scale = dot(scale_parts, pick(b), 0, 0) + jnp.where(lane >= 192, 1.0, 0.0)
        scb[ch, rows, :] = scale
        normed = qkvb[ch, rows, :] * scale
        qkvb[ch, rows, :] = normed
        w = normed * gains
        cs, sn = tables(b)
        wq_, wk_ = w[:, :128], w[:, 128:]
        qr[b] = ((wq_ * cs + partner(wq_) * sn) * 0.125).astype(BF16)
        kv = wk_ * jnp.where(low64, cs, 1.0) + partner(wk_) * jnp.where(low64, sn, 0.0)
        k0 = jnp.where(low64, kv, 0.0)
        v1 = jnp.where(low64, 0.0, kv)
        ka[b] = k0.astype(BF16)
        kb[b] = pltpu.roll(k0, 64, 1).astype(BF16)
        va[b] = pltpu.roll(v1, 64, 1).astype(BF16)
        vb[b] = v1.astype(BF16)
        return 0
    lax.fori_loop(0, 8, rope_step, 0)

    def rs_new(r):
        return cp.group(4, sibb.at[r]), cp.group(1, rin.at[r])

    def rs_first(r, g, ch):
        g[0].put(part.at[r, ch, 1 - k], sibb.at[r, ch], ch, sib)

    def rs_second(r, g, ch):
        g[0].got(sibb.at[r, ch], ch)
        part[r, ch, k] = (part[r, ch, k].astype(F32) + sibb[r, ch].astype(F32)).astype(BF16)
        dz = lax.rem(ch - z + 4, 4)

        @pl.when(dz > 0)
        def _():
            g[1].put(part.at[r, ch, k], rin.at[r, dz - 1], 0, (s, ch * 2 + k))

    def rs_finish(r, g):
        g[1].got(rin.at[r])
        total = part[r, z, k].astype(F32)
        for i in range(3):
            total = total + rin[r, i].astype(F32)
        return total

    st0, st1 = starts[0, 0], starts[0, 1]

    def limits(ch):
        row = ch * 256 + iota((256, 1), 0)
        lim = jnp.where((row >= st0) & (row < st0 + PIECE), st0 + PIECE - 1, row)
        return jnp.where((row >= st1) & (row < st1 + PIECE), st1 + PIECE - 1, lim)

    def keys(ref, length):
        return ref[0:length // 128].reshape(length, 128)

    def attend(ch, length):
        q = qr[pl.ds(2 * ch, 2)].reshape(256, 128)
        allowed = iota((256, length), 1) <= limits(ch)
        out = None
        for h, (kk, vv) in enumerate(((ka, va), (kb, vb))):
            sc = jnp.where(allowed, dot(q, keys(kk, length), 1, 1), MASKED)
            e = jnp.exp(sc - jnp.max(sc, axis=-1, keepdims=True))
            p = (e * (1.0 / jnp.sum(e, axis=-1, keepdims=True))).astype(BF16)
            pb[h, ch, :, 0:length] = p
            o = dot(p, keys(vv, length), 1, 0)
            out = o if out is None else out + o
        at[ch] = out.astype(BF16)

    mid_g = rs_new(0)

    def fwd_step(n, _):
        ch = lax.rem(z + 1 + n, 4)

        @pl.when(ch < 2)
        def _():
            attend(ch, 512)

        @pl.when(ch >= 2)
        def _():
            attend(ch, 1024)

        @pl.when(n == 0)
        def _():
            xy_have(wob, wo_x)
        o = dot(at[ch], wob[...].reshape(1024, 128), 1, 1)
        part[0, ch] = o.astype(BF16).reshape(2, 128, 1024)
        rs_first(0, mid_g, ch)

        @pl.when(n > 0)
        def _():
            rs_second(0, mid_g, lax.rem(z + n, 4))
        return 0
    lax.fori_loop(0, 4, fwd_step, 0)
    rs_second(0, mid_g, z)

    ag_pass(dyb, dy_g, 1)
    ag_pass(dyb, dy_g, 2)
    ag_pass(dyb, dy_g, 3)
    xy_have(wb, w_x)

    def draw_step(n, _):
        ch = ag_have(dyb, dy_g, n)
        drawb[ch] = dot(dyb[pl.ds(2 * ch, 2)].reshape(256, 1024), wd_full(), 1, 0)
        return 0
    lax.fori_loop(0, 4, draw_step, 0)

    mid = hid[...].astype(F32) + rs_finish(0, mid_g)
    midb[...] = mid
    s2 = lax.rsqrt(jnp.mean(mid * mid, axis=-1, keepdims=True) + EPSILON)
    h_own = (mid * s2 * gain_m).astype(BF16)
    hb[c] = h_own
    logits = dot(rout[...], h_own, 1, 1)
    e8 = jnp.exp(logits - jnp.max(logits, axis=0, keepdims=True))
    gates = e8 / jnp.sum(e8, axis=0, keepdims=True)
    er = iota((8, 128), 0)
    member = jnp.zeros((8, 128), F32)
    for j in range(4):
        member = member + jnp.where(rt[j:j + 1, :] == er, 1.0, 0.0)
    gtb[c] = gates * member
    gt_g = ctx_put(gtb, gtb, False)
    h_g = ag_start(hb)

    one_c = jnp.where(lax.rem(iota((16, 128), 0), 8) == c, 1.0, 0.0).astype(BF16)
    dh_g, res_g = rs_new(1), rs_new(2)

    def expert_step(n, _):
        ch = ag_have(hb, h_g, n)
        gu = dot(hb[pl.ds(2 * ch, 2)].reshape(256, 1024), wi_full(), 1, 0)
        g, u = gu[:, :512], gu[:, 512:]
        sig = 1.0 / (1.0 + jnp.exp(-g))
        sw = g * sig
        act = sw * u

        @pl.when(n == 0)
        def _():
            gt_g.got(gtb.at[0:7])
        gate = jnp.concatenate([dot(split(gtb[2 * ch]), one_c, 0, 0), dot(split(gtb[2 * ch + 1]), one_c, 0, 0)], axis=0)
        gate = jnp.concatenate([gate] * 4, axis=1)
        draw = drawb[ch]
        agb[ch] = (act * gate).astype(BF16)
        rows = row_sums(jnp.ones((8, 512), BF16), act * draw)
        dgs[2 * ch] = rows[:, 0:128]
        dgs[2 * ch + 1] = rows[:, 128:256]
        d_act = draw * gate
        dgub[ch, :, 0:512] = (d_act * u * sig * (1.0 + g * (1.0 - sig))).astype(BF16)
        dgub[ch, :, 512:1024] = (d_act * sw).astype(BF16)
        dh = dot(dgub[ch], wi_full(), 1, 1)
        part[1, ch] = dh.astype(BF16).reshape(2, 128, 1024)
        rs_first(1, dh_g, ch)
        rs = dot(agb[ch], wd_full(), 1, 1)
        part[2, ch] = rs.astype(BF16).reshape(2, 128, 1024)
        rs_first(2, res_g, ch)
        ag_next(hb, h_g, n)
        rs_second(1, dh_g, ch)
        return 0
    lax.fori_loop(0, 4, expert_step, 0)
    dgr[c] = dgs[c]
    dg_g = ctx_put(dgs, dgr)

    def gw_step(i, _):
        cols = pl.ds(pl.multiple_of(i * 256, 256), 256)
        g = dot(dyb[:, :, cols].reshape(1024, 256), agb[...].reshape(1024, 512), 0, 0)
        g_s[pl.ds(4 * i, 4), :, 1024:1536] = g.astype(BF16).reshape(4, 64, 512)
        g = dot(hb[:, :, cols].reshape(1024, 256), dgub[...].reshape(1024, 1024), 0, 0)
        g_s[pl.ds(4 * i, 4), :, 0:1024] = g.astype(BF16).reshape(4, 64, 1024)
        return 0
    lax.fori_loop(0, 4, gw_step, 0)
    g1, g2 = cp.group(1, g_s.at[0:12]), cp.group(1, g_s.at[0:3])
    for d in (1, 3, 2):
        for e in range(4):
            g1.put(g_s.at[cross(d, e)], g_r1.at[d - 1, e], 0, (near(d), c))

    dg_g.got(dgr.at[0:7])
    dg = jnp.concatenate([dgr[e, 0:1, :] for e in range(8)], axis=0) * member
    d_logits = (gates * (dg - jnp.sum(gates * dg, axis=0, keepdims=True))).astype(BF16)
    d_h = rs_finish(1, dh_g) + dot(d_logits, rout[...], 0, 0)
    mid = midb[...]
    s2 = lax.rsqrt(jnp.mean(mid * mid, axis=-1, keepdims=True) + EPSILON)
    n2 = mid * s2
    up = d_h * gain_m
    d_mid = og[...].astype(F32) + s2 * (up - n2 * jnp.mean(up * n2, axis=-1, keepdims=True))
    gi_o[...] = d_mid
    dbb[c] = d_mid.astype(BF16)
    db_g = ag_start(dbb)
    for i in range(4):
        rs_second(2, res_g, lax.rem(z + 1 + i, 4))
    g_router = dot(d_logits, hb[c], 1, 0)
    g_mlp = jnp.sum(d_h * n2, axis=0, keepdims=True)
    for p in range(8):
        edge = slice(128 * p, 128 * p + 128)
        sm3[p, 0:8, :] = g_router[:, edge]
        sm3[p, 9:10, :] = g_mlp[:, edge]

    dkv[...] = jnp.zeros_like(dkv)
    low256 = iota((256, 128), 1) < 64

    def attend_back(ch, length):
        da = dab[ch]
        q = qr[pl.ds(2 * ch, 2)].reshape(256, 128).astype(F32)
        daf = da.astype(F32)
        dq = None
        left, right = [], []
        for h, (kk, vv) in enumerate(((ka, va), (kb, vb))):
            p = pb[h, ch, :, 0:length]
            pf = p.astype(F32)
            dp = dot(da, keys(vv, length), 1, 1)
            ds = (pf * (dp - jnp.sum(pf * dp, axis=-1, keepdims=True))).astype(BF16)
            o = dot(ds, keys(kk, length), 1, 0)
            dq = o if dq is None else dq + o
            qh = jnp.where(low256, q if h == 0 else pltpu.roll(q, 64, 1), 0.0)
            dh_ = jnp.where(low256, 0.0, daf if h == 1 else pltpu.roll(daf, 64, 1))
            left += [ds, p]
            right += [qh.astype(BF16), dh_.astype(BF16)]
        dqb[ch] = dq * 0.125
        for l, r in zip(left, right):
            dkv[0:length, :] += dot(l, r, 0, 0)

    def bwd_step(n, _):
        ch = ag_have(dbb, db_g, n)
        dab[ch] = dot(dbb[pl.ds(2 * ch, 2)].reshape(256, 1024), wob[...].reshape(1024, 128), 1, 0).astype(BF16)

        @pl.when(ch < 2)
        def _():
            attend_back(ch, 512)

        @pl.when(ch >= 2)
        def _():
            attend_back(ch, 1024)
        ag_next(dbb, db_g, n)
        return 0
    lax.fori_loop(0, 4, bwd_step, 0)
    g1.got(g_s.at[0:12])

    def fold(e, _):
        own = g_s[cross(0, e)].astype(F32)
        for i in range(3):
            own = own + g_r1[i, e].astype(F32)
        g_p[e] = own.astype(BF16)
        return 0
    lax.fori_loop(0, 4, fold, 0)
    for d in (1, 3, 2):
        g2.put(g_p.at[d], g_r2.at[d - 1], 0, (far(d), c))

    acc[...] = jnp.zeros_like(acc)

    def unrope_step(ch, _):
        for kk in range(2):
            b = 2 * ch + kk
            rows = slice(128 * kk, 128 * kk + 128)
            cs, sn = tables(b)
            wq_ = dqb[ch, rows, :]
            wk_ = dkv[pl.ds(pl.multiple_of(b * 128, 128), 128), :]
            dq = wq_ * cs - partner(wq_) * sn
            dk = wk_ * jnp.where(low64, cs, 1.0) - partner(wk_) * jnp.where(low64, sn, 0.0)
            dn = jnp.concatenate([dq, dk], axis=1)
            normed = qkvb[ch, rows, :]
            acc[1:2, 0:256] += jnp.sum(dn * normed, axis=0, keepdims=True)
            dnb[ch, rows, :] = dn * gains
        put_rows(st2, ch, row_sums(sel8, dnb[ch] * qkvb[ch]))
        return 0
    lax.fori_loop(0, 4, unrope_step, 0)
    finish2 = all_reduce(st2, stb.at[1])

    def go_step(i, _):
        cols = pl.ds(pl.multiple_of(i * 256, 256), 256)
        g = dot(dbb[:, :, cols].reshape(1024, 256), at[...].reshape(1024, 128), 0, 0)
        go_s[pl.ds(4 * i, 4)] = g.astype(BF16).reshape(4, 64, 128)
        return 0
    lax.fori_loop(0, 4, go_step, 0)

    def seq_put(src, dst, spread=True):
        g = cp.group(1, dst.at[0:15])

        def body(ds, _):
            dev = speer(ds)
            g.put(src.at[dev[0]] if spread else src.at[s], dst.at[s], 0, dev)
            return 0
        lax.fori_loop(1, 16, body, 0)
        return g
    go_r[s] = go_s[s]
    go_g = seq_put(go_s, go_r)
    g2.got(g_s.at[0:3])
    gsum[...] = (g_p[0].astype(F32) + g_r2[0].astype(F32) + g_r2[1].astype(F32)
                 + g_r2[2].astype(F32)).reshape(8, 8, 1536)
    gw_o[c] = gsum[c]
    gw_g = ctx_put(gsum, gw_o)
    mean_parts = split(finish2() * count)

    def dqkv_step(b, _):
        rows = pl.ds(lax.rem(b, 2) * 128, 128)
        ch = lax.div(b, 2)
        mean = dot(mean_parts, pick(b), 0, 0)
        d = scb[ch, rows, :] * (dnb[ch, rows, :] - qkvb[ch, rows, :] * mean)
        dqkv[ch, rows, :] = d.astype(BF16)
        return 0
    lax.fori_loop(0, 8, dqkv_step, 0)
    g = dot(dqkv[...].reshape(1024, 256), xl[...].reshape(1024, 1024), 0, 0)
    gq_s[...] = g.astype(BF16).reshape(16, 16, 1024)
    gq_r[s] = gq_s[s]
    gq_g = seq_put(gq_s, gq_r)
    g_attn = jnp.sum(g * wqb[...].reshape(256, 1024).astype(F32), axis=0, keepdims=True) / gain_a
    for p in range(8):
        sm3[p, 8:9, :] = g_attn[:, 128 * p:128 * p + 128]
        sm3[p, 10:16, :] = jnp.zeros((6, 128), F32)
    sm1[c] = sm3[c]
    m1_g = ctx_put(sm3, sm1)

    dx_g = rs_new(3)

    def dx_step(n, _):
        ch = lax.rem(z + 1 + n, 4)
        dx = dot(dqkv[ch], wqb[...].reshape(256, 1024), 1, 0)
        part[3, ch] = dx.astype(BF16).reshape(2, 128, 1024)
        rs_first(3, dx_g, ch)

        @pl.when(n > 0)
        def _():
            rs_second(3, dx_g, lax.rem(z + n, 4))
        return 0
    lax.fori_loop(0, 4, dx_step, 0)
    rs_second(3, dx_g, z)

    m1_g.got(sm1.at[0:7])
    tot = jnp.sum(sm1[...], axis=0)
    r16 = iota((16, 128), 0)
    tot = tot + jnp.where(r16 == 10, acc[1:2, 0:128], 0.0) + jnp.where(r16 == 11, acc[1:2, 128:256], 0.0)
    sm2[s] = tot
    m2_g = seq_put(sm2, sm2, False)
    gq_g.got(gq_r.at[0:15])

    def add_q(i, t):
        return t + gq_r[i].astype(F32)
    gq_t[...] = lax.fori_loop(1, 16, add_q, gq_r[0].astype(F32))
    back_g = cp.group(1, None)

    @pl.when(mine)
    def _():
        gq_o[...] = gq_t[...]

    @pl.when(jnp.logical_not(mine))
    def _():
        back_g.put(gq_t, gq_o, 0, home)
    go_g.got(go_r.at[0:15])

    def add_o(i, t):
        return t + go_r[i].astype(F32)
    gsum_o[...] = lax.fori_loop(1, 16, add_o, go_r[0].astype(F32)).reshape(8, 8, 128)
    go_o[c] = gsum_o[c]
    go2_g = ctx_put(gsum_o, go_o)
    res_o[...] = (midb[...] + rs_finish(2, res_g)).astype(BF16)
    m2_g.got(sm2.at[0:15])
    sm_o[c] = jnp.sum(sm2[...], axis=0)
    m3_g = ctx_put(sm_o, sm_o, False)

    x = hid[...].astype(F32)
    s1 = lax.rsqrt(jnp.mean(x * x, axis=-1, keepdims=True) + EPSILON)
    n1 = x * s1
    up = rs_finish(3, dx_g) * gain_a
    gi_o[...] += s1 * (up - n1 * jnp.mean(up * n1, axis=-1, keepdims=True))

    @pl.when(jnp.logical_not(mine))
    def _():
        back_g.got(gq_o)
        back_g.sent(gq_t)
    for a in range(4):
        @pl.when(not_me(aim(a)))
        def _():
            home_g.sent(wq)
    gw_g.got(gw_o.at[0:7])
    go2_g.got(go_o.at[0:7])
    m3_g.got(sm_o.at[0:7])
    for group, total in cp.drains:
        group.sent(total)


def local(hidden_in, positions, starts, routes, qkv_weight, out_weight, expert_in, expert_out,
          router, attn_gain, query_gain, key_gain, mlp_gain, out_grad):
    par1 = jnp.stack([attn_gain, mlp_gain]).astype(F32)
    par2 = jnp.concatenate([query_gain.astype(F32).reshape(8, 128), key_gain.astype(F32).reshape(8, 64),
                            jnp.ones((8, 64), F32)], axis=1)
    lane = jnp.arange(128)
    freq = ROPE_BASE ** (-(lane % 32).astype(F32) * 2.0 / 64)
    ang = positions[0].astype(F32)[:, None] * freq
    tbl = jnp.where(lane < 32, jnp.cos(ang), jnp.sin(ang))[:, :64]
    tbl = jnp.concatenate([tbl[:64], tbl[64:]], axis=1)
    wo = out_weight.reshape(8, 8, 128).transpose(1, 0, 2)
    wd = jnp.concatenate([expert_in, expert_out], axis=2).transpose(1, 0, 2)
    V = pltpu.VMEM
    scratch = dict(
        xl=V((8, 128, 1024), BF16), dyb=V((8, 128, 1024), BF16), hb=V((8, 128, 1024), BF16),
        dbb=V((8, 128, 1024), BF16), tb=V((8, 64, 128), F32), wqb=V((16, 16, 1024), BF16),
        wo1=V((8, 8, 128), BF16), wd1=V((8, 8, 1536), BF16), wob=V((16, 64, 128), BF16), wb=V((16, 64, 1536), BF16),
        qkvb=V((4, 256, 256), F32), scb=V((4, 256, 256), F32), qr=V((8, 128, 128), BF16),
        ka=V((8, 128, 128), BF16), kb=V((8, 128, 128), BF16), va=V((8, 128, 128), BF16), vb=V((8, 128, 128), BF16),
        at=V((4, 256, 128), BF16), pb=V((2, 4, 256, 1024), BF16), drawb=V((4, 256, 512), F32),
        dgub=V((4, 256, 1024), BF16), agb=V((4, 256, 512), BF16),
        part=V((4, 4, 2, 128, 1024), BF16), sibb=V((4, 4, 128, 1024), BF16), rin=V((4, 3, 128, 1024), BF16),
        st=V((16, 128), F32), stb=V((2, 8, 16, 128), F32), st2=V((16, 128), F32), gtb=V((8, 8, 128), F32),
        dgs=V((8, 8, 128), F32), dgr=V((8, 8, 128), F32), midb=V((128, 1024), F32), dab=V((4, 256, 128), BF16),
        dkv=V((1024, 128), F32), dqkv=V((4, 256, 256), BF16),
        g_s=V((16, 64, 1536), BF16), g_r1=V((3, 4, 64, 1536), BF16), g_p=V((4, 64, 1536), BF16),
        g_r2=V((3, 64, 1536), BF16), go_s=V((16, 64, 128), BF16), go_r=V((16, 64, 128), BF16),
        gq_s=V((16, 16, 1024), BF16), gq_r=V((16, 16, 1024), BF16), gq_t=V((16, 1024), F32),
        gsum=V((8, 8, 1536), F32), gsum_o=V((8, 8, 128), F32),
        sm3=V((8, 16, 128), F32), sm1=V((8, 16, 128), F32), sm2=V((16, 16, 128), F32), acc=V((8, 1024), F32),
        send=pltpu.SemaphoreType.DMA((SENDS,)), recv=pltpu.SemaphoreType.DMA((RECVS,)))
    vm = pl.BlockSpec(memory_space=pltpu.VMEM)
    outs = pl.pallas_call(
        kernel,
        out_shape=[jax.ShapeDtypeStruct(sh, dt) for sh, dt in (
            ((128, 1024), BF16), ((128, 1024), F32), ((16, 1024), F32), ((8, 8, 128), F32),
            ((8, 8, 1536), F32), ((8, 16, 128), F32))],
        in_specs=[vm] * 8 + [pl.BlockSpec(memory_space=pltpu.SMEM)] + [vm] * 2,
        out_specs=[vm] * 6,
        scratch_shapes=list(scratch.values()),
        compiler_params=pltpu.CompilerParams(collective_id=0, has_side_effects=True,
                                             vmem_limit_bytes=60 * 2**20),
        name="layer",
    )(hidden_in[0], out_grad[0], qkv_weight, wo, wd, par1, par2, tbl, starts, routes[0].T, router.T)
    res, gi, gq, go, gw, sm = outs
    gw = gw.transpose(1, 0, 2)
    rows = sm.transpose(1, 0, 2)
    return (res[None], gi[None], gq, go.transpose(1, 0, 2).reshape(8, 1024), gw[:, :, :1024],
            gw[:, :, 1024:], rows[0:8].reshape(8, 1024).T, rows[8].reshape(1024), rows[10].reshape(1024),
            rows[11, :, :64].reshape(512), rows[9].reshape(1024))


def solution(mesh):
    t = ("seq", "ctx")
    in_specs = (P("seq", "ctx", None), P("seq", "ctx"), P("seq", None), P("seq", "ctx", None),
                P(t, None), P(t, None), P(t, None, None), P(t, None, None),
                P(), P(), P(), P(), P(), P("seq", "ctx", None))
    out_specs = (P("seq", "ctx", None), P("seq", "ctx", None), P(t, None), P(t, None),
                 P(t, None, None), P(t, None, None), P(), P(), P(), P(), P())
    return jax.shard_map(local, mesh=mesh, in_specs=in_specs, out_specs=out_specs, check_vma=False)
```

time: 216 us -> 171 us (0.79)
  the two profiles are of different devices: /device:TPU:9 before, /device:TPU:5 now
where the time goes in v3:
time: 171 us; the launch traced here: 170 us
  Pallas kernels  152 us (89%)
  local copies, waits for them, and re-layouts  13.4 us (8%)
  other arithmetic  3.59 us (2%)
    pallas_call x1, Pallas kernels, local(): pl.pallas_call(kernel, out_shape=[jax.ShapeDtypeStruct(sh, dt) for sh, dt...  152 us
    unnamed x28, local copies, waits for them, and re-layouts  7.03 us

profile of v3, /device:TPU:5, one launch (start us, length us, event | category | flops | bytes accessed | tf_op | source)
XLA Modules:
  0.0 169.9 jit_solution(3184398333779768397)
XLA Ops:
  0.6 0.7 convert_bitcast_fusion
  1.3 0.3 fusion
  1.6 0.0 copy-start.2
  1.7 0.7 pad_maximum_fusion.tbl
  2.4 0.2 copy-done.2
  2.5 0.0 copy-start.3
  2.5 0.1 copy.25
  2.6 0.8 copy-done.3
  3.4 0.0 copy-start.6
  3.4 0.7 maximum_bitcast_fusion.wd
  4.1 0.0 copy-done.6
  4.1 0.0 copy-start.9
  4.1 0.7 copy-done.9
  4.8 0.1 reshape.72
  4.9 0.1 pad.4.clone
  5.0 0.0 copy-start.7
  5.0 0.6 maximum_maximum_fusion.par2
  5.6 0.1 copy-done.7
  5.6 0.0 copy-start.8
  5.6 0.7 copy-done.8
  6.3 0.6 maximum_convert_fusion.par1
  6.9 152.2 %layer.1 = (bf16[128,1024]{1,0:T(8,128)(2,1)}, f32[128,1024]{1,0:T(8,128)}, f32[16,1024]{1,0:T(8,128)}, f32[8,8,128]{2,1,0:T(8,128)}, f32[8,8,1536]{2,1,0:T(8,128)}, /*index=5*/f32[8,16,128]{2,1,0:T(8,128)}) custom-call(bf16[128,1024]{1,0:T(8,128)(2,1)} %bitcast.33, bf16[128,1024]{1,0:T(8,128)(2,1)} %bitcast.34, bf16[16,1024]{1,0:T(8,128)(2,1)} %wq.1, ...), custom_call_target="tpu_custom_call" | custom-call | tf_op jit(solution)/shard_map/layer/pallas_call | solution.py:716
  159.1 1.5 fusion.5
  160.6 1.4 slice_bitcast_fusion
  162.0 0.8 slice_reduce_fusion
  162.8 0.7 reshape_squeeze.14
  163.4 1.0 slice.41
  164.4 0.0 copy-start.1
  164.4 0.9 copy.27
  165.3 0.0 copy-start
  165.3 1.0 slice.42
  166.2 0.7 copy.28
  167.0 0.0 copy-done.1
  167.0 0.7 copy.33
  167.7 0.0 copy-done
  167.7 0.0 copy-start.4
  167.7 0.8 copy.34
  168.5 0.1 copy-done.4
  168.5 0.0 copy-start.5
  168.5 0.6 copy.35
  169.2 0.1 copy-done.5
  169.3 0.6 copy.36
  (8 shorter events, 0.1 us)
Async XLA Ops:
  1.6 0.9 copy-start.2
  2.5 0.8 copy-start.3
  3.4 0.7 copy-start.6
  4.1 0.7 copy-start.9
  5.0 0.7 copy-start.7
  5.6 0.7 copy-start.8
  164.4 2.6 %copy-start.1 = (bf16[128,1024]{1,0:T(8,128)(2,1)S(1)}, bf16[128,1024]{1,0:T(8,128)(2,1)}, u32[]{:S(2)}) copy-start(bf16[128,1024]{1,0:T(8,128)(2,1)} %get-tuple-element.17) | copy-start | bytes 786436
  165.3 2.4 %copy-start = (f32[128,1024]{1,0:T(8,128)S(1)}, f32[128,1024]{1,0:T(8,128)}, u32[]{:S(2)}) copy-start(f32[128,1024]{1,0:T(8,128)} %get-tuple-element.18) | copy-start | bytes 1572868
  167.7 0.9 copy-start.4
  168.5 0.8 copy-start.5

commit v4 on v3

--- a/solution.py
+++ b/solution.py
@@ -1,7 +1,6 @@
-import functools
-
 import jax
 import jax.numpy as jnp
+import numpy as np
 from jax import lax
 from jax.experimental import pallas as pl
 from jax.experimental.pallas import tpu as pltpu
@@ -14,7 +13,7 @@
 F32 = jnp.float32
 BF16 = jnp.bfloat16
 MESH = pl.DeviceIdType.MESH
-SENDS, RECVS = 36, 74
+SENDS, RECVS = 36, 86
 
 
 def dot(a, b, ca, cb):
@@ -59,11 +58,11 @@
         self.make(src, src, 0, self.owner.dev).wait_send()
 
 
-def kernel(hid, og, wq, wo, wd, par1, par2, tbl, starts, rt, rout,
+def kernel(hid, og, wq, wo, wd, ag_in, mg_in, qg_in, kg_in, pos, freq, starts, rt, rout,
            res_o, gi_o, gq_o, go_o, gw_o, sm_o,
-           xl, dyb, hb, dbb, tb, wqb, wo1, wd1, wob, wb,
+           xl, dyb, hb, dbb, tb, wqb, wo1, wd1, wof, wb,
            qkvb, scb, qr, ka, kb, va, vb, at, pb, drawb, dgub, agb,
-           part, sibb, rin, st, stb, st2, gtb, dgs, dgr, midb, dab, dkv, dqkv,
+           part, sibb, rin, st, stb, st2, gtb, dgs, dgr, midb, ao, da_s, dab, dkv, dqkv,
            g_s, g_r1, g_p, g_r2, go_s, go_r, gq_s, gq_r, gq_t, gsum, gsum_o,
            sm3, sm1, sm2, acc, send, recv):
     s, c = lax.axis_index("seq"), lax.axis_index("ctx")
@@ -128,13 +127,26 @@
         pl.semaphore_signal(bar, inc=1, device_id=(near(d), c), device_id_type=MESH)
         pl.semaphore_signal(bar, inc=1, device_id=(far(d), c), device_id_type=MESH)
 
-    gain_a = par1[0:1, :]
-    gain_m = par1[1:2, :]
-    gains = par2[pl.ds(c, 1), :]
+    gain_a = ag_in[...].astype(F32).reshape(1, 1024)
+    gain_m = mg_in[...].astype(F32).reshape(1, 1024)
+    gq_all = qg_in[...].astype(F32).reshape(1, 1024)
+    gk_all = kg_in[...].astype(F32).reshape(1, 512)
+    gain_q = gq_all[:, 0:128]
+    pair = gk_all[:, 0:128]
+    for b in range(1, 8):
+        gain_q = jnp.where(c == b, gq_all[:, 128 * b:128 * b + 128], gain_q)
+    for b in range(1, 4):
+        pair = jnp.where(z == b, gk_all[:, 128 * b:128 * b + 128], pair)
+    pair = jnp.where(k == 0, pair, pltpu.roll(pair, 64, 1))
+    gains = jnp.concatenate([gain_q,
+                             jnp.where(iota((1, 128), 1) < 64, pair, 1.0)], axis=1)
+    column = jnp.transpose(jnp.broadcast_to(pos[...].astype(F32), (128, 128)))
+    lane64 = iota((64, 128), 1)
+    angle = jnp.where(lane64 < 64, column[:64], column[64:]) * freq[...]
+    tb[c] = jnp.where(lax.rem(lane64, 64) < 32, jnp.cos(angle), jnp.sin(angle))
     x = hid[...].astype(F32)
     s1 = lax.rsqrt(jnp.mean(x * x, axis=-1, keepdims=True) + EPSILON)
     xl[c] = (x * s1 * gain_a).astype(BF16)
-    tb[c] = tbl[...]
     dyb[c] = og[...]
     wo1[c] = wo[c]
     wd1[c] = wd[c]
@@ -148,51 +160,60 @@
         wqb[ts] = wq[...]
     pl.semaphore_wait(bar, 17 - selfish)
 
-    def ag_start(buf):
-        g = cp.group(7, buf.at[0:7])
+    def ag_start(view, total):
+        g = cp.group(7, total)
         for dz in (1, 3, 2):
-            g.put(buf.at[c], buf.at[c], dz - 1, zdev(dz))
-        g.put(buf.at[c], buf.at[c], 3, sib)
+            g.put(view(c), view(c), dz - 1, zdev(dz))
+        g.put(view(c), view(c), 3, sib)
         return g
 
     def gray(n):
         return jnp.where(n == 2, 3, jnp.where(n == 3, 2, n))
 
-    def ag_pass(buf, g, n):
+    def ag_pass(view, g, n):
         dz = gray(n)
         b = lax.rem(z - dz + 4, 4) * 2 + k
-        g.got(buf.at[b], dz - 1)
-        g.put(buf.at[b], buf.at[b], 3 + dz, sib)
-
-    def ag_have(buf, g, n):
+        g.got(view(b), dz - 1)
+        g.put(view(b), view(b), 3 + dz, sib)
+
+    def ag_have(view, g, n):
         dz = gray(n)
         ch = lax.rem(z - dz + 4, 4)
-        g.got(buf.at[ch * 2 + 1 - k], 3 + dz)
+        g.got(view(ch * 2 + 1 - k), 3 + dz)
         return ch
 
-    def ag_next(buf, g, n):
+    def ag_next(view, g, n):
         @pl.when(n < 3)
         def _():
-            ag_pass(buf, g, n + 1)
-
-    def xy_start(buf):
-        near_g = cp.group(1, buf.at[0:3])
-        far_g = cp.group(1, buf.at[0:12])
+            ag_pass(view, g, n + 1)
+
+    def rows_of(buf):
+        return lambda b: buf.at[b]
+
+    def xy_start(view, total):
+        near_g = cp.group(1, total(3))
+        far_g = cp.group(1, total(12))
         for d in (1, 3, 2):
-            near_g.put(buf.at[s], buf.at[s], 0, (near(d), c))
+            near_g.put(view(s), view(s), 0, (near(d), c))
         for d in (1, 3, 2):
-            far_g.put(buf.at[s], buf.at[s], 0, (far(d), c))
+            far_g.put(view(s), view(s), 0, (far(d), c))
         return near_g, far_g
 
-    def xy_pass(buf, g):
-        g[0].got(buf.at[0:3])
+    def xy_pass(view, total, g):
+        g[0].got(total(3))
         for a in (1, 3, 2):
             block = near(a)
             for d in (1, 3, 2):
-                g[1].put(buf.at[block], buf.at[block], 0, (far(d), c))
-
-    def xy_have(buf, g):
-        g[1].got(buf.at[0:12])
+                g[1].put(view(block), view(block), 0, (far(d), c))
+
+    def out_cols(b):
+        return wof.at[:, :, pl.ds(pl.multiple_of(b * 128, 128), 128)]
+
+    def out_block(b):
+        return wof.at[b, :, pl.ds(pl.multiple_of(c * 128, 128), 128)]
+
+    def out_total(n):
+        return wof.at[0:n, :, 0:128]
 
     def ctx_put(src, dst, own=True):
         g = cp.group(1, dst.at[0:7])
@@ -210,7 +231,7 @@
             home_g.put(wq, wqb.at[ts], a, dev)
     wo_g = ctx_put(wo, wo1)
     wd_g = ctx_put(wd, wd1)
-    x_g = ag_start(xl)
+    x_g = ag_start(rows_of(xl), xl.at[0:7])
     tb_g = ctx_put(tb, tb, False)
 
     wq_g = cp.group(1, wqb.at[0:12])
@@ -223,14 +244,16 @@
         for d in (1, 3, 2):
             wq_g.put(wqb.at[block], wqb.at[block], 0, (far(d), c))
     wo_g.got(wo1.at[0:7])
-    wob[s] = wo1[...].astype(F32).reshape(64, 128).astype(BF16)
-    wo_x = xy_start(wob)
+    out_block(s)[...] = wo1[...].astype(F32).reshape(64, 128).astype(BF16)
+    wo_x = xy_start(out_block, out_total)
     wd_g.got(wd1.at[0:7])
     wb[s] = wd1[...].astype(F32).reshape(64, 1536).astype(BF16)
-    w_x = xy_start(wb)
-    ag_pass(xl, x_g, 1)
-    ag_pass(xl, x_g, 2)
-    xy_pass(wob, wo_x)
+    w_x = xy_start(rows_of(wb), lambda n: wb.at[0:n])
+    ag_pass(rows_of(xl), x_g, 1)
+    ag_pass(rows_of(xl), x_g, 2)
+    xy_pass(out_block, out_total, wo_x)
+    wo_x[1].got(out_total(12))
+    wo_z = ag_start(out_cols, wof.at[:, :, 0:896])
     wq_g.got(wqb.at[0:12])
 
     def wi_full():
@@ -265,8 +288,8 @@
     def qkv_step(n, _):
         @pl.when(n == 2)
         def _():
-            ag_pass(xl, x_g, 3)
-        ch = ag_have(xl, x_g, n)
+            ag_pass(rows_of(xl), x_g, 3)
+        ch = ag_have(rows_of(xl), x_g, n)
         qkv = dot(xl[pl.ds(2 * ch, 2)].reshape(256, 1024), wqb[...].reshape(256, 1024), 1, 1)
         qkvb[ch] = qkv
         put_rows(st, ch, row_sums(sel8, qkv * qkv))
@@ -285,8 +308,7 @@
     row16 = iota((16, 128), 0)
     count = jnp.where(row16 < 8, 1.0 / 1024, 1.0 / 512)
     finish = all_reduce(st, stb.at[0])
-    dy_g = ag_start(dyb)
-    xy_pass(wb, w_x)
+    xy_pass(rows_of(wb), lambda n: wb.at[0:n], w_x)
     tb_g.got(tb.at[0:7])
     scale_parts = split(lax.rsqrt(finish() * count + EPSILON))
 
@@ -372,12 +394,24 @@
             pb[h, ch, :, 0:length] = p
             o = dot(p, keys(vv, length), 1, 0)
             out = o if out is None else out + o
-        at[ch] = out.astype(BF16)
-
-    mid_g = rs_new(0)
+        at[pl.ds(2 * ch, 2)] = out.astype(BF16).reshape(2, 128, 128)
+
+    def step_chip(n):
+        return lax.rem(z + jnp.where(n == 0, 2, jnp.where(n == 1, 1, jnp.where(n == 2, 3, 0))), 4)
+
+    def heads_put(src, dst, g, b):
+        @pl.when(b != c)
+        def _():
+            g.put(src.at[b], dst.at[c], 0, (s, b))
+
+        @pl.when(b == c)
+        def _():
+            dst[c] = src[c]
+
+    ao_g = cp.group(1, ao.at[0:7])
 
     def fwd_step(n, _):
-        ch = lax.rem(z + 1 + n, 4)
+        ch = step_chip(n)
 
         @pl.when(ch < 2)
         def _():
@@ -386,33 +420,20 @@
         @pl.when(ch >= 2)
         def _():
             attend(ch, 1024)
-
-        @pl.when(n == 0)
-        def _():
-            xy_have(wob, wo_x)
-        o = dot(at[ch], wob[...].reshape(1024, 128), 1, 1)
-        part[0, ch] = o.astype(BF16).reshape(2, 128, 1024)
-        rs_first(0, mid_g, ch)
-
-        @pl.when(n > 0)
-        def _():
-            rs_second(0, mid_g, lax.rem(z + n, 4))
+        heads_put(at, ao, ao_g, 2 * ch + k)
+        heads_put(at, ao, ao_g, 2 * ch + 1 - k)
         return 0
     lax.fori_loop(0, 4, fwd_step, 0)
-    rs_second(0, mid_g, z)
-
-    ag_pass(dyb, dy_g, 1)
-    ag_pass(dyb, dy_g, 2)
-    ag_pass(dyb, dy_g, 3)
-    xy_have(wb, w_x)
-
-    def draw_step(n, _):
-        ch = ag_have(dyb, dy_g, n)
-        drawb[ch] = dot(dyb[pl.ds(2 * ch, 2)].reshape(256, 1024), wd_full(), 1, 0)
-        return 0
-    lax.fori_loop(0, 4, draw_step, 0)
-
-    mid = hid[...].astype(F32) + rs_finish(0, mid_g)
+
+    dy_g = ag_start(rows_of(dyb), dyb.at[0:7])
+    for n in (1, 2, 3):
+        ag_pass(out_cols, wo_z, n)
+
+    for n in range(4):
+        ag_have(out_cols, wo_z, n)
+    ao_g.got(ao.at[0:7])
+    wide = jnp.concatenate([ao[b] for b in range(8)], axis=1)
+    mid = hid[...].astype(F32) + dot(wide, wof[...].reshape(1024, 1024), 1, 1)
     midb[...] = mid
     s2 = lax.rsqrt(jnp.mean(mid * mid, axis=-1, keepdims=True) + EPSILON)
     h_own = (mid * s2 * gain_m).astype(BF16)
@@ -425,26 +446,32 @@
     for j in range(4):
         member = member + jnp.where(rt[j:j + 1, :] == er, 1.0, 0.0)
     gtb[c] = gates * member
-    gt_g = ctx_put(gtb, gtb, False)
-    h_g = ag_start(hb)
+    gt_g = cp.group(7, gtb.at[0:7])
+    for dc in (1, 7, 2, 6, 3, 5, 4):
+        gt_g.put(gtb.at[c], gtb.at[c], dc - 1, cpeer(dc))
+    h_g = ag_start(rows_of(hb), hb.at[0:7])
+    ag_pass(rows_of(dyb), dy_g, 1)
+    w_x[1].got(wb.at[0:12])
 
     one_c = jnp.where(lax.rem(iota((16, 128), 0), 8) == c, 1.0, 0.0).astype(BF16)
-    dh_g, res_g = rs_new(1), rs_new(2)
+    dh_g, res_g = rs_new(0), rs_new(1)
 
     def expert_step(n, _):
-        ch = ag_have(hb, h_g, n)
+        ch = ag_have(rows_of(hb), h_g, n)
         gu = dot(hb[pl.ds(2 * ch, 2)].reshape(256, 1024), wi_full(), 1, 0)
         g, u = gu[:, :512], gu[:, 512:]
         sig = 1.0 / (1.0 + jnp.exp(-g))
         sw = g * sig
         act = sw * u
 
-        @pl.when(n == 0)
-        def _():
-            gt_g.got(gtb.at[0:7])
+        for b in (2 * ch, 2 * ch + 1):
+            @pl.when(b != c)
+            def _(b=b):
+                gt_g.got(gtb.at[0], lax.rem(c - b + 8, 8) - 1)
         gate = jnp.concatenate([dot(split(gtb[2 * ch]), one_c, 0, 0), dot(split(gtb[2 * ch + 1]), one_c, 0, 0)], axis=0)
         gate = jnp.concatenate([gate] * 4, axis=1)
-        draw = drawb[ch]
+        ag_have(rows_of(dyb), dy_g, n)
+        draw = dot(dyb[pl.ds(2 * ch, 2)].reshape(256, 1024), wd_full(), 1, 0)
         agb[ch] = (act * gate).astype(BF16)
         rows = row_sums(jnp.ones((8, 512), BF16), act * draw)
         dgs[2 * ch] = rows[:, 0:128]
@@ -453,13 +480,17 @@
         dgub[ch, :, 0:512] = (d_act * u * sig * (1.0 + g * (1.0 - sig))).astype(BF16)
         dgub[ch, :, 512:1024] = (d_act * sw).astype(BF16)
         dh = dot(dgub[ch], wi_full(), 1, 1)
-        part[1, ch] = dh.astype(BF16).reshape(2, 128, 1024)
-        rs_first(1, dh_g, ch)
+        part[0, ch] = dh.astype(BF16).reshape(2, 128, 1024)
+        rs_first(0, dh_g, ch)
         rs = dot(agb[ch], wd_full(), 1, 1)
-        part[2, ch] = rs.astype(BF16).reshape(2, 128, 1024)
-        rs_first(2, res_g, ch)
-        ag_next(hb, h_g, n)
-        rs_second(1, dh_g, ch)
+        part[1, ch] = rs.astype(BF16).reshape(2, 128, 1024)
+        rs_first(1, res_g, ch)
+        ag_next(rows_of(hb), h_g, n)
+
+        @pl.when(n < 2)
+        def _():
+            ag_pass(rows_of(dyb), dy_g, n + 2)
+        rs_second(0, dh_g, ch)
         return 0
     lax.fori_loop(0, 4, expert_step, 0)
     dgr[c] = dgs[c]
@@ -481,17 +512,26 @@
     dg_g.got(dgr.at[0:7])
     dg = jnp.concatenate([dgr[e, 0:1, :] for e in range(8)], axis=0) * member
     d_logits = (gates * (dg - jnp.sum(gates * dg, axis=0, keepdims=True))).astype(BF16)
-    d_h = rs_finish(1, dh_g) + dot(d_logits, rout[...], 0, 0)
+    d_h = rs_finish(0, dh_g) + dot(d_logits, rout[...], 0, 0)
     mid = midb[...]
     s2 = lax.rsqrt(jnp.mean(mid * mid, axis=-1, keepdims=True) + EPSILON)
     n2 = mid * s2
     up = d_h * gain_m
     d_mid = og[...].astype(F32) + s2 * (up - n2 * jnp.mean(up * n2, axis=-1, keepdims=True))
     gi_o[...] = d_mid
-    dbb[c] = d_mid.astype(BF16)
-    db_g = ag_start(dbb)
+    d_branch = d_mid.astype(BF16)
+    d_attn = dot(d_branch, wof[...].reshape(1024, 1024), 1, 0).astype(BF16)
+    for b in range(8):
+        da_s[b] = d_attn[:, 128 * b:128 * b + 128]
+    da_g = cp.group(1, dab.at[0:7])
+    dab[c] = da_s[c]
+    for dc in (4, 3, 5, 2, 6, 1, 7):
+        dev = cpeer(dc)
+        da_g.put(da_s.at[dev[1]], dab.at[c], 0, dev)
+    dbb[c] = d_branch
+    db_g = ag_start(rows_of(dbb), dbb.at[0:7])
     for i in range(4):
-        rs_second(2, res_g, lax.rem(z + 1 + i, 4))
+        rs_second(1, res_g, lax.rem(z + 1 + i, 4))
     g_router = dot(d_logits, hb[c], 1, 0)
     g_mlp = jnp.sum(d_h * n2, axis=0, keepdims=True)
     for p in range(8):
@@ -503,7 +543,7 @@
     low256 = iota((256, 128), 1) < 64
 
     def attend_back(ch, length):
-        da = dab[ch]
+        da = dab[pl.ds(2 * ch, 2)].reshape(256, 128)
         q = qr[pl.ds(2 * ch, 2)].reshape(256, 128).astype(F32)
         daf = da.astype(F32)
         dq = None
@@ -524,8 +564,7 @@
             dkv[0:length, :] += dot(l, r, 0, 0)
 
     def bwd_step(n, _):
-        ch = ag_have(dbb, db_g, n)
-        dab[ch] = dot(dbb[pl.ds(2 * ch, 2)].reshape(256, 1024), wob[...].reshape(1024, 128), 1, 0).astype(BF16)
+        ch = n
 
         @pl.when(ch < 2)
         def _():
@@ -534,20 +573,11 @@
         @pl.when(ch >= 2)
         def _():
             attend_back(ch, 1024)
-        ag_next(dbb, db_g, n)
-        return 0
+        return 0
+    da_g.got(dab.at[0:7])
     lax.fori_loop(0, 4, bwd_step, 0)
-    g1.got(g_s.at[0:12])
-
-    def fold(e, _):
-        own = g_s[cross(0, e)].astype(F32)
-        for i in range(3):
-            own = own + g_r1[i, e].astype(F32)
-        g_p[e] = own.astype(BF16)
-        return 0
-    lax.fori_loop(0, 4, fold, 0)
-    for d in (1, 3, 2):
-        g2.put(g_p.at[d], g_r2.at[d - 1], 0, (far(d), c))
+    for n in (1, 2, 3):
+        ag_pass(rows_of(dbb), db_g, n)
 
     acc[...] = jnp.zeros_like(acc)
 
@@ -569,6 +599,20 @@
     lax.fori_loop(0, 4, unrope_step, 0)
     finish2 = all_reduce(st2, stb.at[1])
 
+    g1.got(g_s.at[0:12])
+
+    def fold(e, _):
+        own = g_s[cross(0, e)].astype(F32)
+        for i in range(3):
+            own = own + g_r1[i, e].astype(F32)
+        g_p[e] = own.astype(BF16)
+        return 0
+    lax.fori_loop(0, 4, fold, 0)
+    for d in (1, 3, 2):
+        g2.put(g_p.at[d], g_r2.at[d - 1], 0, (far(d), c))
+
+    for n in range(4):
+        ag_have(rows_of(dbb), db_g, n)
     def go_step(i, _):
         cols = pl.ds(pl.multiple_of(i * 256, 256), 256)
         g = dot(dbb[:, :, cols].reshape(1024, 256), at[...].reshape(1024, 128), 0, 0)
@@ -587,11 +631,6 @@
         return g
     go_r[s] = go_s[s]
     go_g = seq_put(go_s, go_r)
-    g2.got(g_s.at[0:3])
-    gsum[...] = (g_p[0].astype(F32) + g_r2[0].astype(F32) + g_r2[1].astype(F32)
-                 + g_r2[2].astype(F32)).reshape(8, 8, 1536)
-    gw_o[c] = gsum[c]
-    gw_g = ctx_put(gsum, gw_o)
     mean_parts = split(finish2() * count)
 
     def dqkv_step(b, _):
@@ -613,20 +652,25 @@
     sm1[c] = sm3[c]
     m1_g = ctx_put(sm3, sm1)
 
-    dx_g = rs_new(3)
+    dx_g = rs_new(2)
 
     def dx_step(n, _):
-        ch = lax.rem(z + 1 + n, 4)
+        ch = step_chip(n)
         dx = dot(dqkv[ch], wqb[...].reshape(256, 1024), 1, 0)
-        part[3, ch] = dx.astype(BF16).reshape(2, 128, 1024)
-        rs_first(3, dx_g, ch)
+        part[2, ch] = dx.astype(BF16).reshape(2, 128, 1024)
+        rs_first(2, dx_g, ch)
 
         @pl.when(n > 0)
         def _():
-            rs_second(3, dx_g, lax.rem(z + n, 4))
+            rs_second(2, dx_g, step_chip(n - 1))
         return 0
     lax.fori_loop(0, 4, dx_step, 0)
-    rs_second(3, dx_g, z)
+    rs_second(2, dx_g, z)
+    g2.got(g_s.at[0:3])
+    gsum[...] = (g_p[0].astype(F32) + g_r2[0].astype(F32) + g_r2[1].astype(F32)
+                 + g_r2[2].astype(F32)).reshape(8, 8, 1536)
+    gw_o[c] = gsum[c]
+    gw_g = ctx_put(gsum, gw_o)
 
     m1_g.got(sm1.at[0:7])
     tot = jnp.sum(sm1[...], axis=0)
@@ -655,7 +699,7 @@
     gsum_o[...] = lax.fori_loop(1, 16, add_o, go_r[0].astype(F32)).reshape(8, 8, 128)
     go_o[c] = gsum_o[c]
     go2_g = ctx_put(gsum_o, go_o)
-    res_o[...] = (midb[...] + rs_finish(2, res_g)).astype(BF16)
+    res_o[...] = (midb[...] + rs_finish(1, res_g)).astype(BF16)
     m2_g.got(sm2.at[0:15])
     sm_o[c] = jnp.sum(sm2[...], axis=0)
     m3_g = ctx_put(sm_o, sm_o, False)
@@ -663,7 +707,7 @@
     x = hid[...].astype(F32)
     s1 = lax.rsqrt(jnp.mean(x * x, axis=-1, keepdims=True) + EPSILON)
     n1 = x * s1
-    up = rs_finish(3, dx_g) * gain_a
+    up = rs_finish(2, dx_g) * gain_a
     gi_o[...] += s1 * (up - n1 * jnp.mean(up * n1, axis=-1, keepdims=True))
 
     @pl.when(jnp.logical_not(mine))
@@ -681,30 +725,42 @@
         group.sent(total)
 
 
+def place(res, gi, gq, go, gw, sm, res_o, gi_o, gq_o, go_o, gin_o, gdn_o, gr_o, ga_o, gqg_o, gkg_o, gm_o):
+    res_o[...] = res[...]
+    gi_o[...] = gi[...]
+    gq_o[...] = gq[...]
+    for b in range(8):
+        cols = slice(128 * b, 128 * b + 128)
+        go_o[:, cols] = go[b]
+        gin_o[:, b, :] = gw[b, :, 0:1024]
+        gdn_o[:, b, :] = gw[b, :, 1024:1536]
+        gr_o[:, cols] = sm[b, 0:8, :]
+        ga_o[b:b + 1, :] = sm[b, 8:9, :]
+        gm_o[b:b + 1, :] = sm[b, 9:10, :]
+        gqg_o[b:b + 1, :] = sm[b, 10:11, :]
+    for b in range(4):
+        gkg_o[b:b + 1, :] = jnp.where(iota((1, 128), 1) < 64, sm[2 * b, 11:12, :],
+                                      pltpu.roll(sm[2 * b + 1, 11:12, :], 64, 1))
+
+
 def local(hidden_in, positions, starts, routes, qkv_weight, out_weight, expert_in, expert_out,
           router, attn_gain, query_gain, key_gain, mlp_gain, out_grad):
-    par1 = jnp.stack([attn_gain, mlp_gain]).astype(F32)
-    par2 = jnp.concatenate([query_gain.astype(F32).reshape(8, 128), key_gain.astype(F32).reshape(8, 64),
-                            jnp.ones((8, 64), F32)], axis=1)
-    lane = jnp.arange(128)
-    freq = ROPE_BASE ** (-(lane % 32).astype(F32) * 2.0 / 64)
-    ang = positions[0].astype(F32)[:, None] * freq
-    tbl = jnp.where(lane < 32, jnp.cos(ang), jnp.sin(ang))[:, :64]
-    tbl = jnp.concatenate([tbl[:64], tbl[64:]], axis=1)
+    lanes = np.arange(128, dtype=np.float32) % 32
+    freq = (np.float32(ROPE_BASE) ** (-lanes * np.float32(2.0) / np.float32(64))).astype(np.float32)[None]
     wo = out_weight.reshape(8, 8, 128).transpose(1, 0, 2)
     wd = jnp.concatenate([expert_in, expert_out], axis=2).transpose(1, 0, 2)
     V = pltpu.VMEM
     scratch = dict(
         xl=V((8, 128, 1024), BF16), dyb=V((8, 128, 1024), BF16), hb=V((8, 128, 1024), BF16),
         dbb=V((8, 128, 1024), BF16), tb=V((8, 64, 128), F32), wqb=V((16, 16, 1024), BF16),
-        wo1=V((8, 8, 128), BF16), wd1=V((8, 8, 1536), BF16), wob=V((16, 64, 128), BF16), wb=V((16, 64, 1536), BF16),
+        wo1=V((8, 8, 128), BF16), wd1=V((8, 8, 1536), BF16), wof=V((16, 64, 1024), BF16), wb=V((16, 64, 1536), BF16),
         qkvb=V((4, 256, 256), F32), scb=V((4, 256, 256), F32), qr=V((8, 128, 128), BF16),
         ka=V((8, 128, 128), BF16), kb=V((8, 128, 128), BF16), va=V((8, 128, 128), BF16), vb=V((8, 128, 128), BF16),
-        at=V((4, 256, 128), BF16), pb=V((2, 4, 256, 1024), BF16), drawb=V((4, 256, 512), F32),
+        at=V((8, 128, 128), BF16), pb=V((2, 4, 256, 1024), BF16), drawb=V((4, 256, 512), F32),
         dgub=V((4, 256, 1024), BF16), agb=V((4, 256, 512), BF16),
-        part=V((4, 4, 2, 128, 1024), BF16), sibb=V((4, 4, 128, 1024), BF16), rin=V((4, 3, 128, 1024), BF16),
+        part=V((3, 4, 2, 128, 1024), BF16), sibb=V((3, 4, 128, 1024), BF16), rin=V((3, 3, 128, 1024), BF16),
         st=V((16, 128), F32), stb=V((2, 8, 16, 128), F32), st2=V((16, 128), F32), gtb=V((8, 8, 128), F32),
-        dgs=V((8, 8, 128), F32), dgr=V((8, 8, 128), F32), midb=V((128, 1024), F32), dab=V((4, 256, 128), BF16),
+        dgs=V((8, 8, 128), F32), dgr=V((8, 8, 128), F32), midb=V((128, 1024), F32), ao=V((8, 128, 128), BF16), da_s=V((8, 128, 128), BF16), dab=V((8, 128, 128), BF16),
         dkv=V((1024, 128), F32), dqkv=V((4, 256, 256), BF16),
         g_s=V((16, 64, 1536), BF16), g_r1=V((3, 4, 64, 1536), BF16), g_p=V((4, 64, 1536), BF16),
         g_r2=V((3, 64, 1536), BF16), go_s=V((16, 64, 128), BF16), go_r=V((16, 64, 128), BF16),
@@ -718,19 +774,22 @@
         out_shape=[jax.ShapeDtypeStruct(sh, dt) for sh, dt in (
             ((128, 1024), BF16), ((128, 1024), F32), ((16, 1024), F32), ((8, 8, 128), F32),
             ((8, 8, 1536), F32), ((8, 16, 128), F32))],
-        in_specs=[vm] * 8 + [pl.BlockSpec(memory_space=pltpu.SMEM)] + [vm] * 2,
+        in_specs=[vm] * 11 + [pl.BlockSpec(memory_space=pltpu.SMEM)] + [vm] * 2,
         out_specs=[vm] * 6,
         scratch_shapes=list(scratch.values()),
         compiler_params=pltpu.CompilerParams(collective_id=0, has_side_effects=True,
                                              vmem_limit_bytes=60 * 2**20),
         name="layer",
-    )(hidden_in[0], out_grad[0], qkv_weight, wo, wd, par1, par2, tbl, starts, routes[0].T, router.T)
-    res, gi, gq, go, gw, sm = outs
-    gw = gw.transpose(1, 0, 2)
-    rows = sm.transpose(1, 0, 2)
-    return (res[None], gi[None], gq, go.transpose(1, 0, 2).reshape(8, 1024), gw[:, :, :1024],
-            gw[:, :, 1024:], rows[0:8].reshape(8, 1024).T, rows[8].reshape(1024), rows[10].reshape(1024),
-            rows[11, :, :64].reshape(512), rows[9].reshape(1024))
+    )(hidden_in[0], out_grad[0], qkv_weight, wo, wd, attn_gain, mlp_gain, query_gain, key_gain, positions, freq, starts, routes[0].T, router.T)
+    shapes = (((128, 1024), BF16), ((128, 1024), F32), ((16, 1024), F32), ((8, 1024), F32), ((8, 8, 1024), F32),
+              ((8, 8, 512), F32), ((8, 1024), F32), ((8, 128), F32), ((8, 128), F32), ((4, 128), F32), ((8, 128), F32))
+    res, gi, gq, go, gin, gdn, gr, ga, gqg, gkg, gm = pl.pallas_call(
+        place, out_shape=[jax.ShapeDtypeStruct(sh, dt) for sh, dt in shapes],
+        in_specs=[vm] * 6, out_specs=[vm] * 11, name="place",
+        compiler_params=pltpu.CompilerParams(vmem_limit_bytes=60 * 2**20),
+    )(*outs)
+    return (res[None], gi[None], gq, go, gin, gdn, gr.T, ga.reshape(1024), gqg.reshape(1024), gkg.reshape(512),
+            gm.reshape(1024))
 
 
 def solution(mesh):

time: 171 us -> 161 us (0.942)
  the two profiles are of different devices: /device:TPU:5 before, /device:TPU:9 now
where the time goes in v4:
time: 161 us
  Pallas kernels  159 us (99%)
    pallas_call x1, Pallas kernels, local(): pl.pallas_call(kernel, out_shape=[jax.ShapeDtypeStruct(sh, dt) for sh, dt...  156 us

profile of v4, /device:TPU:9, one launch (start us, length us, event | category | flops | bytes accessed | tf_op | source)
XLA Modules:
  0.0 161.1 jit_solution(3670756709097098646)
XLA Ops:
  0.6 0.0 copy-start
  0.7 0.9 copy.27
  1.6 0.0 copy-done
  1.6 0.1 copy.26
  1.7 0.7 maximum_bitcast_fusion.wd
  2.4 156.4 %layer.1 = (bf16[128,1024]{1,0:T(8,128)(2,1)}, f32[128,1024]{1,0:T(8,128)}, f32[16,1024]{1,0:T(8,128)}, f32[8,8,128]{2,1,0:T(8,128)}, f32[8,8,1536]{2,1,0:T(8,128)}, /*index=5*/f32[8,16,128]{2,1,0:T(8,128)}) custom-call(bf16[128,1024]{1,0:T(8,128)(2,1)} %bitcast.18, bf16[128,1024]{1,0:T(8,128)(2,1)} %bitcast.19, bf16[16,1024]{1,0:T(8,128)(2,1)} %wq.1, ...), custom_call_target="tpu_custom_call" | custom-call | tf_op jit(solution)/shard_map/layer/pallas_call | solution.py:772
  158.7 2.4 %place.1 = (bf16[128,1024]{1,0:T(8,128)(2,1)}, f32[128,1024]{1,0:T(8,128)}, f32[16,1024]{1,0:T(8,128)}, f32[8,1024]{1,0:T(8,128)}, f32[8,8,1024]{2,1,0:T(8,128)}...) custom-call(bf16[128,1024]{1,0:T(8,128)(2,1)} %get-tuple-element.28., ...), custom_call_target="tpu_custom_call" | custom-call | tf_op jit(solution)/shard_map/place/pallas_call | solution.py:786
Async XLA Ops:
  0.6 0.9 copy-start

commit v5 on v4

--- a/solution.py
+++ b/solution.py
@@ -162,7 +162,7 @@
 
     def ag_start(view, total):
         g = cp.group(7, total)
-        for dz in (1, 3, 2):
+        for dz in (1, 3):
             g.put(view(c), view(c), dz - 1, zdev(dz))
         g.put(view(c), view(c), 3, sib)
         return g
@@ -171,21 +171,20 @@
         return jnp.where(n == 2, 3, jnp.where(n == 3, 2, n))
 
     def ag_pass(view, g, n):
-        dz = gray(n)
-        b = lax.rem(z - dz + 4, 4) * 2 + k
-        g.got(view(b), dz - 1)
-        g.put(view(b), view(b), 3 + dz, sib)
+        dz = (0, 1, 3, 2)[n]
+        block = view(lax.rem(z - dz + 4, 4) * 2 + k)
+        g.got(block, dz - 1)
+        if n < 3:
+            size = block.shape[0] // 2
+            half = block.at[pl.ds(size * (n - 1), size)]
+            g.put(half, half, 1, zdev(dz))
+        g.put(block, block, 3 + dz, sib)
 
     def ag_have(view, g, n):
         dz = gray(n)
         ch = lax.rem(z - dz + 4, 4)
         g.got(view(ch * 2 + 1 - k), 3 + dz)
         return ch
-
-    def ag_next(view, g, n):
-        @pl.when(n < 3)
-        def _():
-            ag_pass(view, g, n + 1)
 
     def rows_of(buf):
         return lambda b: buf.at[b]
@@ -308,6 +307,7 @@
     row16 = iota((16, 128), 0)
     count = jnp.where(row16 < 8, 1.0 / 1024, 1.0 / 512)
     finish = all_reduce(st, stb.at[0])
+    dy_g = ag_start(rows_of(dyb), dyb.at[0:7])
     xy_pass(rows_of(wb), lambda n: wb.at[0:n], w_x)
     tb_g.got(tb.at[0:7])
     scale_parts = split(lax.rsqrt(finish() * count + EPSILON))
@@ -350,6 +350,8 @@
         vb[b] = v1.astype(BF16)
         return 0
     lax.fori_loop(0, 8, rope_step, 0)
+    ag_pass(out_cols, wo_z, 1)
+    ag_pass(out_cols, wo_z, 2)
 
     def rs_new(r):
         return cp.group(4, sibb.at[r]), cp.group(1, rin.at[r])
@@ -421,13 +423,17 @@
         def _():
             attend(ch, 1024)
         heads_put(at, ao, ao_g, 2 * ch + k)
+
+        @pl.when(n == 2)
+        def _():
+            ag_pass(out_cols, wo_z, 3)
+            ag_pass(rows_of(dyb), dy_g, 1)
+            ag_pass(rows_of(dyb), dy_g, 2)
         heads_put(at, ao, ao_g, 2 * ch + 1 - k)
         return 0
     lax.fori_loop(0, 4, fwd_step, 0)
 
-    dy_g = ag_start(rows_of(dyb), dyb.at[0:7])
-    for n in (1, 2, 3):
-        ag_pass(out_cols, wo_z, n)
+    ag_pass(rows_of(dyb), dy_g, 3)
 
     for n in range(4):
         ag_have(out_cols, wo_z, n)
@@ -450,8 +456,13 @@
     for dc in (1, 7, 2, 6, 3, 5, 4):
         gt_g.put(gtb.at[c], gtb.at[c], dc - 1, cpeer(dc))
     h_g = ag_start(rows_of(hb), hb.at[0:7])
-    ag_pass(rows_of(dyb), dy_g, 1)
     w_x[1].got(wb.at[0:12])
+
+    def draw_step(n, _):
+        ch = ag_have(rows_of(dyb), dy_g, n)
+        drawb[ch] = dot(dyb[pl.ds(2 * ch, 2)].reshape(256, 1024), wd_full(), 1, 0)
+        return 0
+    lax.fori_loop(0, 4, draw_step, 0)
 
     one_c = jnp.where(lax.rem(iota((16, 128), 0), 8) == c, 1.0, 0.0).astype(BF16)
     dh_g, res_g = rs_new(0), rs_new(1)
@@ -470,8 +481,7 @@
                 gt_g.got(gtb.at[0], lax.rem(c - b + 8, 8) - 1)
         gate = jnp.concatenate([dot(split(gtb[2 * ch]), one_c, 0, 0), dot(split(gtb[2 * ch + 1]), one_c, 0, 0)], axis=0)
         gate = jnp.concatenate([gate] * 4, axis=1)
-        ag_have(rows_of(dyb), dy_g, n)
-        draw = dot(dyb[pl.ds(2 * ch, 2)].reshape(256, 1024), wd_full(), 1, 0)
+        draw = drawb[ch]
         agb[ch] = (act * gate).astype(BF16)
         rows = row_sums(jnp.ones((8, 512), BF16), act * draw)
         dgs[2 * ch] = rows[:, 0:128]
@@ -485,11 +495,15 @@
         rs = dot(agb[ch], wd_full(), 1, 1)
         part[1, ch] = rs.astype(BF16).reshape(2, 128, 1024)
         rs_first(1, res_g, ch)
-        ag_next(rows_of(hb), h_g, n)
-
-        @pl.when(n < 2)
-        def _():
-            ag_pass(rows_of(dyb), dy_g, n + 2)
+
+        @pl.when(n == 0)
+        def _():
+            ag_pass(rows_of(hb), h_g, 1)
+            ag_pass(rows_of(hb), h_g, 2)
+
+        @pl.when(n == 2)
+        def _():
+            ag_pass(rows_of(hb), h_g, 3)
         rs_second(0, dh_g, ch)
         return 0
     lax.fori_loop(0, 4, expert_step, 0)
@@ -508,6 +522,9 @@
     for d in (1, 3, 2):
         for e in range(4):
             g1.put(g_s.at[cross(d, e)], g_r1.at[d - 1, e], 0, (near(d), c))
+
+    for i in range(4):
+        rs_second(1, res_g, lax.rem(z + 1 + i, 4))
 
     dg_g.got(dgr.at[0:7])
     dg = jnp.concatenate([dgr[e, 0:1, :] for e in range(8)], axis=0) * member
@@ -530,8 +547,6 @@
         da_g.put(da_s.at[dev[1]], dab.at[c], 0, dev)
     dbb[c] = d_branch
     db_g = ag_start(rows_of(dbb), dbb.at[0:7])
-    for i in range(4):
-        rs_second(1, res_g, lax.rem(z + 1 + i, 4))
     g_router = dot(d_logits, hb[c], 1, 0)
     g_mlp = jnp.sum(d_h * n2, axis=0, keepdims=True)
     for p in range(8):
@@ -566,6 +581,11 @@
     def bwd_step(n, _):
         ch = n
 
+        @pl.when(n == 2)
+        def _():
+            ag_pass(rows_of(dbb), db_g, 1)
+            ag_pass(rows_of(dbb), db_g, 2)
+
         @pl.when(ch < 2)
         def _():
             attend_back(ch, 512)
@@ -576,8 +596,6 @@
         return 0
     da_g.got(dab.at[0:7])
     lax.fori_loop(0, 4, bwd_step, 0)
-    for n in (1, 2, 3):
-        ag_pass(rows_of(dbb), db_g, n)
 
     acc[...] = jnp.zeros_like(acc)
 
@@ -611,6 +629,7 @@
     for d in (1, 3, 2):
         g2.put(g_p.at[d], g_r2.at[d - 1], 0, (far(d), c))
 
+    ag_pass(rows_of(dbb), db_g, 3)
     for n in range(4):
         ag_have(rows_of(dbb), db_g, n)
     def go_step(i, _):

time: 161 us -> 145 us (0.901)
  Pallas kernels: 159 us -> 143 us
    pallas_call x1, Pallas kernels: 156 us -> 140 us  [local(): pl.pallas_call(kernel, out_shape=[jax.ShapeDtypeStruct(sh, dt) for sh, dt...]
where the time goes in v5:
time: 145 us
  Pallas kernels  143 us (99%)
    pallas_call x1, Pallas kernels, local(): pl.pallas_call(kernel, out_shape=[jax.ShapeDtypeStruct(sh, dt) for sh, dt...  140 us

profile of v5, /device:TPU:9, one launch (start us, length us, event | category | flops | bytes accessed | tf_op | source)
XLA Modules:
  0.0 145.1 jit_solution(15495833028652266319)
XLA Ops:
  0.6 0.0 copy-start
  0.7 0.9 copy.27
  1.6 0.0 copy-done
  1.6 0.1 copy.26
  1.7 0.7 maximum_bitcast_fusion.wd
  2.4 140.3 %layer.1 = (bf16[128,1024]{1,0:T(8,128)(2,1)}, f32[128,1024]{1,0:T(8,128)}, f32[16,1024]{1,0:T(8,128)}, f32[8,8,128]{2,1,0:T(8,128)}, f32[8,8,1536]{2,1,0:T(8,128)}, /*index=5*/f32[8,16,128]{2,1,0:T(8,128)}) custom-call(bf16[128,1024]{1,0:T(8,128)(2,1)} %bitcast.18, bf16[128,1024]{1,0:T(8,128)(2,1)} %bitcast.19, bf16[16,1024]{1,0:T(8,128)(2,1)} %wq.1, ...), custom_call_target="tpu_custom_call" | custom-call | tf_op jit(solution)/shard_map/layer/pallas_call | solution.py:791
  142.7 2.4 %place.1 = (bf16[128,1024]{1,0:T(8,128)(2,1)}, f32[128,1024]{1,0:T(8,128)}, f32[16,1024]{1,0:T(8,128)}, f32[8,1024]{1,0:T(8,128)}, f32[8,8,1024]{2,1,0:T(8,128)}...) custom-call(bf16[128,1024]{1,0:T(8,128)(2,1)} %get-tuple-element.28., ...), custom_call_target="tpu_custom_call" | custom-call | tf_op jit(solution)/shard_map/place/pallas_call | solution.py:805
Async XLA Ops:
  0.6 0.9 copy-start

commit v6 on v5

--- a/solution.py
+++ b/solution.py
@@ -148,7 +148,7 @@
     s1 = lax.rsqrt(jnp.mean(x * x, axis=-1, keepdims=True) + EPSILON)
     xl[c] = (x * s1 * gain_a).astype(BF16)
     dyb[c] = og[...]
-    wo1[c] = wo[c]
+    wo1[c] = wo[...]
     wd1[c] = wd[c]
 
     selfish = jnp.int32(0)
@@ -205,14 +205,14 @@
             for d in (1, 3, 2):
                 g[1].put(view(block), view(block), 0, (far(d), c))
 
-    def out_cols(b):
-        return wof.at[:, :, pl.ds(pl.multiple_of(b * 128, 128), 128)]
+    mine_rows = pl.ds(pl.multiple_of(32 * k, 32), 32)
+    other_rows = pl.ds(pl.multiple_of(32 - 32 * k, 32), 32)
 
     def out_block(b):
-        return wof.at[b, :, pl.ds(pl.multiple_of(c * 128, 128), 128)]
+        return wof.at[b, mine_rows]
 
     def out_total(n):
-        return wof.at[0:n, :, 0:128]
+        return wof.at[0:n, 0:32]
 
     def ctx_put(src, dst, own=True):
         g = cp.group(1, dst.at[0:7])
@@ -228,7 +228,9 @@
         @pl.when(not_me(dev))
         def _(dev=dev, a=a):
             home_g.put(wq, wqb.at[ts], a, dev)
-    wo_g = ctx_put(wo, wo1)
+    wo_g = cp.group(1, wo1.at[0:7])
+    for dc in range(1, 8):
+        wo_g.put(wo, wo1.at[c], 0, cpeer(dc))
     wd_g = ctx_put(wd, wd1)
     x_g = ag_start(rows_of(xl), xl.at[0:7])
     tb_g = ctx_put(tb, tb, False)
@@ -243,16 +245,15 @@
         for d in (1, 3, 2):
             wq_g.put(wqb.at[block], wqb.at[block], 0, (far(d), c))
     wo_g.got(wo1.at[0:7])
-    out_block(s)[...] = wo1[...].astype(F32).reshape(64, 128).astype(BF16)
+    rows64 = wo1[...].astype(F32).reshape(64, 1024)
+    wof[s, mine_rows] = jnp.where(k == 0, rows64[0:32], rows64[32:64]).astype(BF16)
     wo_x = xy_start(out_block, out_total)
     wd_g.got(wd1.at[0:7])
     wb[s] = wd1[...].astype(F32).reshape(64, 1536).astype(BF16)
+    xy_pass(out_block, out_total, wo_x)
     w_x = xy_start(rows_of(wb), lambda n: wb.at[0:n])
     ag_pass(rows_of(xl), x_g, 1)
     ag_pass(rows_of(xl), x_g, 2)
-    xy_pass(out_block, out_total, wo_x)
-    wo_x[1].got(out_total(12))
-    wo_z = ag_start(out_cols, wof.at[:, :, 0:896])
     wq_g.got(wqb.at[0:12])
 
     def wi_full():
@@ -350,8 +351,9 @@
         vb[b] = v1.astype(BF16)
         return 0
     lax.fori_loop(0, 8, rope_step, 0)
-    ag_pass(out_cols, wo_z, 1)
-    ag_pass(out_cols, wo_z, 2)
+    wo_x[1].got(out_total(12))
+    wo_s = cp.group(1, wof.at[:, 0:32])
+    wo_s.put(wof.at[:, mine_rows], wof.at[:, mine_rows], 0, sib)
 
     def rs_new(r):
         return cp.group(4, sibb.at[r]), cp.group(1, rin.at[r])
@@ -426,7 +428,6 @@
 
         @pl.when(n == 2)
         def _():
-            ag_pass(out_cols, wo_z, 3)
             ag_pass(rows_of(dyb), dy_g, 1)
             ag_pass(rows_of(dyb), dy_g, 2)
         heads_put(at, ao, ao_g, 2 * ch + 1 - k)
@@ -435,8 +436,7 @@
 
     ag_pass(rows_of(dyb), dy_g, 3)
 
-    for n in range(4):
-        ag_have(out_cols, wo_z, n)
+    wo_s.got(wof.at[:, other_rows])
     ao_g.got(ao.at[0:7])
     wide = jnp.concatenate([ao[b] for b in range(8)], axis=1)
     mid = hid[...].astype(F32) + dot(wide, wof[...].reshape(1024, 1024), 1, 1)
@@ -766,13 +766,12 @@
           router, attn_gain, query_gain, key_gain, mlp_gain, out_grad):
     lanes = np.arange(128, dtype=np.float32) % 32
     freq = (np.float32(ROPE_BASE) ** (-lanes * np.float32(2.0) / np.float32(64))).astype(np.float32)[None]
-    wo = out_weight.reshape(8, 8, 128).transpose(1, 0, 2)
     wd = jnp.concatenate([expert_in, expert_out], axis=2).transpose(1, 0, 2)
     V = pltpu.VMEM
     scratch = dict(
         xl=V((8, 128, 1024), BF16), dyb=V((8, 128, 1024), BF16), hb=V((8, 128, 1024), BF16),
         dbb=V((8, 128, 1024), BF16), tb=V((8, 64, 128), F32), wqb=V((16, 16, 1024), BF16),
-        wo1=V((8, 8, 128), BF16), wd1=V((8, 8, 1536), BF16), wof=V((16, 64, 1024), BF16), wb=V((16, 64, 1536), BF16),
+        wo1=V((8, 8, 1024), BF16), wd1=V((8, 8, 1536), BF16), wof=V((16, 64, 1024), BF16), wb=V((16, 64, 1536), BF16),
         qkvb=V((4, 256, 256), F32), scb=V((4, 256, 256), F32), qr=V((8, 128, 128), BF16),
         ka=V((8, 128, 128), BF16), kb=V((8, 128, 128), BF16), va=V((8, 128, 128), BF16), vb=V((8, 128, 128), BF16),
         at=V((8, 128, 128), BF16), pb=V((2, 4, 256, 1024), BF16), drawb=V((4, 256, 512), F32),
@@ -799,7 +798,7 @@
         compiler_params=pltpu.CompilerParams(collective_id=0, has_side_effects=True,
                                              vmem_limit_bytes=60 * 2**20),
         name="layer",
-    )(hidden_in[0], out_grad[0], qkv_weight, wo, wd, attn_gain, mlp_gain, query_gain, key_gain, positions, freq, starts, routes[0].T, router.T)
+    )(hidden_in[0], out_grad[0], qkv_weight, out_weight, wd, attn_gain, mlp_gain, query_gain, key_gain, positions, freq, starts, routes[0].T, router.T)
     shapes = (((128, 1024), BF16), ((128, 1024), F32), ((16, 1024), F32), ((8, 1024), F32), ((8, 8, 1024), F32),
               ((8, 8, 512), F32), ((8, 1024), F32), ((8, 128), F32), ((8, 128), F32), ((4, 128), F32), ((8, 128), F32))
     res, gi, gq, go, gin, gdn, gr, ga, gqg, gkg, gm = pl.pallas_call(

time: 145 us -> 138 us (0.952)
  Pallas kernels: 143 us -> 136 us
    pallas_call x1, Pallas kernels: 140 us -> 133 us  [local(): pl.pallas_call(kernel, out_shape=[jax.ShapeDtypeStruct(sh, dt) for sh, dt...]
where the time goes in v6:
time: 138 us
  Pallas kernels  136 us (99%)
    pallas_call x1, Pallas kernels, local(): pl.pallas_call(kernel, out_shape=[jax.ShapeDtypeStruct(sh, dt) for sh, dt...  133 us

profile of v6, /device:TPU:9, one launch (start us, length us, event | category | flops | bytes accessed | tf_op | source)
XLA Modules:
  0.0 138.0 jit_solution(16245658437973445584)
XLA Ops:
  0.6 0.0 copy-start
  0.7 0.9 copy.27
  1.6 0.0 copy-done
  1.6 0.1 copy.26
  1.7 0.7 maximum_bitcast_fusion.wd
  2.4 133.3 %layer.1 = (bf16[128,1024]{1,0:T(8,128)(2,1)}, f32[128,1024]{1,0:T(8,128)}, f32[16,1024]{1,0:T(8,128)}, f32[8,8,128]{2,1,0:T(8,128)}, f32[8,8,1536]{2,1,0:T(8,128)}, /*index=5*/f32[8,16,128]{2,1,0:T(8,128)}) custom-call(bf16[128,1024]{1,0:T(8,128)(2,1)} %bitcast.15, bf16[128,1024]{1,0:T(8,128)(2,1)} %bitcast.16, bf16[16,1024]{1,0:T(8,128)(2,1)} %wq.1, ...), custom_call_target="tpu_custom_call" | custom-call | tf_op jit(solution)/shard_map/layer/pallas_call | solution.py:790
  135.6 2.4 %place.1 = (bf16[128,1024]{1,0:T(8,128)(2,1)}, f32[128,1024]{1,0:T(8,128)}, f32[16,1024]{1,0:T(8,128)}, f32[8,1024]{1,0:T(8,128)}, f32[8,8,1024]{2,1,0:T(8,128)}...) custom-call(bf16[128,1024]{1,0:T(8,128)(2,1)} %get-tuple-element.28., ...), custom_call_target="tpu_custom_call" | custom-call | tf_op jit(solution)/shard_map/place/pallas_call | solution.py:804
Async XLA Ops:
  0.6 0.9 copy-start

commit v7 on v6

--- a/solution.py
+++ b/solution.py
@@ -685,6 +685,20 @@
         return 0
     lax.fori_loop(0, 4, dx_step, 0)
     rs_second(2, dx_g, z)
+    gq_g.got(gq_r.at[0:15])
+
+    def add_q(i, t):
+        return t + gq_r[i].astype(F32)
+    gq_t[...] = lax.fori_loop(1, 16, add_q, gq_r[0].astype(F32))
+    back_g = cp.group(1, None)
+
+    @pl.when(mine)
+    def _():
+        gq_o[...] = gq_t[...]
+
+    @pl.when(jnp.logical_not(mine))
+    def _():
+        back_g.put(gq_t, gq_o, 0, home)
     g2.got(g_s.at[0:3])
     gsum[...] = (g_p[0].astype(F32) + g_r2[0].astype(F32) + g_r2[1].astype(F32)
                  + g_r2[2].astype(F32)).reshape(8, 8, 1536)
@@ -697,20 +711,6 @@
     tot = tot + jnp.where(r16 == 10, acc[1:2, 0:128], 0.0) + jnp.where(r16 == 11, acc[1:2, 128:256], 0.0)
     sm2[s] = tot
     m2_g = seq_put(sm2, sm2, False)
-    gq_g.got(gq_r.at[0:15])
-
-    def add_q(i, t):
-        return t + gq_r[i].astype(F32)
-    gq_t[...] = lax.fori_loop(1, 16, add_q, gq_r[0].astype(F32))
-    back_g = cp.group(1, None)
-
-    @pl.when(mine)
-    def _():
-        gq_o[...] = gq_t[...]
-
-    @pl.when(jnp.logical_not(mine))
-    def _():
-        back_g.put(gq_t, gq_o, 0, home)
     go_g.got(go_r.at[0:15])
 
     def add_o(i, t):

time: 138 us -> 138 us (level)
  no operation moved by 1% of the time
where the time goes in v7:
time: 138 us
  Pallas kernels  136 us (99%)
    pallas_call x1, Pallas kernels, local(): pl.pallas_call(kernel, out_shape=[jax.ShapeDtypeStruct(sh, dt) for sh, dt...  133 us

profile of v7, /device:TPU:9, one launch (start us, length us, event | category | flops | bytes accessed | tf_op | source)
XLA Modules:
  0.0 138.0 jit_solution(706679907949215321)
XLA Ops:
  0.6 0.0 copy-start
  0.7 0.9 copy.27
  1.6 0.0 copy-done
  1.6 0.1 copy.26
  1.7 0.7 maximum_bitcast_fusion.wd
  2.4 133.3 %layer.1 = (bf16[128,1024]{1,0:T(8,128)(2,1)}, f32[128,1024]{1,0:T(8,128)}, f32[16,1024]{1,0:T(8,128)}, f32[8,8,128]{2,1,0:T(8,128)}, f32[8,8,1536]{2,1,0:T(8,128)}, /*index=5*/f32[8,16,128]{2,1,0:T(8,128)}) custom-call(bf16[128,1024]{1,0:T(8,128)(2,1)} %bitcast.15, bf16[128,1024]{1,0:T(8,128)(2,1)} %bitcast.16, bf16[16,1024]{1,0:T(8,128)(2,1)} %wq.1, ...), custom_call_target="tpu_custom_call" | custom-call | tf_op jit(solution)/shard_map/layer/pallas_call | solution.py:790
  135.6 2.4 %place.1 = (bf16[128,1024]{1,0:T(8,128)(2,1)}, f32[128,1024]{1,0:T(8,128)}, f32[16,1024]{1,0:T(8,128)}, f32[8,1024]{1,0:T(8,128)}, f32[8,8,1024]{2,1,0:T(8,128)}...) custom-call(bf16[128,1024]{1,0:T(8,128)(2,1)} %get-tuple-element.28., ...), custom_call_target="tpu_custom_call" | custom-call | tf_op jit(solution)/shard_map/place/pallas_call | solution.py:804
Async XLA Ops:
  0.6 0.9 copy-start
